TPU v7x, 32 devices: a whole 2x2x4 slice. The times are simulated.
32 devices in a mesh: leaf: 2 (over core), row: 4 (over y, x), col: 4 (over z).
Axes of the slice: x: 2, y: 2, z: 4, core: 2. Of those that a mesh axis runs over, the one named last changes fastest.
Arguments:
- sketch_leaf: bfloat16 [16384, 256], P(('leaf', 'row'), 'col'), may hold values from -6 to 6
- sketch_sep: bfloat16 [8192, 256], P(('row', 'col')), may hold values from -6 to 6
- leaf_inverse: bfloat16 [16384, 8192], P(('leaf', 'col'), 'row'), as said below
- coupling: bfloat16 [16384, 2048], P(('leaf', 'col'), 'row'), may hold values from -0.0625 to 0.0625
- sep_inverse: bfloat16 [8192, 8192], P('leaf', ('row', 'col'))
- front_map: int32 [2, 16], replicated, may hold values from 0 to 63, as said below
Outputs:
- sketch_out_leaf: float32 [16384, 256], P(('leaf', 'row'), 'col')
- sketch_out_sep: float32 [8192, 256], P(('row', 'col'))
Inputs may be any that keep to these rules, and one draw needn't show every extreme that they name: `front_map`: row block q of every section's coupling lies in separator blocks q * 4 to q * 4 + 3. leaf_inverse and sep_inverse are inverses of lower triangular factor blocks (in natural order), stored in block-cyclic order.
All inputs are finite; a program needn't handle non-finite values.
Results may differ from a plain program's by a relative error of at most 0.024.
Values may be sent and summed in bfloat16 or wider, within the bound.
No kernel may reach another device: no remote copies, remote signals or barrier semaphores. Data moves between devices by JAX's collectives and lax.ppermute only.
A program may use at most 64 MiB of HBM per device.

v0:
```python
import jax
import jax.numpy as jnp
from jax import lax
from jax.sharding import PartitionSpec as P


def contract_rows(left, right):
    return lax.dot_general(
        left, right, (((0,), (0,)), ((), ())), preferred_element_type=jnp.float32
    )


def shards(sketch_leaf, sketch_sep, leaf_inverse, coupling, sep_inverse, front_map):
    columns = sketch_leaf.shape[1] * lax.axis_size("col")
    q_index = lax.axis_index("row") * lax.axis_size("col") + lax.axis_index("col")
    section = lax.axis_index("leaf")
    partial_value = jnp.dot(
        leaf_inverse,
        lax.all_gather(sketch_leaf, "col", axis=1, tiled=True),
        preferred_element_type=jnp.float32,
    )
    front_z = lax.psum_scatter(partial_value, "row", scatter_dimension=1, tiled=True).astype(
        jnp.bfloat16
    )
    coupled_part = contract_rows(coupling, lax.all_gather(front_z, "row", axis=1, tiled=True))
    coupled = lax.psum_scatter(coupled_part, "col", scatter_dimension=0, tiled=True).astype(
        jnp.bfloat16
    )
    block_rows = coupled.shape[0]
    group = sketch_sep.shape[0] // block_rows
    own_slot = front_map[section, q_index] - q_index * group
    blocks = lax.all_gather(coupled, "leaf", axis=0, tiled=True)
    slots = front_map[:, q_index] - q_index * group
    place = (slots[:, None] == jnp.arange(group, dtype=jnp.int32)[None, :]).astype(jnp.bfloat16)
    stacked = blocks.reshape(slots.shape[0], block_rows, columns)
    total = jnp.einsum("sg,sik->gik", place, stacked, preferred_element_type=jnp.float32).reshape(
        group * block_rows, columns
    )
    sep_rhs = (sketch_sep.astype(jnp.float32) - total).astype(jnp.bfloat16)
    sep_part = jnp.dot(sep_inverse, sep_rhs, preferred_element_type=jnp.float32)
    sep_mid = lax.psum(sep_part.astype(jnp.bfloat16), ("row", "col"))
    sketch_out_sep = lax.psum(
        contract_rows(sep_inverse, sep_mid).astype(jnp.bfloat16), "leaf"
    ).astype(jnp.float32)
    sep_round = sketch_out_sep.astype(jnp.bfloat16)
    pulled = lax.dynamic_slice_in_dim(sep_round, own_slot * block_rows, block_rows, 0)
    back_part = jnp.dot(
        coupling,
        lax.all_gather(pulled, "col", axis=0, tiled=True),
        preferred_element_type=jnp.float32,
    )
    back_slice = lax.psum_scatter(
        back_part.astype(jnp.bfloat16), "row", scatter_dimension=1, tiled=True
    ).astype(jnp.float32)
    leaf_rhs = (front_z.astype(jnp.float32) - back_slice).astype(jnp.bfloat16)
    out_part = contract_rows(leaf_inverse, lax.all_gather(leaf_rhs, "row", axis=1, tiled=True))
    sketch_out_leaf = lax.psum_scatter(
        out_part.astype(jnp.bfloat16), "col", scatter_dimension=1, tiled=True
    ).astype(jnp.float32)
    return (sketch_out_leaf, sketch_out_sep)


def solution(mesh):
    placed = (
        P(("leaf", "row"), "col"),
        P(("row", "col"), None),
        P(("leaf", "col"), "row"),
        P(("leaf", "col"), "row"),
        P("leaf", ("row", "col")),
        P(),
    )
    return jax.shard_map(
        shards,
        mesh=mesh,
        in_specs=placed,
        out_specs=(P(("leaf", "row"), "col"), P(("row", "col"), None)),
        check_vma=False,
    )
```

profile of v0, /device:TPU:0, one launch (start us, length us, event | category | flops | bytes accessed | tf_op | source)
XLA Modules:
  0.0 407.7 jit_solution(16510389504449765819)
XLA Ops:
  7.2 0.0 copy-start
  7.2 0.0 all-gather.4.cloned.1.call-start
  7.2 0.7 all-gather.4.cloned.1.call-update
  7.9 0.0 reduce-scatter.5.cloned.1.call-start
  8.0 32.3 %all-gather.4.cloned.1.call-done = bf16[2048,256]{0,1:T(8,128)(2,1)} async-done(((bf16[2048,64]{0,1:T(8,128)(2,1)}), bf16[2048,256]{0,1:T(8,128)(2,1)}) %all-gather.4.cloned.1.call-update) | async-done | bytes 1048592 | tf_op jit(solution)/shard_map/all_gather | solution.py:19
  40.3 7.3 %fusion.10 = f32[2048,256]{0,1:T(8,128)} fusion(bf16[2048,2048]{1,0:T(8,128)(2,1)} %param.8, bf16[2048,256]{0,1:T(8,128)(2,1)} %all-gather.4.cloned.1.call-done), kind=kOutput, calls=%fused_computation.19 | convolution fusion | flops 2147483648 | bytes 11534336 | tf_op jit(solution)/shard_map/dot_general | solution.py:17
  47.6 0.0 reduce-scatter.5.cloned.1.call-update
  47.6 0.0 all-gather.6.cloned.1.call-start
  47.7 34.7 %reduce-scatter.5.cloned.1.call-done = f32[2048,64]{0,1:T(8,128)} async-done(((f32[2048,256]{0,1:T(8,128)}), f32[2048,64]{0,1:T(8,128)}) %reduce-scatter.5.cloned.1.call-update) | async-done | bytes 524304 | tf_op jit(solution)/shard_map/reduce_scatter | solution.py:22
  82.3 1.8 convert_element_type.53
  84.1 0.0 all-gather.6.cloned.1.call-update
  84.2 0.0 reduce-scatter.7.cloned.1.call-start
  84.2 27.1 %all-gather.6.cloned.1.call-done = bf16[2048,256]{0,1:T(8,128)(2,1)} async-done(((bf16[2048,64]{0,1:T(8,128)(2,1)}), bf16[2048,256]{0,1:T(8,128)(2,1)}) %all-gather.6.cloned.1.call-update) | async-done | bytes 1048592 | tf_op jit(solution)/shard_map/all_gather | solution.py:25
  111.3 2.7 convolution_bitcast_fusion
  114.0 0.0 reduce-scatter.7.cloned.1.call-update
  114.1 0.0 all-reduce.3.cloned.1.call-start
  114.1 0.2 subtract_reduce_fusion
  114.3 21.7 %reduce-scatter.7.cloned.1.call-done = f32[128,256]{0,1:T(8,128)} async-done(((f32[512,256]{0,1:T(8,128)}), f32[128,256]{0,1:T(8,128)}) %reduce-scatter.7.cloned.1.call-update) | async-done | bytes 131088 | tf_op jit(solution)/shard_map/reduce_scatter | solution.py:26
  136.0 0.9 convert_element_type.56
  136.9 1.9 all_gather.17
  138.9 0.1 copy.10
  139.0 0.4 fusion.5
  139.5 0.1 copy.11
  139.6 0.1 fusion.4
  139.7 4.8 %fusion = bf16[4096,256]{0,1:T(8,128)(2,1)} fusion(bf16[512,256]{1,0:T(8,128)(2,1)S(1)} %fusion.4, bf16[4096,512]{1,0:T(8,128)(2,1)} %param.10), kind=kOutput, calls=%fused_computation.1 | convolution fusion | flops 1074790400 | bytes 6553600 | tf_op jit(solution)/shard_map/dot_general | solution.py:40
  144.5 0.0 all-reduce.3.cloned.1.call-update
  144.5 0.0 all-reduce.5.cloned.1.call-start
  144.5 125.0 %all-reduce.3.cloned.1.call-done = bf16[4096,256]{0,1:T(8,128)(2,1)} async-done(((bf16[4096,256]{0,1:T(8,128)(2,1)}), bf16[4096,256]{0,1:T(8,128)(2,1)}) %all-reduce.3.cloned.1.call-update) | async-done | bytes 2097168 | tf_op jit(solution)/shard_map/psum | solution.py:41
  269.5 4.8 %fusion.3 = bf16[512,256]{0,1:T(8,128)(2,1)} fusion(bf16[4096,256]{0,1:T(8,128)(2,1)} %all-reduce.3.cloned.1.call-done, bf16[4096,512]{1,0:T(8,128)(2,1)} %param.10), kind=kOutput, calls=%fused_computation.8 | convolution fusion | flops 1073872896 | bytes 6553600 | tf_op jit(solution)/shard_map/dot_general | solution.py:8
  274.3 0.0 all-reduce.5.cloned.1.call-update
  274.3 0.0 reduce-scatter.9.cloned.1.call-start
  274.4 0.6 dynamic_slice.10
  275.6 16.3 %all-reduce.5.cloned.1.call-done = bf16[512,256]{0,1:T(8,128)(2,1)} async-done(((bf16[512,256]{0,1:T(8,128)(2,1)}), bf16[512,256]{0,1:T(8,128)(2,1)}) %all-reduce.5.cloned.1.call-update) | async-done | bytes 262160 | tf_op jit(solution)/shard_map/psum | solution.py:42
  291.9 0.8 constant_dynamic-slice_fusion
  292.8 13.1 %all_gather.18 = bf16[512,256]{0,1:T(8,128)(2,1)S(1)} all-gather(bf16[128,256]{0,1:T(8,128)(2,1)S(1)} %constant_dynamic-slice_fusion), channel_id=1, replica_groups=mesh['leaf'=2,'row'=4,'col'=4] {'col'}, dimensions={0}, use_global_device_ids=true | all-gather | bytes 327680 | tf_op jit(solution)/shard_map/all_gather | solution.py:49
  305.9 1.7 fusion.2
  307.6 0.0 reduce-scatter.9.cloned.1.call-update
  307.7 0.0 all-gather.8.cloned.1.call-start
  307.7 28.2 %reduce-scatter.9.cloned.1.call-done = bf16[2048,64]{0,1:T(8,128)(2,1)} async-done(((bf16[2048,256]{0,1:T(8,128)(2,1)}), bf16[2048,64]{0,1:T(8,128)(2,1)}) %reduce-scatter.9.cloned.1.call-update) | async-done | bytes 262160 | tf_op jit(solution)/shard_map/reduce_scatter | solution.py:52
  335.9 1.7 subtract_convert_fusion
  337.6 0.0 all-gather.8.cloned.1.call-update
  337.7 0.0 reduce-scatter.11.cloned.1.call-start
  337.7 27.2 %all-gather.8.cloned.1.call-done = bf16[2048,256]{0,1:T(8,128)(2,1)} async-done(((bf16[2048,64]{0,1:T(8,128)(2,1)}), bf16[2048,256]{0,1:T(8,128)(2,1)}) %all-gather.8.cloned.1.call-update) | async-done | bytes 1048592 | tf_op jit(solution)/shard_map/all_gather | solution.py:56
  364.9 7.0 %fusion.1 = bf16[2048,256]{0,1:T(8,128)(2,1)} fusion(bf16[2048,256]{0,1:T(8,128)(2,1)} %all-gather.8.cloned.1.call-done, bf16[2048,2048]{1,0:T(8,128)(2,1)} %param.8), kind=kOutput, calls=%fused_computation.4 | convolution fusion | flops 2148007936 | bytes 10485760 | tf_op jit(solution)/shard_map/dot_general | solution.py:8
  371.9 0.0 reduce-scatter.11.cloned.1.call-update
  371.9 0.9 copy.12
  372.9 26.5 %reduce-scatter.11.cloned.1.call-done = bf16[2048,64]{0,1:T(8,128)(2,1)} async-done(((bf16[2048,256]{0,1:T(8,128)(2,1)}), bf16[2048,64]{0,1:T(8,128)(2,1)}) %reduce-scatter.11.cloned.1.call-update) | async-done | bytes 262160 | tf_op jit(solution)/shard_map/reduce_scatter | solution.py:57
  399.4 1.8 convert_element_type.68
  (10 shorter events, 0.1 us)
Async XLA Ops:
  7.2 104.1 %copy-start = (bf16[2048,512]{1,0:T(8,128)(2,1)S(1)}, bf16[2048,512]{1,0:T(8,128)(2,1)}, u32[]{:S(2)}) copy-start(bf16[2048,512]{1,0:T(8,128)(2,1)} %param.9) | copy-start | bytes 6291460
  7.2 33.1 %all-gather.4.cloned.1.call-start = ((), (), s32[]{:S(2)}) async-start(), calls=%async_computation.4 | async-start | bytes 1310720 | tf_op jit(solution)/shard_map/all_gather | solution.py:19
  7.9 74.4 %reduce-scatter.5.cloned.1.call-start = ((), (), s32[]{:S(2)}) async-start(), calls=%async_computation.5 | async-start | bytes 2621440 | tf_op jit(solution)/shard_map/reduce_scatter | solution.py:22
  47.6 63.7 %all-gather.6.cloned.1.call-start = ((), (), s32[]{:S(2)}) async-start(), calls=%async_computation.6 | async-start | bytes 1310720 | tf_op jit(solution)/shard_map/all_gather | solution.py:25
  84.1 30.0 %copy-start.4 = (s32[2,16]{1,0:T(2,128)S(1)}, s32[2,16]{1,0:T(2,128)}, u32[]{:S(2)}) copy-start(s32[2,16]{1,0:T(2,128)} %param.11) | copy-start | bytes 388
  84.2 51.9 %reduce-scatter.7.cloned.1.call-start = ((), (), s32[]{:S(2)}) async-start(), calls=%async_computation.7 | async-start | bytes 655360 | tf_op jit(solution)/shard_map/reduce_scatter | solution.py:26
  114.0 25.5 %copy-start.3 = (bf16[512,256]{1,0:T(8,128)(2,1)S(1)}, bf16[512,256]{1,0:T(8,128)(2,1)}, u32[]{:S(2)}) copy-start(bf16[512,256]{1,0:T(8,128)(2,1)} %param.7) | copy-start | bytes 786436
  114.1 155.5 %all-reduce.3.cloned.1.call-start = ((), (), s32[]{:S(2)}) async-start(), calls=%async_computation.8 | async-start | bytes 4194304 | tf_op jit(solution)/shard_map/psum | solution.py:41
  144.5 147.4 %all-reduce.5.cloned.1.call-start = ((), (), s32[]{:S(2)}) async-start(), calls=%async_computation.9 | async-start | bytes 524288 | tf_op jit(solution)/shard_map/psum | solution.py:42
  274.3 61.6 %reduce-scatter.9.cloned.1.call-start = ((), (), s32[]{:S(2)}) async-start(), calls=%async_computation.10 | async-start | bytes 1310720 | tf_op jit(solution)/shard_map/reduce_scatter | solution.py:52
  305.9 30.0 %copy-start.1 = (f32[2048,64]{0,1:T(8,128)S(1)}, f32[2048,64]{0,1:T(8,128)}, u32[]{:S(2)}) copy-start(f32[2048,64]{0,1:T(8,128)} %reduce-scatter.5.cloned.1.call-done) | copy-start | bytes 1572868
  307.7 57.2 %all-gather.8.cloned.1.call-start = ((), (), s32[]{:S(2)}) async-start(), calls=%async_computation.11 | async-start | bytes 1310720 | tf_op jit(solution)/shard_map/all_gather | solution.py:56
  337.6 34.3 %copy-start.2 = (bf16[512,256]{0,1:T(8,128)(2,1)S(1)}, bf16[512,256]{0,1:T(8,128)(2,1)}, u32[]{:S(2)}) copy-start(bf16[512,256]{0,1:T(8,128)(2,1)} %all-reduce.5.cloned.1.call-done) | copy-start | bytes 786436
  337.7 61.7 %reduce-scatter.11.cloned.1.call-start = ((), (), s32[]{:S(2)}) async-start(), calls=%async_computation.12 | async-start | bytes 1310720 | tf_op jit(solution)/shard_map/reduce_scatter | solution.py:57
Sparse Core Ops, SparseCore 0:
  9.6 30.6 all-gather.3
  47.7 34.5 reduce-scatter.4
  84.8 26.4 all-gather.5
  114.2 21.8 reduce-scatter.6
  144.6 124.8 all-reduce.2
  274.4 17.4 all-reduce.4
  307.8 28.0 reduce-scatter.8
  338.3 26.4 all-gather.7
  372.0 27.2 reduce-scatter.10
where the time goes:
time: 408 us
  waiting for transfers between devices  340 us (83%)
  matrix products  28.8 us (7%)
  blocking collectives  15.1 us (4%)
  between operations  14.6 us (4%)
  other arithmetic  6.41 us (2%)
    psum x1, waiting for transfers between devices, shards(): sep_mid = lax.psum(sep_part.astype(jnp.bfloat16), ('row', 'col'))  125 us
    reduce_scatter x1, waiting for transfers between devices, shards(): lax.psum_scatter(partial_value, 'row', scatter_dimension=1, tiled=True)  34.7 us
    all_gather x1, waiting for transfers between devices, shards(): lax.all_gather(sketch_leaf, 'col', axis=1, tiled=True)  32.3 us
    reduce_scatter x1, waiting for transfers between devices, shards(): lax.psum_scatter(back_part.astype(jnp.bfloat16), 'row', scatter_dimension...  28.2 us
    all_gather x1, waiting for transfers between devices, shards(): lax.all_gather(leaf_rhs, 'row', axis=1, tiled=True)  27.2 us
    all_gather x1, waiting for transfers between devices, shards(): lax.all_gather(front_z, 'row', axis=1, tiled=True)  27.1 us
    reduce_scatter x1, waiting for transfers between devices, shards(): lax.psum_scatter(out_part.astype(jnp.bfloat16), 'col', scatter_dimension=...  26.5 us
    reduce_scatter x1, waiting for transfers between devices, shards(): lax.psum_scatter(coupled_part, 'col', scatter_dimension=0, tiled=True)  21.7 us
  transfers between devices with their start and end apart: 9, of which 9 were waited for; matrix products, arithmetic and copies ran while one was open for 0% of the time, Pallas kernels for 0%

commit v1 on v0

v1 whole, which is shorter than its diff:
```python
import jax
import jax.numpy as jnp
from jax import lax
from jax.experimental import pallas as pl
from jax.experimental.pallas import tpu as pltpu
from jax.sharding import PartitionSpec as P


PHASES = 1
STREAMS = 2
KERNEL_BYTES = 24 << 20
TILE = 256
COVER = 40
SETTLE = 10**10
F32 = jnp.float32
BF16 = jnp.bfloat16


def dot_nt(left, right):
    return lax.dot_general(left, right, (((1,), (1,)), ((), ())), preferred_element_type=F32)


def dot_nn(left, right):
    return lax.dot_general(left, right, (((1,), (0,)), ((), ())), preferred_element_type=F32)


def call(kernel, outs, index, operands, scratch, flops):
    moved = sum(a.size * a.dtype.itemsize for a in operands)
    return pl.pallas_call(
        kernel,
        out_shape=outs,
        in_specs=[pl.BlockSpec(memory_space=pltpu.SMEM)]
        + [pl.BlockSpec(memory_space=pltpu.VMEM)] * len(operands),
        out_specs=[pl.BlockSpec(memory_space=pltpu.VMEM)] * len(outs),
        scratch_shapes=scratch,
        cost_estimate=pl.CostEstimate(flops=flops, bytes_accessed=moved, transcendentals=0),
        compiler_params=pltpu.CompilerParams(vmem_limit_bytes=KERNEL_BYTES),
    )(index, *operands)


def after(value, *done):
    return lax.optimization_barrier((value, *done))[0]


def settle(index):
    def kernel(index, out):
        for k in range(index.shape[0]):
            out[k] = index[k]

    return pl.pallas_call(
        kernel,
        out_shape=jax.ShapeDtypeStruct(index.shape, index.dtype),
        in_specs=[pl.BlockSpec(memory_space=pltpu.SMEM)],
        out_specs=pl.BlockSpec(memory_space=pltpu.SMEM),
        cost_estimate=pl.CostEstimate(flops=SETTLE, bytes_accessed=64, transcendentals=0),
        name="settle",
    )(index)


def exchange(pieces, axis):
    size = lax.axis_size(axis)
    out = [pieces[0]]
    for o in range(1, size):
        out.append(lax.ppermute(pieces[o], axis, [(i, i ^ o) for i in range(size)]))
    return out


def spread(piece, axis):
    return exchange([piece] * lax.axis_size(axis), axis)


def add_all(pieces):
    total = pieces[0].astype(F32)
    for piece in pieces[1:]:
        total = total + piece.astype(F32)
    return total


def at(index, step):
    return pl.ds(pl.multiple_of(index * step, step), step)


def shape(*dims, dtype=BF16):
    return jax.ShapeDtypeStruct(dims, dtype)


def shards(sketch_leaf, sketch_sep, leaf_inverse, coupling, sep_inverse, front_map):
    n_leaf, n_row, n_col = (lax.axis_size(a) for a in ("leaf", "row", "col"))
    assert n_row == n_col and n_row & (n_row - 1) == 0 and n_leaf & (n_leaf - 1) == 0
    n = n_row
    section, r, c = (lax.axis_index(a) for a in ("leaf", "row", "col"))
    q = r * n_col + c
    rows, width = leaf_inverse.shape
    chunk = sketch_leaf.shape[1] // STREAMS
    cols = chunk * n
    blk = coupling.shape[1] * n_row // front_map.shape[1]
    span = coupling.shape[1]
    sep_rows, sep_width = sep_inverse.shape
    group = sketch_sep.shape[0] // blk
    half = rows // PHASES
    assert rows == width

    slots = [
        jnp.clip(front_map[section ^ o, q] - q * group, 0, group - 1) for o in range(n_leaf)
    ]
    index = settle(jnp.stack([r, c] + slots).astype(jnp.int32))

    def needed(row_end, row_parts, col_parts, limit):
        last = (row_end // blk) * row_parts - 1
        return min(limit, (last // col_parts + 1) * blk)

    def first_row(col_start, row_parts, col_parts, limit):
        return min(limit, (col_start // blk) * col_parts // row_parts * blk)

    def forward_leaf(h, index):
        base = h * half
        depth = needed(base + half, n_col, n_row, width)
        assert depth <= (h + 1) * half

        def kernel(idx, inv, *refs):
            count = n * (h + 1)
            pieces, outs, lhs = refs[:count], refs[count : count + n], refs[count + n]
            for k in range(h + 1):
                for o in range(n):
                    lhs[at(idx[0] ^ o, chunk), k * half : (k + 1) * half] = pieces[k * n + o][...]
            for start in range(0, half, TILE):
                reach = needed(base + start + TILE, n_col, n_row, width)
                acc = dot_nt(
                    lhs[:, :reach], inv[base + start : base + start + TILE, :reach]
                ).astype(BF16)
                for p in range(n):
                    outs[p][:, start : start + TILE] = acc[p * chunk : (p + 1) * chunk]

        return lambda pieces: call(
            kernel, [shape(chunk, half)] * n, index, [leaf_inverse] + pieces,
            [pltpu.VMEM((cols, (h + 1) * half), BF16)], 2 * cols * half * depth,
        )

    def forward_coupling(pieces):
        def kernel(idx, cpl, *refs):
            count = n * PHASES
            pieces, outs = refs[:count], refs[count : count + n]
            lhs, res = refs[count + n :]
            for k in range(PHASES):
                for p in range(n):
                    place = at(idx[0] ^ idx[1] ^ p, chunk)
                    lhs[place, k * half : (k + 1) * half] = pieces[k * n + p][...]
            for s in range(0, span, TILE):
                res[:, s : s + TILE] = dot_nn(lhs[...], cpl[:, s : s + TILE])
            for o in range(n):
                outs[o][...] = res[:, at(idx[1] ^ o, blk)].astype(BF16)

        return call(
            kernel, [shape(cols, blk)] * n, index, [coupling] + pieces,
            [pltpu.VMEM((cols, rows), BF16), pltpu.VMEM((cols, span), F32)],
            COVER * cols * rows * span,
        )

    def sep_rhs(sketch, blocks):
        def kernel(idx, sketch, *refs):
            blocks, outs, rhs = refs[:n_leaf], refs[n_leaf:-1], refs[-1]
            rhs[...] = sketch[...].astype(F32)
            for o in range(n_leaf):
                place = at(idx[2 + o], blk)
                rhs[:, place] = rhs[:, place] - blocks[o][...].astype(F32)
            for k in range(n):
                rounded = rhs[k * chunk : (k + 1) * chunk, :].astype(BF16)
                for axis in range(2):
                    outs[axis][at(idx[axis] ^ k, chunk), :] = rounded

        return call(
            kernel, [shape(cols, sep_width)] * 2, index, [sketch] + blocks,
            [pltpu.VMEM((cols, sep_width), F32)], cols * sep_width,
        )

    def forward_sep(index, base, size, rhs):
        def kernel(idx, inv, lhs, *outs):
            for start in range(0, size, TILE):
                reach = needed(base + start + TILE, n_leaf, n_row * n_col, sep_width)
                acc = dot_nt(
                    lhs[:, :reach], inv[base + start : base + start + TILE, :reach]
                ).astype(BF16)
                for p in range(n):
                    outs[p][:, start : start + TILE] = acc[p * chunk : (p + 1) * chunk]

        return call(
            kernel, [shape(chunk, size)] * n, index, [sep_inverse, rhs], [],
            2 * cols * size * sep_width,
        )

    def reduce_first(size, second, pieces):
        part = size // n

        def kernel(idx, *refs):
            pieces, outs = refs[:n], refs[n:]
            for o in range(n):
                place = at(idx[second] ^ o, part)
                outs[o][...] = add_all([piece[:, place] for piece in pieces]).astype(BF16)

        return call(kernel, [shape(chunk, part)] * n, index, pieces, [], n * chunk * size)

    def backward_sep(base, size, first_axis, pieces, before):
        part = size // n
        given = [] if before is None else [before]

        def kernel(idx, inv, *refs):
            pieces, before, (out, lhs) = refs[:n], refs[n:-2], refs[-2:]
            for p in range(n):
                for o in range(n):
                    place = at(idx[first_axis] ^ p, chunk), at(idx[1 - first_axis] ^ o, part)
                    lhs[place] = pieces[p][o]
            for start in range(0, sep_width, TILE):
                first = max(first_row(start, n_leaf, n_row * n_col, sep_rows) - base, 0)
                stop = start + TILE
                if first < size:
                    acc = dot_nn(lhs[:, first:], inv[base + first : base + size, start:stop])
                else:
                    acc = jnp.zeros((cols, TILE), F32)
                for old in before:
                    acc = acc + old[:, start:stop]
                out[:, start:stop] = acc

        return call(
            kernel, [shape(cols, sep_width, dtype=F32)], index, [sep_inverse] + pieces + given,
            [pltpu.VMEM((cols, size), BF16)], 2 * cols * size * sep_width,
        )[0]

    def pull(parts):
        def kernel(idx, *refs):
            parts, out, pulled = refs[:n_leaf], refs[n_leaf], refs[n_leaf + 1]
            out[...] = add_all([ref[...] for ref in parts])
            pulled[...] = out[:, at(idx[2], blk)].astype(BF16)

        return call(
            kernel, [shape(cols, sep_width, dtype=F32), shape(cols, blk)], index, parts, [],
            cols * sep_width,
        )

    def backward_coupling(h, pieces):
        base = h * half

        def kernel(idx, cpl, *refs):
            pieces, outs, lhs = refs[:n], refs[n : 2 * n], refs[2 * n]
            for o in range(n):
                for k in range(n):
                    lhs[at(idx[0] ^ idx[1] ^ k, chunk), at(idx[1] ^ o, blk)] = pieces[o][
                        k * chunk : (k + 1) * chunk, :
                    ]
            for start in range(0, half, TILE):
                acc = dot_nt(lhs[...], cpl[base + start : base + start + TILE, :]).astype(BF16)
                for p in range(n):
                    outs[p][:, start : start + TILE] = acc[p * chunk : (p + 1) * chunk]

        return call(
            kernel, [shape(chunk, half)] * n, index, [coupling] + pieces,
            [pltpu.VMEM((cols, span), BF16)], COVER * cols * half * span,
        )

    def backward_leaf(index, h, pieces):
        base = h * half
        later = PHASES - h

        def kernel(idx, inv, *refs):
            count = n * later
            pieces, outs, lhs = refs[:count], refs[count : count + n], refs[count + n]
            for k in range(later):
                for p in range(n):
                    lhs[at(idx[0] ^ p, chunk), k * half : (k + 1) * half] = pieces[k * n + p][...]
            for start in range(0, half, TILE):
                first = first_row(base + start, n_col, n_row, rows)
                assert first >= base
                acc = dot_nn(
                    lhs[:, first - base :], inv[first:, base + start : base + start + TILE]
                ).astype(BF16)
                for o in range(n):
                    outs[o][:, start : start + TILE] = acc[o * chunk : (o + 1) * chunk]

        return call(
            kernel, [shape(chunk, half)] * n, index, [leaf_inverse] + pieces,
            [pltpu.VMEM((cols, later * half), BF16)], 2 * cols * half * half * later,
        )

    leaf_t = sketch_leaf.T
    sep_t = sketch_sep.T.reshape(n, STREAMS, chunk, sep_width)

    def stream(h):
        source = leaf_t[h * chunk : (h + 1) * chunk]
        if h:
            source = after(source, *arrived[-1][1:])
        pieces = spread(source, "col")
        arrived.append(pieces)
        parts = forward_leaf(0, index)(pieces)
        front = add_all(exchange(parts, "row")).astype(BF16)
        parts = forward_coupling(spread(front, "row"))
        coupled = add_all(exchange(parts, "col")).astype(BF16)
        sketch = sep_t[:, h].reshape(cols, sep_width)
        rhs = sep_rhs(sketch, spread(coupled, "leaf"))
        parts = exchange(forward_sep(index, 0, sep_rows, rhs[0]), "row")
        parts = exchange(reduce_first(sep_rows, 1, parts), "col")
        mid = add_all(parts).astype(BF16)
        pieces = spread(jnp.stack(spread(mid, "col")), "row")
        total = backward_sep(0, sep_rows, 0, pieces, None)
        out_sep, pulled = pull(spread(total, "leaf"))
        parts = backward_coupling(0, spread(pulled, "col"))
        back = add_all(exchange(parts, "row"))
        leaf_rhs = (front.astype(F32) - back).astype(BF16)
        parts = backward_leaf(index, 0, spread(leaf_rhs, "row"))
        return add_all(exchange(parts, "col")), out_sep

    arrived = []
    results = [stream(h) for h in range(STREAMS)]
    out_leaf = jnp.concatenate([leaf for leaf, _ in results], axis=0)
    out_sep = jnp.stack([sep.reshape(n, chunk, sep_width) for _, sep in results], axis=1)
    return out_leaf.T, out_sep.reshape(sketch_sep.shape[1], sep_width).T


def solution(mesh):
    placed = (
        P(("leaf", "row"), "col"),
        P(("row", "col"), None),
        P(("leaf", "col"), "row"),
        P(("leaf", "col"), "row"),
        P("leaf", ("row", "col")),
        P(),
    )

    return jax.shard_map(
        shards,
        mesh=mesh,
        in_specs=placed,
        out_specs=(P(("leaf", "row"), "col"), P(("row", "col"), None)),
        check_vma=False,
    )
```

time: 408 us -> 192 us (0.47)
  waiting for transfers between devices: 340 us -> 52.6 us
  starting transfers between devices: 0.37 us -> 96.3 us
  matrix products: 28.8 us -> 0 us
  Pallas kernels: 0 us -> 23.8 us
  blocking collectives: 15.1 us -> 0 us
  between operations: 14.6 us -> 2.23 us
  local copies, waits for them, and re-layouts: 2.67 us -> 14.3 us
  other arithmetic: 6.41 us -> 2.14 us
    psum x2 -> x0, waiting for transfers between devices: 141 us -> none  [the longest x1 125 us: shards(): sep_mid = lax.psum(sep_part.astype(jnp.bfloat16), ('row', 'col'))]
    reduce_scatter x4 -> x0, waiting for transfers between devices: 111 us -> none  [the longest x1 34.7 us: shards(): lax.psum_scatter(partial_value, 'row', scatter_dimension=1, tiled=True)]
    ppermute x0 -> x76, starting transfers between devices: none -> 96.3 us  [exchange(): out.append(lax.ppermute(pieces[o], axis, [(i, i ^ o) for i in range(size)]))]
    all_gather x3 -> x0, waiting for transfers between devices: 86.6 us -> none  [the longest x1 32.3 us: shards(): lax.all_gather(sketch_leaf, 'col', axis=1, tiled=True)]
    ppermute x0 -> x76, waiting for transfers between devices: none -> 52.6 us  [exchange(): out.append(lax.ppermute(pieces[o], axis, [(i, i ^ o) for i in range(size)]))]
    dot_general x7 -> x0, matrix products: 28.8 us -> none  [the longest x3 14.5 us: contract_rows(): lax.dot_general(left, right, (((0,), (0,)), ((), ())), preferred_element_...]
    pallas_call x0 -> x19, Pallas kernels: none -> 23.8 us  [the longest x18 22.4 us: call(): pl.pallas_call(kernel, out_shape=outs, in_specs=[pl.BlockSpec(memory_spac...]
    all_gather x2 -> x0, blocking collectives: 15.1 us -> none  [the longest x1 13.1 us: shards(): lax.all_gather(pulled, 'col', axis=0, tiled=True)]
  transfers between devices with their start and end apart: 9 -> 76, of which waited for: 9 -> 26; matrix products, arithmetic and copies ran while one was open for 0% -> 2% of each run, Pallas kernels for 0% -> 10%
where the time goes in v1:
time: 192 us; the launch traced here: 191 us
  starting transfers between devices  96.3 us (50%)
  waiting for transfers between devices  52.6 us (27%)
  Pallas kernels  23.8 us (12%)
  local copies, waits for them, and re-layouts  14.3 us (7%)
  between operations  2.23 us (1%)
  other arithmetic  2.14 us (1%)
    ppermute x76, starting transfers between devices, exchange(): out.append(lax.ppermute(pieces[o], axis, [(i, i ^ o) for i in range(size)]))  96.3 us
    ppermute x76, waiting for transfers between devices, exchange(): out.append(lax.ppermute(pieces[o], axis, [(i, i ^ o) for i in range(size)]))  52.6 us
    pallas_call x18, Pallas kernels, call(): pl.pallas_call(kernel, out_shape=outs, in_specs=[pl.BlockSpec(memory_spac...  22.4 us
    unnamed x22, local copies, waits for them, and re-layouts  12 us
  transfers between devices with their start and end apart: 76, of which 26 were waited for; matrix products, arithmetic and copies ran while one was open for 2% of the time, Pallas kernels for 10%

profile of v1, /device:TPU:0, one launch (start us, length us, event | category | flops | bytes accessed | tf_op | source)
XLA Modules:
  0.0 191.4 jit_solution(7567059446179561270)
XLA Ops:
  1.6 5.1 %collective-permute-start.2 = (bf16[32,2048]{1,0:T(8,128)(2,1)S(1)}, bf16[32,2048]{1,0:T(8,128)(2,1)S(1)}, u32[]{:S(2)}, u32[]{:S(2)}) collective-permute-start(bf16[32,2048]{1,0:T(8,128)(2,1)S(1)} %get-tuple-element.116.refs_0_), channel_id=1, source_target_pairs={{0,3},{1,2},{2,1},{3,0},{4,7},{5,6},{6,5},{7,4},{8,11},{9,10},{10,... | collective-permute-start | bytes 393224 | tf_op jit(solution)/shard_map/ppermute | solution.py:64
  11.9 5.9 %collective-permute-done.1.refs_2_ = bf16[32,2048]{1,0:T(8,128)(2,1)S(1)} collective-permute-done((bf16[32,2048]{1,0:T(8,128)(2,1)S(1)}, bf16[32,2048]{1,0:T(8,128)(2,1)S(1)}, u32[]{:S(2)}, u32[]{:S(2)}) %collective-permute-start.1) | collective-permute-done | bytes 131104 | tf_op jit(solution)/shard_map/ppermute | solution.py:64
  17.8 3.4 %copy-done = bf16[2048,2048]{1,0:T(8,128)(2,1)S(1)} copy-done((bf16[2048,2048]{1,0:T(8,128)(2,1)S(1)}, bf16[2048,2048]{1,0:T(8,128)(2,1)}, u32[]{:S(2)}) %copy-start) | copy-done | bytes 8388632
  21.9 2.2 %shard_map.77 = (bf16[32,2048]{1,0:T(8,128)(2,1)S(1)}, bf16[32,2048]{1,0:T(8,128)(2,1)S(1)}, bf16[32,2048]{1,0:T(8,128)(2,1)S(1)}, bf16[32,2048]{1,0:T(8,128)(2,1)S(1)}) custom-call(s32[4]{0:T(128)S(1)} %copy-done.4, bf16[2048,2048]{1,0:T(8,128)(2,1)S(1)} %copy-done, bf16[32,2048]{1,0:T(8,128)(2,1)S(1)} %get-tuple-element.116.refs_0_, ...), custom_call_target="tpu_custom_call" | custom-call | flops 1073741824 | bytes 8912896 | tf_op jit(solution)/shard_map/pallas_call | solution.py:29
  24.1 1.6 collective-permute-start.3
  25.6 1.5 collective-permute-start.4
  27.6 2.5 %collective-permute-start.40 = (bf16[32,2048]{1,0:T(8,128)(2,1)S(1)}, bf16[32,2048]{1,0:T(8,128)(2,1)S(1)}, u32[]{:S(2)}, u32[]{:S(2)}) collective-permute-start(bf16[32,2048]{1,0:T(8,128)(2,1)S(1)} %get-tuple-element.83.refs_0_), channel_id=1, source_target_pairs={{0,3},{1,2},{2,1},{3,0},{4,7},{5,6},{6,5},{7,4},{8,11},{9,10},{10,... | collective-permute-start | bytes 393224 | tf_op jit(solution)/shard_map/ppermute | solution.py:64
  30.1 1.9 collective-permute-start.38
  37.5 2.7 %collective-permute-done.39.refs_2_ = bf16[32,2048]{1,0:T(8,128)(2,1)S(1)} collective-permute-done((bf16[32,2048]{1,0:T(8,128)(2,1)S(1)}, bf16[32,2048]{1,0:T(8,128)(2,1)S(1)}, u32[]{:S(2)}, u32[]{:S(2)}) %collective-permute-start.39) | collective-permute-done | bytes 131104 | tf_op jit(solution)/shard_map/ppermute | solution.py:64
  40.2 3.4 %copy-done.1 = bf16[2048,2048]{1,0:T(8,128)(2,1)S(1)} copy-done((bf16[2048,2048]{1,0:T(8,128)(2,1)S(1)}, bf16[2048,2048]{1,0:T(8,128)(2,1)}, u32[]{:S(2)}) %copy-start.1) | copy-done | bytes 8388632
  43.6 2.2 %shard_map.86 = (bf16[32,2048]{1,0:T(8,128)(2,1)S(1)}, bf16[32,2048]{1,0:T(8,128)(2,1)S(1)}, bf16[32,2048]{1,0:T(8,128)(2,1)S(1)}, bf16[32,2048]{1,0:T(8,128)(2,1)S(1)}) custom-call(s32[4]{0:T(128)S(1)} %copy-done.5, bf16[2048,2048]{1,0:T(8,128)(2,1)S(1)} %copy-done.1, bf16[32,2048]{1,0:T(8,128)(2,1)S(1)} %get-tuple-element.83.refs_0_, ...), custom_call_target="tpu_custom_call" | custom-call | flops 1073741824 | bytes 8912896 | tf_op jit(solution)/shard_map/pallas_call | solution.py:29
  45.8 1.6 collective-permute-start.41
  47.4 1.5 collective-permute-start.42
  52.7 2.2 %collective-permute-start.11 = (bf16[128,128]{1,0:T(8,128)(2,1)S(1)}, bf16[128,128]{1,0:T(8,128)(2,1)S(1)}, u32[]{:S(2)}, u32[]{:S(2)}) collective-permute-start(bf16[128,128]{1,0:T(8,128)(2,1)S(1)} %get-tuple-element.64), channel_id=1, source_target_pairs={{0,3},{1,2},{2,1},{3,0},{4,7},{5,6},{6,5},{7,4},{8,11},{9,10},{10,... | collective-permute-start | bytes 98312 | tf_op jit(solution)/shard_map/ppermute | solution.py:64
  55.1 2.4 %collective-permute-start.46 = (bf16[32,2048]{1,0:T(8,128)(2,1)S(1)}, bf16[32,2048]{1,0:T(8,128)(2,1)S(1)}, u32[]{:S(2)}, u32[]{:S(2)}) collective-permute-start(bf16[32,2048]{1,0:T(8,128)(2,1)S(1)} %add_convert_fusion.refs_0_), channel_id=1, source_target_pairs={{0,12},{4,8},{8,4},{12,0},{1,13},{5,9},{9,5},{13,1},{2,14},{6,10},... | collective-permute-start | bytes 393224 | tf_op jit(solution)/shard_map/ppermute | solution.py:64
  64.1 2.2 %collective-permute-start.48 = (bf16[128,128]{1,0:T(8,128)(2,1)S(1)}, bf16[128,128]{1,0:T(8,128)(2,1)S(1)}, u32[]{:S(2)}, u32[]{:S(2)}) collective-permute-start(bf16[128,128]{1,0:T(8,128)(2,1)S(1)} %get-tuple-element.90), channel_id=1, source_target_pairs={{0,2},{1,3},{2,0},{3,1},{4,6},{5,7},{6,4},{7,5},{8,10},{9,11},{10,... | collective-permute-start | bytes 98312 | tf_op jit(solution)/shard_map/ppermute | solution.py:64
  66.3 2.2 %collective-permute-start.49 = (bf16[128,128]{1,0:T(8,128)(2,1)S(1)}, bf16[128,128]{1,0:T(8,128)(2,1)S(1)}, u32[]{:S(2)}, u32[]{:S(2)}) collective-permute-start(bf16[128,128]{1,0:T(8,128)(2,1)S(1)} %get-tuple-element.91), channel_id=1, source_target_pairs={{0,3},{1,2},{2,1},{3,0},{4,7},{5,6},{6,5},{7,4},{8,11},{9,10},{10,... | collective-permute-start | bytes 98312 | tf_op jit(solution)/shard_map/ppermute | solution.py:64
  68.5 1.5 shard_map.80
  76.1 2.5 %collective-permute-done.13.refs_1_ = bf16[32,4096]{1,0:T(8,128)(2,1)S(1)} collective-permute-done((bf16[32,4096]{1,0:T(8,128)(2,1)S(1)}, bf16[32,4096]{1,0:T(8,128)(2,1)S(1)}, u32[]{:S(2)}, u32[]{:S(2)}) %collective-permute-start.13) | collective-permute-done | bytes 262176 | tf_op jit(solution)/shard_map/ppermute | solution.py:64
  78.7 4.0 %collective-permute-done.14.refs_2_ = bf16[32,4096]{1,0:T(8,128)(2,1)S(1)} collective-permute-done((bf16[32,4096]{1,0:T(8,128)(2,1)S(1)}, bf16[32,4096]{1,0:T(8,128)(2,1)S(1)}, u32[]{:S(2)}, u32[]{:S(2)}) %collective-permute-start.14) | collective-permute-done | bytes 262176 | tf_op jit(solution)/shard_map/ppermute | solution.py:64
  83.4 2.6 %collective-permute-start.17 = (bf16[32,1024]{1,0:T(8,128)(2,1)S(1)}, bf16[32,1024]{1,0:T(8,128)(2,1)S(1)}, u32[]{:S(2)}, u32[]{:S(2)}) collective-permute-start(bf16[32,1024]{1,0:T(8,128)(2,1)S(1)} %get-tuple-element.72), channel_id=1, source_target_pairs={{0,2},{1,3},{2,0},{3,1},{4,6},{5,7},{6,4},{7,5},{8,10},{9,11},{10,... | collective-permute-start | bytes 196616 | tf_op jit(solution)/shard_map/ppermute | solution.py:64
  86.0 1.8 collective-permute-start.18
  87.7 1.5 shard_map.89
  89.3 1.6 collective-permute-start.51
  92.9 2.1 %collective-permute-start.21 = (bf16[32,1024]{1,0:T(8,128)(2,1)S(1)}, bf16[32,1024]{1,0:T(8,128)(2,1)S(1)}, u32[]{:S(2)}, u32[]{:S(2)}) collective-permute-start(bf16[32,1024]{1,0:T(8,128)(2,1)S(1)} %add_convert_fusion.3), channel_id=1, source_target_pairs={{0,3},{1,2},{2,1},{3,0},{4,7},{5,6},{6,5},{7,4},{8,11},{9,10},{10,... | collective-permute-start | bytes 196616 | tf_op jit(solution)/shard_map/ppermute | solution.py:64
  95.0 1.6 collective-permute-done.51.refs_1_
  97.3 3.5 %collective-permute-done.52.refs_2_ = bf16[32,4096]{1,0:T(8,128)(2,1)S(1)} collective-permute-done((bf16[32,4096]{1,0:T(8,128)(2,1)S(1)}, bf16[32,4096]{1,0:T(8,128)(2,1)S(1)}, u32[]{:S(2)}, u32[]{:S(2)}) %collective-permute-start.52) | collective-permute-done | bytes 262176 | tf_op jit(solution)/shard_map/ppermute | solution.py:64
  101.6 2.9 %collective-permute-start.55 = (bf16[32,1024]{1,0:T(8,128)(2,1)S(1)}, bf16[32,1024]{1,0:T(8,128)(2,1)S(1)}, u32[]{:S(2)}, u32[]{:S(2)}) collective-permute-start(bf16[32,1024]{1,0:T(8,128)(2,1)S(1)} %get-tuple-element.99), channel_id=1, source_target_pairs={{0,2},{1,3},{2,0},{3,1},{4,6},{5,7},{6,4},{7,5},{8,10},{9,11},{10,... | collective-permute-start | bytes 196616 | tf_op jit(solution)/shard_map/ppermute | solution.py:64
  106.0 1.5 collective-permute-start.24
  107.6 3.0 %collective-permute-done.56 = bf16[32,1024]{1,0:T(8,128)(2,1)S(1)} collective-permute-done((bf16[32,1024]{1,0:T(8,128)(2,1)S(1)}, bf16[32,1024]{1,0:T(8,128)(2,1)S(1)}, u32[]{:S(2)}, u32[]{:S(2)}) %collective-permute-start.56) | collective-permute-done | bytes 65568 | tf_op jit(solution)/shard_map/ppermute | solution.py:64
  110.6 1.6 collective-permute-start.59
  112.3 2.8 %collective-permute-start.57 = (bf16[32,1024]{1,0:T(8,128)(2,1)S(1)}, bf16[32,1024]{1,0:T(8,128)(2,1)S(1)}, u32[]{:S(2)}, u32[]{:S(2)}) collective-permute-start(bf16[32,1024]{1,0:T(8,128)(2,1)S(1)} %add_convert_fusion.2), channel_id=1, source_target_pairs={{0,1},{1,0},{2,3},{3,2},{4,5},{5,4},{6,7},{7,6},{8,9},{9,8},{10,11... | collective-permute-start | bytes 196616 | tf_op jit(solution)/shard_map/ppermute | solution.py:64
  118.2 2.2 %collective-permute-start.62 = (bf16[4,32,1024]{2,1,0:T(8,128)(2,1)S(1)}, bf16[4,32,1024]{2,1,0:T(8,128)(2,1)S(1)}, u32[]{:S(2)}, u32[]{:S(2)}) collective-permute-start(bf16[4,32,1024]{2,1,0:T(8,128)(2,1)S(1)} %pad_maximum_fusion.2.refs_0_), channel_id=1, source_target_pairs={{0,12},{4,8},{8,4},{12,0},{1,13},{5,9},{9,5},{13,1},{2,14},{6,10},... | collective-permute-start | bytes 786440 | tf_op jit(solution)/shard_map/ppermute | solution.py:64
  121.8 4.1 %collective-permute-done.23.refs_2_ = bf16[4,32,1024]{2,1,0:T(8,128)(2,1)S(1)} collective-permute-done((bf16[4,32,1024]{2,1,0:T(8,128)(2,1)S(1)}, bf16[4,32,1024]{2,1,0:T(8,128)(2,1)S(1)}, u32[]{:S(2)}, u32[]{:S(2)}) %collective-permute-start.23) | collective-permute-done | bytes 262176 | tf_op jit(solution)/shard_map/ppermute | solution.py:64
  127.3 2.4 %collective-permute-done.62.refs_3_ = bf16[4,32,1024]{2,1,0:T(8,128)(2,1)S(1)} collective-permute-done((bf16[4,32,1024]{2,1,0:T(8,128)(2,1)S(1)}, bf16[4,32,1024]{2,1,0:T(8,128)(2,1)S(1)}, u32[]{:S(2)}, u32[]{:S(2)}) %collective-permute-start.62) | collective-permute-done | bytes 262176 | tf_op jit(solution)/shard_map/ppermute | solution.py:64
  129.7 1.8 collective-permute-done.61.refs_2_
  135.5 3.5 %collective-permute-start.26 = (bf16[128,128]{1,0:T(8,128)(2,1)S(1)}, bf16[128,128]{1,0:T(8,128)(2,1)S(1)}, u32[]{:S(2)}, u32[]{:S(2)}) collective-permute-start(bf16[128,128]{1,0:T(8,128)(2,1)S(1)} %get-tuple-element.74.refs_0_), channel_id=1, source_target_pairs={{0,1},{1,0},{2,3},{3,2},{4,5},{5,4},{6,7},{7,6},{8,9},{9,8},{10,11... | collective-permute-start | bytes 98312 | tf_op jit(solution)/shard_map/ppermute | solution.py:64
  141.1 2.9 %collective-permute-start.64 = (bf16[128,128]{1,0:T(8,128)(2,1)S(1)}, bf16[128,128]{1,0:T(8,128)(2,1)S(1)}, u32[]{:S(2)}, u32[]{:S(2)}) collective-permute-start(bf16[128,128]{1,0:T(8,128)(2,1)S(1)} %get-tuple-element.101.refs_0_), channel_id=1, source_target_pairs={{0,1},{1,0},{2,3},{3,2},{4,5},{5,4},{6,7},{7,6},{8,9},{9,8},{10,11... | collective-permute-start | bytes 98312 | tf_op jit(solution)/shard_map/ppermute | solution.py:64
  147.1 1.8 collective-permute-start.31
  152.0 1.8 collective-permute-start.69
  154.5 1.9 collective-permute-start.34
  158.1 4.5 %collective-permute-done.68 = bf16[32,2048]{1,0:T(8,128)(2,1)S(1)} collective-permute-done((bf16[32,2048]{1,0:T(8,128)(2,1)S(1)}, bf16[32,2048]{1,0:T(8,128)(2,1)S(1)}, u32[]{:S(2)}, u32[]{:S(2)}) %collective-permute-start.68) | collective-permute-done | bytes 131104 | tf_op jit(solution)/shard_map/ppermute | solution.py:64
  164.0 2.0 %collective-permute-start.71 = (bf16[32,2048]{1,0:T(8,128)(2,1)S(1)}, bf16[32,2048]{1,0:T(8,128)(2,1)S(1)}, u32[]{:S(2)}, u32[]{:S(2)}) collective-permute-start(bf16[32,2048]{1,0:T(8,128)(2,1)S(1)} %subtract_convert_fusion.refs_0_), channel_id=1, source_target_pairs={{0,8},{4,12},{8,0},{12,4},{1,9},{5,13},{9,1},{13,5},{2,10},{6,14},... | collective-permute-start | bytes 393224 | tf_op jit(solution)/shard_map/ppermute | solution.py:64
  169.9 2.9 %collective-permute-start.37 = (bf16[32,2048]{1,0:T(8,128)(2,1)S(1)}, bf16[32,2048]{1,0:T(8,128)(2,1)S(1)}, u32[]{:S(2)}, u32[]{:S(2)}) collective-permute-start(bf16[32,2048]{1,0:T(8,128)(2,1)S(1)} %get-tuple-element.82), channel_id=1, source_target_pairs={{0,3},{1,2},{2,1},{3,0},{4,7},{5,6},{6,5},{7,4},{8,11},{9,10},{10,... | collective-permute-start | bytes 393224 | tf_op jit(solution)/shard_map/ppermute | solution.py:64
  173.8 3.4 %copy-done.2 = bf16[2048,2048]{1,0:T(8,128)(2,1)S(1)} copy-done((bf16[2048,2048]{1,0:T(8,128)(2,1)S(1)}, bf16[2048,2048]{1,0:T(8,128)(2,1)}, u32[]{:S(2)}) %copy-start.2) | copy-done | bytes 8388632
  180.2 2.9 %collective-permute-start.75 = (bf16[32,2048]{1,0:T(8,128)(2,1)S(1)}, bf16[32,2048]{1,0:T(8,128)(2,1)S(1)}, u32[]{:S(2)}, u32[]{:S(2)}) collective-permute-start(bf16[32,2048]{1,0:T(8,128)(2,1)S(1)} %get-tuple-element.109), channel_id=1, source_target_pairs={{0,3},{1,2},{2,1},{3,0},{4,7},{5,6},{6,5},{7,4},{8,11},{9,10},{10,... | collective-permute-start | bytes 393224 | tf_op jit(solution)/shard_map/ppermute | solution.py:64
  183.2 2.1 %collective-permute-done.73 = bf16[32,2048]{1,0:T(8,128)(2,1)S(1)} collective-permute-done((bf16[32,2048]{1,0:T(8,128)(2,1)S(1)}, bf16[32,2048]{1,0:T(8,128)(2,1)S(1)}, u32[]{:S(2)}, u32[]{:S(2)}) %collective-permute-start.73) | collective-permute-done | bytes 131104 | tf_op jit(solution)/shard_map/ppermute | solution.py:64
  185.2 5.2 %collective-permute-done.74 = bf16[32,2048]{1,0:T(8,128)(2,1)S(1)} collective-permute-done((bf16[32,2048]{1,0:T(8,128)(2,1)S(1)}, bf16[32,2048]{1,0:T(8,128)(2,1)S(1)}, u32[]{:S(2)}, u32[]{:S(2)}) %collective-permute-start.74) | collective-permute-done | bytes 131104 | tf_op jit(solution)/shard_map/ppermute | solution.py:64
  (164 shorter events, 64.5 us)
Async XLA Ops:
  1.6 10.3 %collective-permute-start.2 = (bf16[32,2048]{1,0:T(8,128)(2,1)S(1)}, bf16[32,2048]{1,0:T(8,128)(2,1)S(1)}, u32[]{:S(2)}, u32[]{:S(2)}) collective-permute-start(bf16[32,2048]{1,0:T(8,128)(2,1)S(1)} %get-tuple-element.116.refs_0_), channel_id=1, source_target_pairs={{0,3},{1,2},{2,1},{3,0},{4,7},{5,6},{6,5},{7,4},{8,11},{9,10},{10,... | collective-permute-start | bytes 393224 | tf_op jit(solution)/shard_map/ppermute | solution.py:64
  6.8 11.1 %collective-permute-start.1 = (bf16[32,2048]{1,0:T(8,128)(2,1)S(1)}, bf16[32,2048]{1,0:T(8,128)(2,1)S(1)}, u32[]{:S(2)}, u32[]{:S(2)}) collective-permute-start(bf16[32,2048]{1,0:T(8,128)(2,1)S(1)} %get-tuple-element.116.refs_0_), channel_id=1, source_target_pairs={{0,2},{1,3},{2,0},{3,1},{4,6},{5,7},{6,4},{7,5},{8,10},{9,11},{10,... | collective-permute-start | bytes 393224 | tf_op jit(solution)/shard_map/ppermute | solution.py:64
  6.8 11.1 %collective-permute-start = (bf16[32,2048]{1,0:T(8,128)(2,1)S(1)}, bf16[32,2048]{1,0:T(8,128)(2,1)S(1)}, u32[]{:S(2)}, u32[]{:S(2)}) collective-permute-start(bf16[32,2048]{1,0:T(8,128)(2,1)S(1)} %get-tuple-element.116.refs_0_), channel_id=1, source_target_pairs={{0,1},{1,0},{2,3},{3,2},{4,5},{5,4},{6,7},{7,6},{8,9},{9,8},{10,11... | collective-permute-start | bytes 393224 | tf_op jit(solution)/shard_map/ppermute | solution.py:64
  25.6 7.8 %collective-permute-start.4 = (bf16[32,2048]{1,0:T(8,128)(2,1)S(1)}, bf16[32,2048]{1,0:T(8,128)(2,1)S(1)}, u32[]{:S(2)}, u32[]{:S(2)}) collective-permute-start(bf16[32,2048]{1,0:T(8,128)(2,1)S(1)} %get-tuple-element.59), channel_id=1, source_target_pairs={{0,8},{4,12},{8,0},{12,4},{1,9},{5,13},{9,1},{13,5},{2,10},{6,14},... | collective-permute-start | bytes 393224 | tf_op jit(solution)/shard_map/ppermute | solution.py:64
  27.6 8.2 %collective-permute-start.40 = (bf16[32,2048]{1,0:T(8,128)(2,1)S(1)}, bf16[32,2048]{1,0:T(8,128)(2,1)S(1)}, u32[]{:S(2)}, u32[]{:S(2)}) collective-permute-start(bf16[32,2048]{1,0:T(8,128)(2,1)S(1)} %get-tuple-element.83.refs_0_), channel_id=1, source_target_pairs={{0,3},{1,2},{2,1},{3,0},{4,7},{5,6},{6,5},{7,4},{8,11},{9,10},{10,... | collective-permute-start | bytes 393224 | tf_op jit(solution)/shard_map/ppermute | solution.py:64
  30.1 10.1 %collective-permute-start.39 = (bf16[32,2048]{1,0:T(8,128)(2,1)S(1)}, bf16[32,2048]{1,0:T(8,128)(2,1)S(1)}, u32[]{:S(2)}, u32[]{:S(2)}) collective-permute-start(bf16[32,2048]{1,0:T(8,128)(2,1)S(1)} %get-tuple-element.83.refs_0_), channel_id=1, source_target_pairs={{0,2},{1,3},{2,0},{3,1},{4,6},{5,7},{6,4},{7,5},{8,10},{9,11},{10,... | collective-permute-start | bytes 393224 | tf_op jit(solution)/shard_map/ppermute | solution.py:64
  30.1 10.1 %collective-permute-start.38 = (bf16[32,2048]{1,0:T(8,128)(2,1)S(1)}, bf16[32,2048]{1,0:T(8,128)(2,1)S(1)}, u32[]{:S(2)}, u32[]{:S(2)}) collective-permute-start(bf16[32,2048]{1,0:T(8,128)(2,1)S(1)} %get-tuple-element.83.refs_0_), channel_id=1, source_target_pairs={{0,1},{1,0},{2,3},{3,2},{4,5},{5,4},{6,7},{7,6},{8,9},{9,8},{10,11... | collective-permute-start | bytes 393224 | tf_op jit(solution)/shard_map/ppermute | solution.py:64
  33.5 15.4 %collective-permute-start.8 = (bf16[32,2048]{1,0:T(8,128)(2,1)S(1)}, bf16[32,2048]{1,0:T(8,128)(2,1)S(1)}, u32[]{:S(2)}, u32[]{:S(2)}) collective-permute-start(bf16[32,2048]{1,0:T(8,128)(2,1)S(1)} %add_convert_fusion.1.refs_0_), channel_id=1, source_target_pairs={{0,12},{4,8},{8,4},{12,0},{1,13},{5,9},{9,5},{13,1},{2,14},{6,10},... | collective-permute-start | bytes 393224 | tf_op jit(solution)/shard_map/ppermute | solution.py:64
  34.6 14.7 %collective-permute-start.7 = (bf16[32,2048]{1,0:T(8,128)(2,1)S(1)}, bf16[32,2048]{1,0:T(8,128)(2,1)S(1)}, u32[]{:S(2)}, u32[]{:S(2)}) collective-permute-start(bf16[32,2048]{1,0:T(8,128)(2,1)S(1)} %add_convert_fusion.1.refs_0_), channel_id=1, source_target_pairs={{0,8},{4,12},{8,0},{12,4},{1,9},{5,13},{9,1},{13,5},{2,10},{6,14},... | collective-permute-start | bytes 393224 | tf_op jit(solution)/shard_map/ppermute | solution.py:64
  35.8 13.5 %collective-permute-start.6 = (bf16[32,2048]{1,0:T(8,128)(2,1)S(1)}, bf16[32,2048]{1,0:T(8,128)(2,1)S(1)}, u32[]{:S(2)}, u32[]{:S(2)}) collective-permute-start(bf16[32,2048]{1,0:T(8,128)(2,1)S(1)} %add_convert_fusion.1.refs_0_), channel_id=1, source_target_pairs={{0,4},{4,0},{8,12},{12,8},{1,5},{5,1},{9,13},{13,9},{2,6},{6,2},{1... | collective-permute-start | bytes 393224 | tf_op jit(solution)/shard_map/ppermute | solution.py:64
  47.4 7.6 %collective-permute-start.42 = (bf16[32,2048]{1,0:T(8,128)(2,1)S(1)}, bf16[32,2048]{1,0:T(8,128)(2,1)S(1)}, u32[]{:S(2)}, u32[]{:S(2)}) collective-permute-start(bf16[32,2048]{1,0:T(8,128)(2,1)S(1)} %get-tuple-element.86), channel_id=1, source_target_pairs={{0,8},{4,12},{8,0},{12,4},{1,9},{5,13},{9,1},{13,5},{2,10},{6,14},... | collective-permute-start | bytes 393224 | tf_op jit(solution)/shard_map/ppermute | solution.py:64
  50.4 7.6 %collective-permute-start.9 = (bf16[128,128]{1,0:T(8,128)(2,1)S(1)}, bf16[128,128]{1,0:T(8,128)(2,1)S(1)}, u32[]{:S(2)}, u32[]{:S(2)}) collective-permute-start(bf16[128,128]{1,0:T(8,128)(2,1)S(1)} %get-tuple-element.62), channel_id=1, source_target_pairs={{0,1},{1,0},{2,3},{3,2},{4,5},{5,4},{6,7},{7,6},{8,9},{9,8},{10,11... | collective-permute-start | bytes 98312 | tf_op jit(solution)/shard_map/ppermute | solution.py:64
  64.1 8.1 %collective-permute-start.47 = (bf16[128,128]{1,0:T(8,128)(2,1)S(1)}, bf16[128,128]{1,0:T(8,128)(2,1)S(1)}, u32[]{:S(2)}, u32[]{:S(2)}) collective-permute-start(bf16[128,128]{1,0:T(8,128)(2,1)S(1)} %get-tuple-element.89), channel_id=1, source_target_pairs={{0,1},{1,0},{2,3},{3,2},{4,5},{5,4},{6,7},{7,6},{8,9},{9,8},{10,11... | collective-permute-start | bytes 98312 | tf_op jit(solution)/shard_map/ppermute | solution.py:64
  64.1 9.5 %collective-permute-start.48 = (bf16[128,128]{1,0:T(8,128)(2,1)S(1)}, bf16[128,128]{1,0:T(8,128)(2,1)S(1)}, u32[]{:S(2)}, u32[]{:S(2)}) collective-permute-start(bf16[128,128]{1,0:T(8,128)(2,1)S(1)} %get-tuple-element.90), channel_id=1, source_target_pairs={{0,2},{1,3},{2,0},{3,1},{4,6},{5,7},{6,4},{7,5},{8,10},{9,11},{10,... | collective-permute-start | bytes 98312 | tf_op jit(solution)/shard_map/ppermute | solution.py:64
  70.0 8.6 %collective-permute-start.13 = (bf16[32,4096]{1,0:T(8,128)(2,1)S(1)}, bf16[32,4096]{1,0:T(8,128)(2,1)S(1)}, u32[]{:S(2)}, u32[]{:S(2)}) collective-permute-start(bf16[32,4096]{1,0:T(8,128)(2,1)S(1)} %get-tuple-element.67), channel_id=1, source_target_pairs={{0,4},{4,0},{8,12},{12,8},{1,5},{5,1},{9,13},{13,9},{2,6},{6,2},{1... | collective-permute-start | bytes 786440 | tf_op jit(solution)/shard_map/ppermute | solution.py:64
  71.0 11.6 %collective-permute-start.14 = (bf16[32,4096]{1,0:T(8,128)(2,1)S(1)}, bf16[32,4096]{1,0:T(8,128)(2,1)S(1)}, u32[]{:S(2)}, u32[]{:S(2)}) collective-permute-start(bf16[32,4096]{1,0:T(8,128)(2,1)S(1)} %get-tuple-element.68), channel_id=1, source_target_pairs={{0,8},{4,12},{8,0},{12,4},{1,9},{5,13},{9,1},{13,5},{2,10},{6,14},... | collective-permute-start | bytes 786440 | tf_op jit(solution)/shard_map/ppermute | solution.py:64
  72.2 10.5 %collective-permute-start.15 = (bf16[32,4096]{1,0:T(8,128)(2,1)S(1)}, bf16[32,4096]{1,0:T(8,128)(2,1)S(1)}, u32[]{:S(2)}, u32[]{:S(2)}) collective-permute-start(bf16[32,4096]{1,0:T(8,128)(2,1)S(1)} %get-tuple-element.69), channel_id=1, source_target_pairs={{0,12},{4,8},{8,4},{12,0},{1,13},{5,9},{9,5},{13,1},{2,14},{6,10},... | collective-permute-start | bytes 786440 | tf_op jit(solution)/shard_map/ppermute | solution.py:64
  83.3 8.3 %collective-permute-start.16 = (bf16[32,1024]{1,0:T(8,128)(2,1)S(1)}, bf16[32,1024]{1,0:T(8,128)(2,1)S(1)}, u32[]{:S(2)}, u32[]{:S(2)}) collective-permute-start(bf16[32,1024]{1,0:T(8,128)(2,1)S(1)} %get-tuple-element.71), channel_id=1, source_target_pairs={{0,1},{1,0},{2,3},{3,2},{4,5},{5,4},{6,7},{7,6},{8,9},{9,8},{10,11... | collective-permute-start | bytes 196616 | tf_op jit(solution)/shard_map/ppermute | solution.py:64
  83.4 9.5 %collective-permute-start.17 = (bf16[32,1024]{1,0:T(8,128)(2,1)S(1)}, bf16[32,1024]{1,0:T(8,128)(2,1)S(1)}, u32[]{:S(2)}, u32[]{:S(2)}) collective-permute-start(bf16[32,1024]{1,0:T(8,128)(2,1)S(1)} %get-tuple-element.72), channel_id=1, source_target_pairs={{0,2},{1,3},{2,0},{3,1},{4,6},{5,7},{6,4},{7,5},{8,10},{9,11},{10,... | collective-permute-start | bytes 196616 | tf_op jit(solution)/shard_map/ppermute | solution.py:64
  90.8 10.0 %collective-permute-start.52 = (bf16[32,4096]{1,0:T(8,128)(2,1)S(1)}, bf16[32,4096]{1,0:T(8,128)(2,1)S(1)}, u32[]{:S(2)}, u32[]{:S(2)}) collective-permute-start(bf16[32,4096]{1,0:T(8,128)(2,1)S(1)} %get-tuple-element.95), channel_id=1, source_target_pairs={{0,8},{4,12},{8,0},{12,4},{1,9},{5,13},{9,1},{13,5},{2,10},{6,14},... | collective-permute-start | bytes 786440 | tf_op jit(solution)/shard_map/ppermute | solution.py:64
  91.6 9.2 %collective-permute-start.53 = (bf16[32,4096]{1,0:T(8,128)(2,1)S(1)}, bf16[32,4096]{1,0:T(8,128)(2,1)S(1)}, u32[]{:S(2)}, u32[]{:S(2)}) collective-permute-start(bf16[32,4096]{1,0:T(8,128)(2,1)S(1)} %get-tuple-element.96), channel_id=1, source_target_pairs={{0,12},{4,8},{8,4},{12,0},{1,13},{5,9},{9,5},{13,1},{2,14},{6,10},... | collective-permute-start | bytes 786440 | tf_op jit(solution)/shard_map/ppermute | solution.py:64
  92.9 11.7 %collective-permute-start.21 = (bf16[32,1024]{1,0:T(8,128)(2,1)S(1)}, bf16[32,1024]{1,0:T(8,128)(2,1)S(1)}, u32[]{:S(2)}, u32[]{:S(2)}) collective-permute-start(bf16[32,1024]{1,0:T(8,128)(2,1)S(1)} %add_convert_fusion.3), channel_id=1, source_target_pairs={{0,3},{1,2},{2,1},{3,0},{4,7},{5,6},{6,5},{7,4},{8,11},{9,10},{10,... | collective-permute-start | bytes 196616 | tf_op jit(solution)/shard_map/ppermute | solution.py:64
  95.0 11.0 %collective-permute-start.20 = (bf16[32,1024]{1,0:T(8,128)(2,1)S(1)}, bf16[32,1024]{1,0:T(8,128)(2,1)S(1)}, u32[]{:S(2)}, u32[]{:S(2)}) collective-permute-start(bf16[32,1024]{1,0:T(8,128)(2,1)S(1)} %add_convert_fusion.3), channel_id=1, source_target_pairs={{0,2},{1,3},{2,0},{3,1},{4,6},{5,7},{6,4},{7,5},{8,10},{9,11},{10,... | collective-permute-start | bytes 196616 | tf_op jit(solution)/shard_map/ppermute | solution.py:64
  96.6 9.4 %collective-permute-start.19 = (bf16[32,1024]{1,0:T(8,128)(2,1)S(1)}, bf16[32,1024]{1,0:T(8,128)(2,1)S(1)}, u32[]{:S(2)}, u32[]{:S(2)}) collective-permute-start(bf16[32,1024]{1,0:T(8,128)(2,1)S(1)} %add_convert_fusion.3), channel_id=1, source_target_pairs={{0,1},{1,0},{2,3},{3,2},{4,5},{5,4},{6,7},{7,6},{8,9},{9,8},{10,11... | collective-permute-start | bytes 196616 | tf_op jit(solution)/shard_map/ppermute | solution.py:64
  106.0 14.8 %collective-permute-start.24 = (bf16[4,32,1024]{2,1,0:T(8,128)(2,1)S(1)}, bf16[4,32,1024]{2,1,0:T(8,128)(2,1)S(1)}, u32[]{:S(2)}, u32[]{:S(2)}) collective-permute-start(bf16[4,32,1024]{2,1,0:T(8,128)(2,1)S(1)} %pad_maximum_fusion.1.refs_0_), channel_id=1, source_target_pairs={{0,12},{4,8},{8,4},{12,0},{1,13},{5,9},{9,5},{13,1},{2,14},{6,10},... | collective-permute-start | bytes 786440 | tf_op jit(solution)/shard_map/ppermute | solution.py:64
  115.1 10.8 %collective-permute-start.23 = (bf16[4,32,1024]{2,1,0:T(8,128)(2,1)S(1)}, bf16[4,32,1024]{2,1,0:T(8,128)(2,1)S(1)}, u32[]{:S(2)}, u32[]{:S(2)}) collective-permute-start(bf16[4,32,1024]{2,1,0:T(8,128)(2,1)S(1)} %pad_maximum_fusion.1.refs_0_), channel_id=1, source_target_pairs={{0,8},{4,12},{8,0},{12,4},{1,9},{5,13},{9,1},{13,5},{2,10},{6,14},... | collective-permute-start | bytes 786440 | tf_op jit(solution)/shard_map/ppermute | solution.py:64
  116.8 9.2 %collective-permute-start.22 = (bf16[4,32,1024]{2,1,0:T(8,128)(2,1)S(1)}, bf16[4,32,1024]{2,1,0:T(8,128)(2,1)S(1)}, u32[]{:S(2)}, u32[]{:S(2)}) collective-permute-start(bf16[4,32,1024]{2,1,0:T(8,128)(2,1)S(1)} %pad_maximum_fusion.1.refs_0_), channel_id=1, source_target_pairs={{0,4},{4,0},{8,12},{12,8},{1,5},{5,1},{9,13},{13,9},{2,6},{6,2},{1... | collective-permute-start | bytes 786440 | tf_op jit(solution)/shard_map/ppermute | solution.py:64
  118.2 11.5 %collective-permute-start.62 = (bf16[4,32,1024]{2,1,0:T(8,128)(2,1)S(1)}, bf16[4,32,1024]{2,1,0:T(8,128)(2,1)S(1)}, u32[]{:S(2)}, u32[]{:S(2)}) collective-permute-start(bf16[4,32,1024]{2,1,0:T(8,128)(2,1)S(1)} %pad_maximum_fusion.2.refs_0_), channel_id=1, source_target_pairs={{0,12},{4,8},{8,4},{12,0},{1,13},{5,9},{9,5},{13,1},{2,14},{6,10},... | collective-permute-start | bytes 786440 | tf_op jit(solution)/shard_map/ppermute | solution.py:64
  120.4 11.1 %collective-permute-start.61 = (bf16[4,32,1024]{2,1,0:T(8,128)(2,1)S(1)}, bf16[4,32,1024]{2,1,0:T(8,128)(2,1)S(1)}, u32[]{:S(2)}, u32[]{:S(2)}) collective-permute-start(bf16[4,32,1024]{2,1,0:T(8,128)(2,1)S(1)} %pad_maximum_fusion.2.refs_0_), channel_id=1, source_target_pairs={{0,8},{4,12},{8,0},{12,4},{1,9},{5,13},{9,1},{13,5},{2,10},{6,14},... | collective-permute-start | bytes 786440 | tf_op jit(solution)/shard_map/ppermute | solution.py:64
  120.8 11.8 %collective-permute-start.60 = (bf16[4,32,1024]{2,1,0:T(8,128)(2,1)S(1)}, bf16[4,32,1024]{2,1,0:T(8,128)(2,1)S(1)}, u32[]{:S(2)}, u32[]{:S(2)}) collective-permute-start(bf16[4,32,1024]{2,1,0:T(8,128)(2,1)S(1)} %pad_maximum_fusion.2.refs_0_), channel_id=1, source_target_pairs={{0,4},{4,0},{8,12},{12,8},{1,5},{5,1},{9,13},{13,9},{2,6},{6,2},{1... | collective-permute-start | bytes 786440 | tf_op jit(solution)/shard_map/ppermute | solution.py:64
  135.5 8.5 %collective-permute-start.27 = (bf16[128,128]{1,0:T(8,128)(2,1)S(1)}, bf16[128,128]{1,0:T(8,128)(2,1)S(1)}, u32[]{:S(2)}, u32[]{:S(2)}) collective-permute-start(bf16[128,128]{1,0:T(8,128)(2,1)S(1)} %get-tuple-element.74.refs_0_), channel_id=1, source_target_pairs={{0,2},{1,3},{2,0},{3,1},{4,6},{5,7},{6,4},{7,5},{8,10},{9,11},{10,... | collective-permute-start | bytes 98312 | tf_op jit(solution)/shard_map/ppermute | solution.py:64
  135.5 8.5 %collective-permute-start.26 = (bf16[128,128]{1,0:T(8,128)(2,1)S(1)}, bf16[128,128]{1,0:T(8,128)(2,1)S(1)}, u32[]{:S(2)}, u32[]{:S(2)}) collective-permute-start(bf16[128,128]{1,0:T(8,128)(2,1)S(1)} %get-tuple-element.74.refs_0_), channel_id=1, source_target_pairs={{0,1},{1,0},{2,3},{3,2},{4,5},{5,4},{6,7},{7,6},{8,9},{9,8},{10,11... | collective-permute-start | bytes 98312 | tf_op jit(solution)/shard_map/ppermute | solution.py:64
  139.5 7.6 %collective-permute-start.66 = (bf16[128,128]{1,0:T(8,128)(2,1)S(1)}, bf16[128,128]{1,0:T(8,128)(2,1)S(1)}, u32[]{:S(2)}, u32[]{:S(2)}) collective-permute-start(bf16[128,128]{1,0:T(8,128)(2,1)S(1)} %get-tuple-element.101.refs_0_), channel_id=1, source_target_pairs={{0,3},{1,2},{2,1},{3,0},{4,7},{5,6},{6,5},{7,4},{8,11},{9,10},{10,... | collective-permute-start | bytes 98312 | tf_op jit(solution)/shard_map/ppermute | solution.py:64
  140.5 8.4 %collective-permute-start.65 = (bf16[128,128]{1,0:T(8,128)(2,1)S(1)}, bf16[128,128]{1,0:T(8,128)(2,1)S(1)}, u32[]{:S(2)}, u32[]{:S(2)}) collective-permute-start(bf16[128,128]{1,0:T(8,128)(2,1)S(1)} %get-tuple-element.101.refs_0_), channel_id=1, source_target_pairs={{0,2},{1,3},{2,0},{3,1},{4,6},{5,7},{6,4},{7,5},{8,10},{9,11},{10,... | collective-permute-start | bytes 98312 | tf_op jit(solution)/shard_map/ppermute | solution.py:64
  141.1 7.9 %collective-permute-start.64 = (bf16[128,128]{1,0:T(8,128)(2,1)S(1)}, bf16[128,128]{1,0:T(8,128)(2,1)S(1)}, u32[]{:S(2)}, u32[]{:S(2)}) collective-permute-start(bf16[128,128]{1,0:T(8,128)(2,1)S(1)} %get-tuple-element.101.refs_0_), channel_id=1, source_target_pairs={{0,1},{1,0},{2,3},{3,2},{4,5},{5,4},{6,7},{7,6},{8,9},{9,8},{10,11... | collective-permute-start | bytes 98312 | tf_op jit(solution)/shard_map/ppermute | solution.py:64
  145.7 8.1 %collective-permute-start.30 = (bf16[32,2048]{1,0:T(8,128)(2,1)S(1)}, bf16[32,2048]{1,0:T(8,128)(2,1)S(1)}, u32[]{:S(2)}, u32[]{:S(2)}) collective-permute-start(bf16[32,2048]{1,0:T(8,128)(2,1)S(1)} %get-tuple-element.77), channel_id=1, source_target_pairs={{0,8},{4,12},{8,0},{12,4},{1,9},{5,13},{9,1},{13,5},{2,10},{6,14},... | collective-permute-start | bytes 393224 | tf_op jit(solution)/shard_map/ppermute | solution.py:64
  150.6 12.0 %collective-permute-start.68 = (bf16[32,2048]{1,0:T(8,128)(2,1)S(1)}, bf16[32,2048]{1,0:T(8,128)(2,1)S(1)}, u32[]{:S(2)}, u32[]{:S(2)}) collective-permute-start(bf16[32,2048]{1,0:T(8,128)(2,1)S(1)} %get-tuple-element.104), channel_id=1, source_target_pairs={{0,8},{4,12},{8,0},{12,4},{1,9},{5,13},{9,1},{13,5},{2,10},{6,14},... | collective-permute-start | bytes 393224 | tf_op jit(solution)/shard_map/ppermute | solution.py:64
  152.0 10.6 %collective-permute-start.69 = (bf16[32,2048]{1,0:T(8,128)(2,1)S(1)}, bf16[32,2048]{1,0:T(8,128)(2,1)S(1)}, u32[]{:S(2)}, u32[]{:S(2)}) collective-permute-start(bf16[32,2048]{1,0:T(8,128)(2,1)S(1)} %get-tuple-element.105), channel_id=1, source_target_pairs={{0,12},{4,8},{8,4},{12,0},{1,13},{5,9},{9,5},{13,1},{2,14},{6,10},... | collective-permute-start | bytes 393224 | tf_op jit(solution)/shard_map/ppermute | solution.py:64
  154.5 11.5 %collective-permute-start.34 = (bf16[32,2048]{1,0:T(8,128)(2,1)S(1)}, bf16[32,2048]{1,0:T(8,128)(2,1)S(1)}, u32[]{:S(2)}, u32[]{:S(2)}) collective-permute-start(bf16[32,2048]{1,0:T(8,128)(2,1)S(1)} %subtract_convert_fusion.1.refs_0_), channel_id=1, source_target_pairs={{0,12},{4,8},{8,4},{12,0},{1,13},{5,9},{9,5},{13,1},{2,14},{6,10},... | collective-permute-start | bytes 393224 | tf_op jit(solution)/shard_map/ppermute | solution.py:64
  156.4 10.6 %collective-permute-start.33 = (bf16[32,2048]{1,0:T(8,128)(2,1)S(1)}, bf16[32,2048]{1,0:T(8,128)(2,1)S(1)}, u32[]{:S(2)}, u32[]{:S(2)}) collective-permute-start(bf16[32,2048]{1,0:T(8,128)(2,1)S(1)} %subtract_convert_fusion.1.refs_0_), channel_id=1, source_target_pairs={{0,8},{4,12},{8,0},{12,4},{1,9},{5,13},{9,1},{13,5},{2,10},{6,14},... | collective-permute-start | bytes 393224 | tf_op jit(solution)/shard_map/ppermute | solution.py:64
  157.4 9.6 %collective-permute-start.32 = (bf16[32,2048]{1,0:T(8,128)(2,1)S(1)}, bf16[32,2048]{1,0:T(8,128)(2,1)S(1)}, u32[]{:S(2)}, u32[]{:S(2)}) collective-permute-start(bf16[32,2048]{1,0:T(8,128)(2,1)S(1)} %subtract_convert_fusion.1.refs_0_), channel_id=1, source_target_pairs={{0,4},{4,0},{8,12},{12,8},{1,5},{5,1},{9,13},{13,9},{2,6},{6,2},{1... | collective-permute-start | bytes 393224 | tf_op jit(solution)/shard_map/ppermute | solution.py:64
  164.0 9.9 %collective-permute-start.71 = (bf16[32,2048]{1,0:T(8,128)(2,1)S(1)}, bf16[32,2048]{1,0:T(8,128)(2,1)S(1)}, u32[]{:S(2)}, u32[]{:S(2)}) collective-permute-start(bf16[32,2048]{1,0:T(8,128)(2,1)S(1)} %subtract_convert_fusion.refs_0_), channel_id=1, source_target_pairs={{0,8},{4,12},{8,0},{12,4},{1,9},{5,13},{9,1},{13,5},{2,10},{6,14},... | collective-permute-start | bytes 393224 | tf_op jit(solution)/shard_map/ppermute | solution.py:64
  166.0 7.8 %collective-permute-start.70 = (bf16[32,2048]{1,0:T(8,128)(2,1)S(1)}, bf16[32,2048]{1,0:T(8,128)(2,1)S(1)}, u32[]{:S(2)}, u32[]{:S(2)}) collective-permute-start(bf16[32,2048]{1,0:T(8,128)(2,1)S(1)} %subtract_convert_fusion.refs_0_), channel_id=1, source_target_pairs={{0,4},{4,0},{8,12},{12,8},{1,5},{5,1},{9,13},{13,9},{2,6},{6,2},{1... | collective-permute-start | bytes 393224 | tf_op jit(solution)/shard_map/ppermute | solution.py:64
  168.3 11.8 %collective-permute-start.35 = (bf16[32,2048]{1,0:T(8,128)(2,1)S(1)}, bf16[32,2048]{1,0:T(8,128)(2,1)S(1)}, u32[]{:S(2)}, u32[]{:S(2)}) collective-permute-start(bf16[32,2048]{1,0:T(8,128)(2,1)S(1)} %get-tuple-element.80), channel_id=1, source_target_pairs={{0,1},{1,0},{2,3},{3,2},{4,5},{5,4},{6,7},{7,6},{8,9},{9,8},{10,11... | collective-permute-start | bytes 393224 | tf_op jit(solution)/shard_map/ppermute | solution.py:64
  168.4 14.7 %collective-permute-start.36 = (bf16[32,2048]{1,0:T(8,128)(2,1)S(1)}, bf16[32,2048]{1,0:T(8,128)(2,1)S(1)}, u32[]{:S(2)}, u32[]{:S(2)}) collective-permute-start(bf16[32,2048]{1,0:T(8,128)(2,1)S(1)} %get-tuple-element.81), channel_id=1, source_target_pairs={{0,2},{1,3},{2,0},{3,1},{4,6},{5,7},{6,4},{7,5},{8,10},{9,11},{10,... | collective-permute-start | bytes 393224 | tf_op jit(solution)/shard_map/ppermute | solution.py:64
  169.9 13.2 %collective-permute-start.37 = (bf16[32,2048]{1,0:T(8,128)(2,1)S(1)}, bf16[32,2048]{1,0:T(8,128)(2,1)S(1)}, u32[]{:S(2)}, u32[]{:S(2)}) collective-permute-start(bf16[32,2048]{1,0:T(8,128)(2,1)S(1)} %get-tuple-element.82), channel_id=1, source_target_pairs={{0,3},{1,2},{2,1},{3,0},{4,7},{5,6},{6,5},{7,4},{8,11},{9,10},{10,... | collective-permute-start | bytes 393224 | tf_op jit(solution)/shard_map/ppermute | solution.py:64
  178.7 11.8 %collective-permute-start.74 = (bf16[32,2048]{1,0:T(8,128)(2,1)S(1)}, bf16[32,2048]{1,0:T(8,128)(2,1)S(1)}, u32[]{:S(2)}, u32[]{:S(2)}) collective-permute-start(bf16[32,2048]{1,0:T(8,128)(2,1)S(1)} %get-tuple-element.108), channel_id=1, source_target_pairs={{0,2},{1,3},{2,0},{3,1},{4,6},{5,7},{6,4},{7,5},{8,10},{9,11},{10,... | collective-permute-start | bytes 393224 | tf_op jit(solution)/shard_map/ppermute | solution.py:64
  180.2 10.3 %collective-permute-start.75 = (bf16[32,2048]{1,0:T(8,128)(2,1)S(1)}, bf16[32,2048]{1,0:T(8,128)(2,1)S(1)}, u32[]{:S(2)}, u32[]{:S(2)}) collective-permute-start(bf16[32,2048]{1,0:T(8,128)(2,1)S(1)} %get-tuple-element.109), channel_id=1, source_target_pairs={{0,3},{1,2},{2,1},{3,0},{4,7},{5,6},{6,5},{7,4},{8,11},{9,10},{10,... | collective-permute-start | bytes 393224 | tf_op jit(solution)/shard_map/ppermute | solution.py:64
  (38 other events, 276.6 us)

commit v2 on v1

--- a/solution.py
+++ b/solution.py
@@ -12,6 +12,7 @@
 TILE = 256
 COVER = 40
 SETTLE = 10**10
+TOUCH = False, False, False, False
 F32 = jnp.float32
 BF16 = jnp.bfloat16
 
@@ -57,11 +58,38 @@
     )(index)
 
 
+def touch(index, panel, done):
+    def kernel(index, panel, done, out):
+        for k in range(index.shape[0]):
+            out[k] = index[k]
+
+    spaces = pltpu.SMEM, pltpu.VMEM, pl.ANY
+    return pl.pallas_call(
+        kernel,
+        out_shape=jax.ShapeDtypeStruct(index.shape, index.dtype),
+        in_specs=[pl.BlockSpec(memory_space=space) for space in spaces],
+        out_specs=pl.BlockSpec(memory_space=pltpu.SMEM),
+        compiler_params=pltpu.CompilerParams(vmem_limit_bytes=KERNEL_BYTES),
+        name="touch",
+    )(index, panel, done)
+
+
 def exchange(pieces, axis):
     size = lax.axis_size(axis)
     out = [pieces[0]]
     for o in range(1, size):
         out.append(lax.ppermute(pieces[o], axis, [(i, i ^ o) for i in range(size)]))
+    return out
+
+
+def relay(near, far, axis):
+    size = lax.axis_size(axis)
+    if size != 4:
+        return exchange([near] + [far] * (size - 1), axis)
+    out = [near, None, None, None]
+    for o, piece in ((3, far), (1, near), (2, None)):
+        piece = out[3] if o == 2 else piece
+        out[o] = lax.ppermute(piece, axis, [(i, i ^ {1: 1, 2: 1, 3: 3}[o]) for i in range(size)])
     return out
 
 
@@ -286,28 +314,41 @@
     def stream(h):
         source = leaf_t[h * chunk : (h + 1) * chunk]
         if h:
-            source = after(source, *arrived[-1][1:])
-        pieces = spread(source, "col")
-        arrived.append(pieces)
-        parts = forward_leaf(0, index)(pieces)
+            source = after(source, seen["A"][1], seen["A"][3])
+        pieces = relay(source, source, "col")
+        if TOUCH[h]:
+            own = touch(index, leaf_inverse, seen["L"] if h else pieces[1])
+        else:
+            own = index
+        seen["A"] = pieces
+        parts = forward_leaf(0, own)(pieces)
+        seen["L"] = parts[0]
         front = add_all(exchange(parts, "row")).astype(BF16)
         parts = forward_coupling(spread(front, "row"))
         coupled = add_all(exchange(parts, "col")).astype(BF16)
         sketch = sep_t[:, h].reshape(cols, sep_width)
         rhs = sep_rhs(sketch, spread(coupled, "leaf"))
         parts = exchange(forward_sep(index, 0, sep_rows, rhs[0]), "row")
+        if h:
+            parts = [after(parts[0], seen["mid"])] + parts[1:]
         parts = exchange(reduce_first(sep_rows, 1, parts), "col")
+        if h:
+            parts = [after(parts[0], seen["stack"])] + parts[1:]
         mid = add_all(parts).astype(BF16)
-        pieces = spread(jnp.stack(spread(mid, "col")), "row")
+        stack = jnp.stack(spread(mid, "col"))
+        seen["mid"], seen["stack"] = mid, stack
+        pieces = spread(stack, "row")
         total = backward_sep(0, sep_rows, 0, pieces, None)
         out_sep, pulled = pull(spread(total, "leaf"))
         parts = backward_coupling(0, spread(pulled, "col"))
         back = add_all(exchange(parts, "row"))
         leaf_rhs = (front.astype(F32) - back).astype(BF16)
-        parts = backward_leaf(index, 0, spread(leaf_rhs, "row"))
+        pieces = spread(leaf_rhs, "row")
+        own = touch(index, leaf_inverse, leaf_rhs) if TOUCH[2 + h] else index
+        parts = backward_leaf(own, 0, pieces)
         return add_all(exchange(parts, "col")), out_sep
 
-    arrived = []
+    seen = {}
     results = [stream(h) for h in range(STREAMS)]
     out_leaf = jnp.concatenate([leaf for leaf, _ in results], axis=0)
     out_sep = jnp.stack([sep.reshape(n, chunk, sep_width) for _, sep in results], axis=1)

time: 192 us -> 187 us (0.974)
  waiting for transfers between devices: 52.6 us -> 43.3 us
  starting transfers between devices: 96.3 us -> 101 us
    ppermute x0 -> x6, starting transfers between devices: none -> 11.5 us  [relay(): lax.ppermute(piece, axis, [(i, i ^ {1: 1, 2: 1, 3: 3}[o]) for i in range(...]
    ppermute x76 -> x70, waiting for transfers between devices: 52.6 us -> 42.1 us  [exchange(): out.append(lax.ppermute(pieces[o], axis, [(i, i ^ o) for i in range(size)]))]
    ppermute x76 -> x70, starting transfers between devices: 96.3 us -> 89.8 us  [exchange(): out.append(lax.ppermute(pieces[o], axis, [(i, i ^ o) for i in range(size)]))]
  transfers between devices with their start and end apart: 76 -> 76, of which waited for: 26 -> 28; matrix products, arithmetic and copies ran while one was open for 2% -> 2% of each run, Pallas kernels for 10% -> 12%
where the time goes in v2:
time: 187 us
  starting transfers between devices  101 us (54%)
  waiting for transfers between devices  43.3 us (23%)
  Pallas kernels  23.6 us (13%)
  local copies, waits for them, and re-layouts  14.3 us (8%)
  between operations  2.25 us (1%)
  other arithmetic  2.14 us (1%)
    ppermute x70, starting transfers between devices, exchange(): out.append(lax.ppermute(pieces[o], axis, [(i, i ^ o) for i in range(size)]))  89.8 us
    ppermute x70, waiting for transfers between devices, exchange(): out.append(lax.ppermute(pieces[o], axis, [(i, i ^ o) for i in range(size)]))  42.1 us
    pallas_call x18, Pallas kernels, call(): pl.pallas_call(kernel, out_shape=outs, in_specs=[pl.BlockSpec(memory_spac...  22.4 us
    unnamed x22, local copies, waits for them, and re-layouts  12 us
    ppermute x6, starting transfers between devices, relay(): lax.ppermute(piece, axis, [(i, i ^ {1: 1, 2: 1, 3: 3}[o]) for i in range(...  11.5 us
  transfers between devices with their start and end apart: 76, of which 28 were waited for; matrix products, arithmetic and copies ran while one was open for 2% of the time, Pallas kernels for 12%

profile of v2, /device:TPU:0, one launch (start us, length us, event | category | flops | bytes accessed | tf_op | source)
XLA Modules:
  0.0 187.1 jit_solution(2559473169920095141)
XLA Ops:
  1.6 5.1 %collective-permute-start.1 = (bf16[32,2048]{1,0:T(8,128)(2,1)S(1)}, bf16[32,2048]{1,0:T(8,128)(2,1)S(1)}, u32[]{:S(2)}, u32[]{:S(2)}) collective-permute-start(bf16[32,2048]{1,0:T(8,128)(2,1)S(1)} %get-tuple-element.120.refs_0_), channel_id=1, source_target_pairs={{0,3},{1,2},{2,1},{3,0},{4,7},{5,6},{6,5},{7,4},{8,11},{9,10},{10,... | collective-permute-start | bytes 393224 | tf_op jit(solution)/shard_map/ppermute | solution.py:92
  11.2 1.6 collective-permute-start.2
  14.0 2.3 %collective-permute-start.39 = (bf16[32,2048]{1,0:T(8,128)(2,1)S(1)}, bf16[32,2048]{1,0:T(8,128)(2,1)S(1)}, u32[]{:S(2)}, u32[]{:S(2)}) collective-permute-start(bf16[32,2048]{1,0:T(8,128)(2,1)S(1)} %get-tuple-element.85.refs_0_), channel_id=1, source_target_pairs={{0,3},{1,2},{2,1},{3,0},{4,7},{5,6},{6,5},{7,4},{8,11},{9,10},{10,... | collective-permute-start | bytes 393224 | tf_op jit(solution)/shard_map/ppermute | solution.py:92
  16.3 3.4 %copy-done = bf16[2048,2048]{1,0:T(8,128)(2,1)S(1)} copy-done((bf16[2048,2048]{1,0:T(8,128)(2,1)S(1)}, bf16[2048,2048]{1,0:T(8,128)(2,1)}, u32[]{:S(2)}) %copy-start) | copy-done | bytes 8388632
  20.3 2.2 %shard_map.77 = (bf16[32,2048]{1,0:T(8,128)(2,1)S(1)}, bf16[32,2048]{1,0:T(8,128)(2,1)S(1)}, bf16[32,2048]{1,0:T(8,128)(2,1)S(1)}, bf16[32,2048]{1,0:T(8,128)(2,1)S(1)}) custom-call(s32[4]{0:T(128)S(1)} %copy-done.4, bf16[2048,2048]{1,0:T(8,128)(2,1)S(1)} %copy-done, bf16[32,2048]{1,0:T(8,128)(2,1)S(1)} %get-tuple-element.120.refs_0_, ...), custom_call_target="tpu_custom_call" | custom-call | flops 1073741824 | bytes 8912896 | tf_op jit(solution)/shard_map/pallas_call | solution.py:30
  22.5 1.6 collective-permute-start.3
  24.1 1.5 collective-permute-start.4
  26.1 2.5 %collective-permute-start.38 = (bf16[32,2048]{1,0:T(8,128)(2,1)S(1)}, bf16[32,2048]{1,0:T(8,128)(2,1)S(1)}, u32[]{:S(2)}, u32[]{:S(2)}) collective-permute-start(bf16[32,2048]{1,0:T(8,128)(2,1)S(1)} %get-tuple-element.85.refs_0_), channel_id=1, source_target_pairs={{0,1},{1,0},{2,3},{3,2},{4,5},{5,4},{6,7},{7,6},{8,9},{9,8},{10,11... | collective-permute-start | bytes 393224 | tf_op jit(solution)/shard_map/ppermute | solution.py:92
  29.7 1.8 collective-permute-done.5
  32.7 2.5 %collective-permute-start.8 = (bf16[32,2048]{1,0:T(8,128)(2,1)S(1)}, bf16[32,2048]{1,0:T(8,128)(2,1)S(1)}, u32[]{:S(2)}, u32[]{:S(2)}) collective-permute-start(bf16[32,2048]{1,0:T(8,128)(2,1)S(1)} %add_convert_fusion.1.refs_0_), channel_id=1, source_target_pairs={{0,12},{4,8},{8,4},{12,0},{1,13},{5,9},{9,5},{13,1},{2,14},{6,10},... | collective-permute-start | bytes 393224 | tf_op jit(solution)/shard_map/ppermute | solution.py:81
  35.3 3.4 %copy-done.1 = bf16[2048,2048]{1,0:T(8,128)(2,1)S(1)} copy-done((bf16[2048,2048]{1,0:T(8,128)(2,1)S(1)}, bf16[2048,2048]{1,0:T(8,128)(2,1)}, u32[]{:S(2)}) %copy-start.1) | copy-done | bytes 8388632
  38.7 2.2 %shard_map.86 = (bf16[32,2048]{1,0:T(8,128)(2,1)S(1)}, bf16[32,2048]{1,0:T(8,128)(2,1)S(1)}, bf16[32,2048]{1,0:T(8,128)(2,1)S(1)}, bf16[32,2048]{1,0:T(8,128)(2,1)S(1)}) custom-call(s32[4]{0:T(128)S(1)} %copy-done.5, bf16[2048,2048]{1,0:T(8,128)(2,1)S(1)} %copy-done.1, bf16[32,2048]{1,0:T(8,128)(2,1)S(1)} %get-tuple-element.85.refs_0_, ...), custom_call_target="tpu_custom_call" | custom-call | flops 1073741824 | bytes 8912896 | tf_op jit(solution)/shard_map/pallas_call | solution.py:30
  42.2 2.3 %collective-permute-start.43 = (bf16[32,2048]{1,0:T(8,128)(2,1)S(1)}, bf16[32,2048]{1,0:T(8,128)(2,1)S(1)}, u32[]{:S(2)}, u32[]{:S(2)}) collective-permute-start(bf16[32,2048]{1,0:T(8,128)(2,1)S(1)} %get-tuple-element.89), channel_id=1, source_target_pairs={{0,12},{4,8},{8,4},{12,0},{1,13},{5,9},{9,5},{13,1},{2,14},{6,10},... | collective-permute-start | bytes 393224 | tf_op jit(solution)/shard_map/ppermute | solution.py:81
  45.6 4.7 %collective-permute-start.10 = (bf16[128,128]{1,0:T(8,128)(2,1)S(1)}, bf16[128,128]{1,0:T(8,128)(2,1)S(1)}, u32[]{:S(2)}, u32[]{:S(2)}) collective-permute-start(bf16[128,128]{1,0:T(8,128)(2,1)S(1)} %get-tuple-element.65), channel_id=1, source_target_pairs={{0,2},{1,3},{2,0},{3,1},{4,6},{5,7},{6,4},{7,5},{8,10},{9,11},{10,... | collective-permute-start | bytes 98312 | tf_op jit(solution)/shard_map/ppermute | solution.py:81
  50.2 1.8 collective-permute-start.11
  52.6 1.4 collective-permute-start.44
  54.5 1.7 collective-permute-start.46
  61.5 1.8 collective-permute-start.47
  63.3 3.1 %collective-permute-start.48 = (bf16[128,128]{1,0:T(8,128)(2,1)S(1)}, bf16[128,128]{1,0:T(8,128)(2,1)S(1)}, u32[]{:S(2)}, u32[]{:S(2)}) collective-permute-start(bf16[128,128]{1,0:T(8,128)(2,1)S(1)} %get-tuple-element.92), channel_id=1, source_target_pairs={{0,2},{1,3},{2,0},{3,1},{4,6},{5,7},{6,4},{7,5},{8,10},{9,11},{10,... | collective-permute-start | bytes 98312 | tf_op jit(solution)/shard_map/ppermute | solution.py:81
  66.4 1.5 shard_map.80
  68.0 1.5 collective-permute-start.13
  69.9 1.6 collective-permute-start.15
  74.7 1.9 %collective-permute-done.13.refs_1_ = bf16[32,4096]{1,0:T(8,128)(2,1)S(1)} collective-permute-done((bf16[32,4096]{1,0:T(8,128)(2,1)S(1)}, bf16[32,4096]{1,0:T(8,128)(2,1)S(1)}, u32[]{:S(2)}, u32[]{:S(2)}) %collective-permute-start.13) | collective-permute-done | bytes 262176 | tf_op jit(solution)/shard_map/ppermute | solution.py:81
  76.6 4.0 %collective-permute-done.14.refs_2_ = bf16[32,4096]{1,0:T(8,128)(2,1)S(1)} collective-permute-done((bf16[32,4096]{1,0:T(8,128)(2,1)S(1)}, bf16[32,4096]{1,0:T(8,128)(2,1)S(1)}, u32[]{:S(2)}, u32[]{:S(2)}) %collective-permute-start.14) | collective-permute-done | bytes 262176 | tf_op jit(solution)/shard_map/ppermute | solution.py:81
  81.9 2.8 %collective-permute-start.17 = (bf16[32,1024]{1,0:T(8,128)(2,1)S(1)}, bf16[32,1024]{1,0:T(8,128)(2,1)S(1)}, u32[]{:S(2)}, u32[]{:S(2)}) collective-permute-start(bf16[32,1024]{1,0:T(8,128)(2,1)S(1)} %get-tuple-element.74), channel_id=1, source_target_pairs={{0,2},{1,3},{2,0},{3,1},{4,6},{5,7},{6,4},{7,5},{8,10},{9,11},{10,... | collective-permute-start | bytes 196616 | tf_op jit(solution)/shard_map/ppermute | solution.py:81
  85.8 1.5 shard_map.89
  89.2 1.6 collective-permute-start.53
  91.6 2.7 %collective-permute-start.20 = (bf16[32,1024]{1,0:T(8,128)(2,1)S(1)}, bf16[32,1024]{1,0:T(8,128)(2,1)S(1)}, u32[]{:S(2)}, u32[]{:S(2)}) collective-permute-start(bf16[32,1024]{1,0:T(8,128)(2,1)S(1)} %add_convert_fusion.3), channel_id=1, source_target_pairs={{0,2},{1,3},{2,0},{3,1},{4,6},{5,7},{6,4},{7,5},{8,10},{9,11},{10,... | collective-permute-start | bytes 196616 | tf_op jit(solution)/shard_map/ppermute | solution.py:81
  94.3 2.2 %collective-permute-start.21 = (bf16[32,1024]{1,0:T(8,128)(2,1)S(1)}, bf16[32,1024]{1,0:T(8,128)(2,1)S(1)}, u32[]{:S(2)}, u32[]{:S(2)}) collective-permute-start(bf16[32,1024]{1,0:T(8,128)(2,1)S(1)} %add_convert_fusion.3), channel_id=1, source_target_pairs={{0,3},{1,2},{2,1},{3,0},{4,7},{5,6},{6,5},{7,4},{8,11},{9,10},{10,... | collective-permute-start | bytes 196616 | tf_op jit(solution)/shard_map/ppermute | solution.py:81
  98.4 3.8 %collective-permute-start.55 = (bf16[32,1024]{1,0:T(8,128)(2,1)S(1)}, bf16[32,1024]{1,0:T(8,128)(2,1)S(1)}, u32[]{:S(2)}, u32[]{:S(2)}) collective-permute-start(bf16[32,1024]{1,0:T(8,128)(2,1)S(1)} %get-tuple-element.103), channel_id=1, source_target_pairs={{0,2},{1,3},{2,0},{3,1},{4,6},{5,7},{6,4},{7,5},{8,10},{9,11},{10,... | collective-permute-start | bytes 196616 | tf_op jit(solution)/shard_map/ppermute | solution.py:81
  105.2 3.9 %collective-permute-done.56 = bf16[32,1024]{1,0:T(8,128)(2,1)S(1)} collective-permute-done((bf16[32,1024]{1,0:T(8,128)(2,1)S(1)}, bf16[32,1024]{1,0:T(8,128)(2,1)S(1)}, u32[]{:S(2)}, u32[]{:S(2)}) %collective-permute-start.56) | collective-permute-done | bytes 65568 | tf_op jit(solution)/shard_map/ppermute | solution.py:81
  109.2 2.0 %collective-permute-start.58 = (bf16[32,1024]{1,0:T(8,128)(2,1)S(1)}, bf16[32,1024]{1,0:T(8,128)(2,1)S(1)}, u32[]{:S(2)}, u32[]{:S(2)}) collective-permute-start(bf16[32,1024]{1,0:T(8,128)(2,1)S(1)} %add_convert_fusion.2), channel_id=1, source_target_pairs={{0,2},{1,3},{2,0},{3,1},{4,6},{5,7},{6,4},{7,5},{8,10},{9,11},{10,... | collective-permute-start | bytes 196616 | tf_op jit(solution)/shard_map/ppermute | solution.py:81
  111.2 2.4 %collective-permute-start.59 = (bf16[32,1024]{1,0:T(8,128)(2,1)S(1)}, bf16[32,1024]{1,0:T(8,128)(2,1)S(1)}, u32[]{:S(2)}, u32[]{:S(2)}) collective-permute-start(bf16[32,1024]{1,0:T(8,128)(2,1)S(1)} %add_convert_fusion.2), channel_id=1, source_target_pairs={{0,3},{1,2},{2,1},{3,0},{4,7},{5,6},{6,5},{7,4},{8,11},{9,10},{10,... | collective-permute-start | bytes 196616 | tf_op jit(solution)/shard_map/ppermute | solution.py:81
  114.8 2.4 %collective-permute-done.59 = bf16[32,1024]{1,0:T(8,128)(2,1)S(1)} collective-permute-done((bf16[32,1024]{1,0:T(8,128)(2,1)S(1)}, bf16[32,1024]{1,0:T(8,128)(2,1)S(1)}, u32[]{:S(2)}, u32[]{:S(2)}) %collective-permute-start.59) | collective-permute-done | bytes 65568 | tf_op jit(solution)/shard_map/ppermute | solution.py:81
  118.7 2.1 %collective-permute-start.62 = (bf16[4,32,1024]{2,1,0:T(8,128)(2,1)S(1)}, bf16[4,32,1024]{2,1,0:T(8,128)(2,1)S(1)}, u32[]{:S(2)}, u32[]{:S(2)}) collective-permute-start(bf16[4,32,1024]{2,1,0:T(8,128)(2,1)S(1)} %pad_maximum_fusion.2.refs_0_), channel_id=1, source_target_pairs={{0,12},{4,8},{8,4},{12,0},{1,13},{5,9},{9,5},{13,1},{2,14},{6,10},... | collective-permute-start | bytes 786440 | tf_op jit(solution)/shard_map/ppermute | solution.py:81
  120.8 6.1 %collective-permute-done.23.refs_2_ = bf16[4,32,1024]{2,1,0:T(8,128)(2,1)S(1)} collective-permute-done((bf16[4,32,1024]{2,1,0:T(8,128)(2,1)S(1)}, bf16[4,32,1024]{2,1,0:T(8,128)(2,1)S(1)}, u32[]{:S(2)}, u32[]{:S(2)}) %collective-permute-start.23) | collective-permute-done | bytes 262176 | tf_op jit(solution)/shard_map/ppermute | solution.py:81
  128.2 1.5 collective-permute-done.61.refs_2_
  132.3 2.2 %collective-permute-start.27 = (bf16[128,128]{1,0:T(8,128)(2,1)S(1)}, bf16[128,128]{1,0:T(8,128)(2,1)S(1)}, u32[]{:S(2)}, u32[]{:S(2)}) collective-permute-start(bf16[128,128]{1,0:T(8,128)(2,1)S(1)} %get-tuple-element.76.refs_0_), channel_id=1, source_target_pairs={{0,2},{1,3},{2,0},{3,1},{4,6},{5,7},{6,4},{7,5},{8,10},{9,11},{10,... | collective-permute-start | bytes 98312 | tf_op jit(solution)/shard_map/ppermute | solution.py:81
  134.6 1.5 collective-permute-start.28
  136.7 2.9 %collective-permute-start.65 = (bf16[128,128]{1,0:T(8,128)(2,1)S(1)}, bf16[128,128]{1,0:T(8,128)(2,1)S(1)}, u32[]{:S(2)}, u32[]{:S(2)}) collective-permute-start(bf16[128,128]{1,0:T(8,128)(2,1)S(1)} %get-tuple-element.105.refs_0_), channel_id=1, source_target_pairs={{0,2},{1,3},{2,0},{3,1},{4,6},{5,7},{6,4},{7,5},{8,10},{9,11},{10,... | collective-permute-start | bytes 98312 | tf_op jit(solution)/shard_map/ppermute | solution.py:81
  139.6 1.5 collective-permute-start.66
  155.8 1.7 collective-permute-done.68
  161.4 1.7 collective-permute-done.33.refs_2_
  164.7 3.3 %collective-permute-start.36 = (bf16[32,2048]{1,0:T(8,128)(2,1)S(1)}, bf16[32,2048]{1,0:T(8,128)(2,1)S(1)}, u32[]{:S(2)}, u32[]{:S(2)}) collective-permute-start(bf16[32,2048]{1,0:T(8,128)(2,1)S(1)} %get-tuple-element.83), channel_id=1, source_target_pairs={{0,2},{1,3},{2,0},{3,1},{4,6},{5,7},{6,4},{7,5},{8,10},{9,11},{10,... | collective-permute-start | bytes 393224 | tf_op jit(solution)/shard_map/ppermute | solution.py:81
  170.2 3.4 %copy-done.2 = bf16[2048,2048]{1,0:T(8,128)(2,1)S(1)} copy-done((bf16[2048,2048]{1,0:T(8,128)(2,1)S(1)}, bf16[2048,2048]{1,0:T(8,128)(2,1)}, u32[]{:S(2)}) %copy-start.2) | copy-done | bytes 8388632
  175.0 3.3 %collective-permute-start.74 = (bf16[32,2048]{1,0:T(8,128)(2,1)S(1)}, bf16[32,2048]{1,0:T(8,128)(2,1)S(1)}, u32[]{:S(2)}, u32[]{:S(2)}) collective-permute-start(bf16[32,2048]{1,0:T(8,128)(2,1)S(1)} %get-tuple-element.112), channel_id=1, source_target_pairs={{0,2},{1,3},{2,0},{3,1},{4,6},{5,7},{6,4},{7,5},{8,10},{9,11},{10,... | collective-permute-start | bytes 393224 | tf_op jit(solution)/shard_map/ppermute | solution.py:81
  179.5 2.1 %collective-permute-done.73 = bf16[32,2048]{1,0:T(8,128)(2,1)S(1)} collective-permute-done((bf16[32,2048]{1,0:T(8,128)(2,1)S(1)}, bf16[32,2048]{1,0:T(8,128)(2,1)S(1)}, u32[]{:S(2)}, u32[]{:S(2)}) %collective-permute-start.73) | collective-permute-done | bytes 131104 | tf_op jit(solution)/shard_map/ppermute | solution.py:81
  181.6 4.6 %collective-permute-done.74 = bf16[32,2048]{1,0:T(8,128)(2,1)S(1)} collective-permute-done((bf16[32,2048]{1,0:T(8,128)(2,1)S(1)}, bf16[32,2048]{1,0:T(8,128)(2,1)S(1)}, u32[]{:S(2)}, u32[]{:S(2)}) %collective-permute-start.74) | collective-permute-done | bytes 131104 | tf_op jit(solution)/shard_map/ppermute | solution.py:81
  (164 shorter events, 64.3 us)
Async XLA Ops:
  1.6 9.5 %collective-permute-start.1 = (bf16[32,2048]{1,0:T(8,128)(2,1)S(1)}, bf16[32,2048]{1,0:T(8,128)(2,1)S(1)}, u32[]{:S(2)}, u32[]{:S(2)}) collective-permute-start(bf16[32,2048]{1,0:T(8,128)(2,1)S(1)} %get-tuple-element.120.refs_0_), channel_id=1, source_target_pairs={{0,3},{1,2},{2,1},{3,0},{4,7},{5,6},{6,5},{7,4},{8,11},{9,10},{10,... | collective-permute-start | bytes 393224 | tf_op jit(solution)/shard_map/ppermute | solution.py:92
  14.0 14.6 %collective-permute-start.39 = (bf16[32,2048]{1,0:T(8,128)(2,1)S(1)}, bf16[32,2048]{1,0:T(8,128)(2,1)S(1)}, u32[]{:S(2)}, u32[]{:S(2)}) collective-permute-start(bf16[32,2048]{1,0:T(8,128)(2,1)S(1)} %get-tuple-element.85.refs_0_), channel_id=1, source_target_pairs={{0,3},{1,2},{2,1},{3,0},{4,7},{5,6},{6,5},{7,4},{8,11},{9,10},{10,... | collective-permute-start | bytes 393224 | tf_op jit(solution)/shard_map/ppermute | solution.py:92
  26.1 9.2 %collective-permute-start.38 = (bf16[32,2048]{1,0:T(8,128)(2,1)S(1)}, bf16[32,2048]{1,0:T(8,128)(2,1)S(1)}, u32[]{:S(2)}, u32[]{:S(2)}) collective-permute-start(bf16[32,2048]{1,0:T(8,128)(2,1)S(1)} %get-tuple-element.85.refs_0_), channel_id=1, source_target_pairs={{0,1},{1,0},{2,3},{3,2},{4,5},{5,4},{6,7},{7,6},{8,9},{9,8},{10,11... | collective-permute-start | bytes 393224 | tf_op jit(solution)/shard_map/ppermute | solution.py:92
  31.6 10.6 %collective-permute-start.6 = (bf16[32,2048]{1,0:T(8,128)(2,1)S(1)}, bf16[32,2048]{1,0:T(8,128)(2,1)S(1)}, u32[]{:S(2)}, u32[]{:S(2)}) collective-permute-start(bf16[32,2048]{1,0:T(8,128)(2,1)S(1)} %add_convert_fusion.1.refs_0_), channel_id=1, source_target_pairs={{0,4},{4,0},{8,12},{12,8},{1,5},{5,1},{9,13},{13,9},{2,6},{6,2},{1... | collective-permute-start | bytes 393224 | tf_op jit(solution)/shard_map/ppermute | solution.py:81
  32.4 12.1 %collective-permute-start.7 = (bf16[32,2048]{1,0:T(8,128)(2,1)S(1)}, bf16[32,2048]{1,0:T(8,128)(2,1)S(1)}, u32[]{:S(2)}, u32[]{:S(2)}) collective-permute-start(bf16[32,2048]{1,0:T(8,128)(2,1)S(1)} %add_convert_fusion.1.refs_0_), channel_id=1, source_target_pairs={{0,8},{4,12},{8,0},{12,4},{1,9},{5,13},{9,1},{13,5},{2,10},{6,14},... | collective-permute-start | bytes 393224 | tf_op jit(solution)/shard_map/ppermute | solution.py:81
  32.7 11.8 %collective-permute-start.8 = (bf16[32,2048]{1,0:T(8,128)(2,1)S(1)}, bf16[32,2048]{1,0:T(8,128)(2,1)S(1)}, u32[]{:S(2)}, u32[]{:S(2)}) collective-permute-start(bf16[32,2048]{1,0:T(8,128)(2,1)S(1)} %add_convert_fusion.1.refs_0_), channel_id=1, source_target_pairs={{0,12},{4,8},{8,4},{12,0},{1,13},{5,9},{9,5},{13,1},{2,14},{6,10},... | collective-permute-start | bytes 393224 | tf_op jit(solution)/shard_map/ppermute | solution.py:81
  40.9 11.1 %collective-permute-start.41 = (bf16[32,2048]{1,0:T(8,128)(2,1)S(1)}, bf16[32,2048]{1,0:T(8,128)(2,1)S(1)}, u32[]{:S(2)}, u32[]{:S(2)}) collective-permute-start(bf16[32,2048]{1,0:T(8,128)(2,1)S(1)} %get-tuple-element.87), channel_id=1, source_target_pairs={{0,4},{4,0},{8,12},{12,8},{1,5},{5,1},{9,13},{13,9},{2,6},{6,2},{1... | collective-permute-start | bytes 393224 | tf_op jit(solution)/shard_map/ppermute | solution.py:81
  41.8 10.8 %collective-permute-start.42 = (bf16[32,2048]{1,0:T(8,128)(2,1)S(1)}, bf16[32,2048]{1,0:T(8,128)(2,1)S(1)}, u32[]{:S(2)}, u32[]{:S(2)}) collective-permute-start(bf16[32,2048]{1,0:T(8,128)(2,1)S(1)} %get-tuple-element.88), channel_id=1, source_target_pairs={{0,8},{4,12},{8,0},{12,4},{1,9},{5,13},{9,1},{13,5},{2,10},{6,14},... | collective-permute-start | bytes 393224 | tf_op jit(solution)/shard_map/ppermute | solution.py:81
  42.2 10.3 %collective-permute-start.43 = (bf16[32,2048]{1,0:T(8,128)(2,1)S(1)}, bf16[32,2048]{1,0:T(8,128)(2,1)S(1)}, u32[]{:S(2)}, u32[]{:S(2)}) collective-permute-start(bf16[32,2048]{1,0:T(8,128)(2,1)S(1)} %get-tuple-element.89), channel_id=1, source_target_pairs={{0,12},{4,8},{8,4},{12,0},{1,13},{5,9},{9,5},{13,1},{2,14},{6,10},... | collective-permute-start | bytes 393224 | tf_op jit(solution)/shard_map/ppermute | solution.py:81
  45.6 8.9 %collective-permute-start.10 = (bf16[128,128]{1,0:T(8,128)(2,1)S(1)}, bf16[128,128]{1,0:T(8,128)(2,1)S(1)}, u32[]{:S(2)}, u32[]{:S(2)}) collective-permute-start(bf16[128,128]{1,0:T(8,128)(2,1)S(1)} %get-tuple-element.65), channel_id=1, source_target_pairs={{0,2},{1,3},{2,0},{3,1},{4,6},{5,7},{6,4},{7,5},{8,10},{9,11},{10,... | collective-permute-start | bytes 98312 | tf_op jit(solution)/shard_map/ppermute | solution.py:81
  61.5 8.4 %collective-permute-start.47 = (bf16[128,128]{1,0:T(8,128)(2,1)S(1)}, bf16[128,128]{1,0:T(8,128)(2,1)S(1)}, u32[]{:S(2)}, u32[]{:S(2)}) collective-permute-start(bf16[128,128]{1,0:T(8,128)(2,1)S(1)} %get-tuple-element.91), channel_id=1, source_target_pairs={{0,1},{1,0},{2,3},{3,2},{4,5},{5,4},{6,7},{7,6},{8,9},{9,8},{10,11... | collective-permute-start | bytes 98312 | tf_op jit(solution)/shard_map/ppermute | solution.py:81
  63.3 8.2 %collective-permute-start.48 = (bf16[128,128]{1,0:T(8,128)(2,1)S(1)}, bf16[128,128]{1,0:T(8,128)(2,1)S(1)}, u32[]{:S(2)}, u32[]{:S(2)}) collective-permute-start(bf16[128,128]{1,0:T(8,128)(2,1)S(1)} %get-tuple-element.92), channel_id=1, source_target_pairs={{0,2},{1,3},{2,0},{3,1},{4,6},{5,7},{6,4},{7,5},{8,10},{9,11},{10,... | collective-permute-start | bytes 98312 | tf_op jit(solution)/shard_map/ppermute | solution.py:81
  68.0 8.7 %collective-permute-start.13 = (bf16[32,4096]{1,0:T(8,128)(2,1)S(1)}, bf16[32,4096]{1,0:T(8,128)(2,1)S(1)}, u32[]{:S(2)}, u32[]{:S(2)}) collective-permute-start(bf16[32,4096]{1,0:T(8,128)(2,1)S(1)} %get-tuple-element.69), channel_id=1, source_target_pairs={{0,4},{4,0},{8,12},{12,8},{1,5},{5,1},{9,13},{13,9},{2,6},{6,2},{1... | collective-permute-start | bytes 786440 | tf_op jit(solution)/shard_map/ppermute | solution.py:81
  69.4 11.2 %collective-permute-start.14 = (bf16[32,4096]{1,0:T(8,128)(2,1)S(1)}, bf16[32,4096]{1,0:T(8,128)(2,1)S(1)}, u32[]{:S(2)}, u32[]{:S(2)}) collective-permute-start(bf16[32,4096]{1,0:T(8,128)(2,1)S(1)} %get-tuple-element.70), channel_id=1, source_target_pairs={{0,8},{4,12},{8,0},{12,4},{1,9},{5,13},{9,1},{13,5},{2,10},{6,14},... | collective-permute-start | bytes 786440 | tf_op jit(solution)/shard_map/ppermute | solution.py:81
  69.9 10.7 %collective-permute-start.15 = (bf16[32,4096]{1,0:T(8,128)(2,1)S(1)}, bf16[32,4096]{1,0:T(8,128)(2,1)S(1)}, u32[]{:S(2)}, u32[]{:S(2)}) collective-permute-start(bf16[32,4096]{1,0:T(8,128)(2,1)S(1)} %get-tuple-element.71), channel_id=1, source_target_pairs={{0,12},{4,8},{8,4},{12,0},{1,13},{5,9},{9,5},{13,1},{2,14},{6,10},... | collective-permute-start | bytes 786440 | tf_op jit(solution)/shard_map/ppermute | solution.py:81
  81.3 7.9 %collective-permute-start.16 = (bf16[32,1024]{1,0:T(8,128)(2,1)S(1)}, bf16[32,1024]{1,0:T(8,128)(2,1)S(1)}, u32[]{:S(2)}, u32[]{:S(2)}) collective-permute-start(bf16[32,1024]{1,0:T(8,128)(2,1)S(1)} %get-tuple-element.73), channel_id=1, source_target_pairs={{0,1},{1,0},{2,3},{3,2},{4,5},{5,4},{6,7},{7,6},{8,9},{9,8},{10,11... | collective-permute-start | bytes 196616 | tf_op jit(solution)/shard_map/ppermute | solution.py:81
  81.9 8.9 %collective-permute-start.17 = (bf16[32,1024]{1,0:T(8,128)(2,1)S(1)}, bf16[32,1024]{1,0:T(8,128)(2,1)S(1)}, u32[]{:S(2)}, u32[]{:S(2)}) collective-permute-start(bf16[32,1024]{1,0:T(8,128)(2,1)S(1)} %get-tuple-element.74), channel_id=1, source_target_pairs={{0,2},{1,3},{2,0},{3,1},{4,6},{5,7},{6,4},{7,5},{8,10},{9,11},{10,... | collective-permute-start | bytes 196616 | tf_op jit(solution)/shard_map/ppermute | solution.py:81
  88.2 9.2 %collective-permute-start.52 = (bf16[32,4096]{1,0:T(8,128)(2,1)S(1)}, bf16[32,4096]{1,0:T(8,128)(2,1)S(1)}, u32[]{:S(2)}, u32[]{:S(2)}) collective-permute-start(bf16[32,4096]{1,0:T(8,128)(2,1)S(1)} %get-tuple-element.98), channel_id=1, source_target_pairs={{0,8},{4,12},{8,0},{12,4},{1,9},{5,13},{9,1},{13,5},{2,10},{6,14},... | collective-permute-start | bytes 786440 | tf_op jit(solution)/shard_map/ppermute | solution.py:81
  89.2 8.1 %collective-permute-start.53 = (bf16[32,4096]{1,0:T(8,128)(2,1)S(1)}, bf16[32,4096]{1,0:T(8,128)(2,1)S(1)}, u32[]{:S(2)}, u32[]{:S(2)}) collective-permute-start(bf16[32,4096]{1,0:T(8,128)(2,1)S(1)} %get-tuple-element.99), channel_id=1, source_target_pairs={{0,12},{4,8},{8,4},{12,0},{1,13},{5,9},{9,5},{13,1},{2,14},{6,10},... | collective-permute-start | bytes 786440 | tf_op jit(solution)/shard_map/ppermute | solution.py:81
  91.5 10.8 %collective-permute-start.19 = (bf16[32,1024]{1,0:T(8,128)(2,1)S(1)}, bf16[32,1024]{1,0:T(8,128)(2,1)S(1)}, u32[]{:S(2)}, u32[]{:S(2)}) collective-permute-start(bf16[32,1024]{1,0:T(8,128)(2,1)S(1)} %add_convert_fusion.3), channel_id=1, source_target_pairs={{0,1},{1,0},{2,3},{3,2},{4,5},{5,4},{6,7},{7,6},{8,9},{9,8},{10,11... | collective-permute-start | bytes 196616 | tf_op jit(solution)/shard_map/ppermute | solution.py:81
  91.6 10.9 %collective-permute-start.20 = (bf16[32,1024]{1,0:T(8,128)(2,1)S(1)}, bf16[32,1024]{1,0:T(8,128)(2,1)S(1)}, u32[]{:S(2)}, u32[]{:S(2)}) collective-permute-start(bf16[32,1024]{1,0:T(8,128)(2,1)S(1)} %add_convert_fusion.3), channel_id=1, source_target_pairs={{0,2},{1,3},{2,0},{3,1},{4,6},{5,7},{6,4},{7,5},{8,10},{9,11},{10,... | collective-permute-start | bytes 196616 | tf_op jit(solution)/shard_map/ppermute | solution.py:81
  94.3 8.2 %collective-permute-start.21 = (bf16[32,1024]{1,0:T(8,128)(2,1)S(1)}, bf16[32,1024]{1,0:T(8,128)(2,1)S(1)}, u32[]{:S(2)}, u32[]{:S(2)}) collective-permute-start(bf16[32,1024]{1,0:T(8,128)(2,1)S(1)} %add_convert_fusion.3), channel_id=1, source_target_pairs={{0,3},{1,2},{2,1},{3,0},{4,7},{5,6},{6,5},{7,4},{8,11},{9,10},{10,... | collective-permute-start | bytes 196616 | tf_op jit(solution)/shard_map/ppermute | solution.py:81
  102.5 16.2 %collective-permute-start.22 = (bf16[4,32,1024]{2,1,0:T(8,128)(2,1)S(1)}, bf16[4,32,1024]{2,1,0:T(8,128)(2,1)S(1)}, u32[]{:S(2)}, u32[]{:S(2)}) collective-permute-start(bf16[4,32,1024]{2,1,0:T(8,128)(2,1)S(1)} %pad_maximum_fusion.1.refs_0_), channel_id=1, source_target_pairs={{0,4},{4,0},{8,12},{12,8},{1,5},{5,1},{9,13},{13,9},{2,6},{6,2},{1... | collective-permute-start | bytes 786440 | tf_op jit(solution)/shard_map/ppermute | solution.py:81
  113.6 13.3 %collective-permute-start.23 = (bf16[4,32,1024]{2,1,0:T(8,128)(2,1)S(1)}, bf16[4,32,1024]{2,1,0:T(8,128)(2,1)S(1)}, u32[]{:S(2)}, u32[]{:S(2)}) collective-permute-start(bf16[4,32,1024]{2,1,0:T(8,128)(2,1)S(1)} %pad_maximum_fusion.1.refs_0_), channel_id=1, source_target_pairs={{0,8},{4,12},{8,0},{12,4},{1,9},{5,13},{9,1},{13,5},{2,10},{6,14},... | collective-permute-start | bytes 786440 | tf_op jit(solution)/shard_map/ppermute | solution.py:81
  113.6 13.3 %collective-permute-start.24 = (bf16[4,32,1024]{2,1,0:T(8,128)(2,1)S(1)}, bf16[4,32,1024]{2,1,0:T(8,128)(2,1)S(1)}, u32[]{:S(2)}, u32[]{:S(2)}) collective-permute-start(bf16[4,32,1024]{2,1,0:T(8,128)(2,1)S(1)} %pad_maximum_fusion.1.refs_0_), channel_id=1, source_target_pairs={{0,12},{4,8},{8,4},{12,0},{1,13},{5,9},{9,5},{13,1},{2,14},{6,10},... | collective-permute-start | bytes 786440 | tf_op jit(solution)/shard_map/ppermute | solution.py:81
  117.3 10.9 %collective-permute-start.60 = (bf16[4,32,1024]{2,1,0:T(8,128)(2,1)S(1)}, bf16[4,32,1024]{2,1,0:T(8,128)(2,1)S(1)}, u32[]{:S(2)}, u32[]{:S(2)}) collective-permute-start(bf16[4,32,1024]{2,1,0:T(8,128)(2,1)S(1)} %pad_maximum_fusion.2.refs_0_), channel_id=1, source_target_pairs={{0,4},{4,0},{8,12},{12,8},{1,5},{5,1},{9,13},{13,9},{2,6},{6,2},{1... | collective-permute-start | bytes 786440 | tf_op jit(solution)/shard_map/ppermute | solution.py:81
  117.6 12.1 %collective-permute-start.61 = (bf16[4,32,1024]{2,1,0:T(8,128)(2,1)S(1)}, bf16[4,32,1024]{2,1,0:T(8,128)(2,1)S(1)}, u32[]{:S(2)}, u32[]{:S(2)}) collective-permute-start(bf16[4,32,1024]{2,1,0:T(8,128)(2,1)S(1)} %pad_maximum_fusion.2.refs_0_), channel_id=1, source_target_pairs={{0,8},{4,12},{8,0},{12,4},{1,9},{5,13},{9,1},{13,5},{2,10},{6,14},... | collective-permute-start | bytes 786440 | tf_op jit(solution)/shard_map/ppermute | solution.py:81
  118.7 11.0 %collective-permute-start.62 = (bf16[4,32,1024]{2,1,0:T(8,128)(2,1)S(1)}, bf16[4,32,1024]{2,1,0:T(8,128)(2,1)S(1)}, u32[]{:S(2)}, u32[]{:S(2)}) collective-permute-start(bf16[4,32,1024]{2,1,0:T(8,128)(2,1)S(1)} %pad_maximum_fusion.2.refs_0_), channel_id=1, source_target_pairs={{0,12},{4,8},{8,4},{12,0},{1,13},{5,9},{9,5},{13,1},{2,14},{6,10},... | collective-permute-start | bytes 786440 | tf_op jit(solution)/shard_map/ppermute | solution.py:81
  131.6 8.0 %collective-permute-start.26 = (bf16[128,128]{1,0:T(8,128)(2,1)S(1)}, bf16[128,128]{1,0:T(8,128)(2,1)S(1)}, u32[]{:S(2)}, u32[]{:S(2)}) collective-permute-start(bf16[128,128]{1,0:T(8,128)(2,1)S(1)} %get-tuple-element.76.refs_0_), channel_id=1, source_target_pairs={{0,1},{1,0},{2,3},{3,2},{4,5},{5,4},{6,7},{7,6},{8,9},{9,8},{10,11... | collective-permute-start | bytes 98312 | tf_op jit(solution)/shard_map/ppermute | solution.py:81
  132.3 8.8 %collective-permute-start.27 = (bf16[128,128]{1,0:T(8,128)(2,1)S(1)}, bf16[128,128]{1,0:T(8,128)(2,1)S(1)}, u32[]{:S(2)}, u32[]{:S(2)}) collective-permute-start(bf16[128,128]{1,0:T(8,128)(2,1)S(1)} %get-tuple-element.76.refs_0_), channel_id=1, source_target_pairs={{0,2},{1,3},{2,0},{3,1},{4,6},{5,7},{6,4},{7,5},{8,10},{9,11},{10,... | collective-permute-start | bytes 98312 | tf_op jit(solution)/shard_map/ppermute | solution.py:81
  136.6 8.1 %collective-permute-start.64 = (bf16[128,128]{1,0:T(8,128)(2,1)S(1)}, bf16[128,128]{1,0:T(8,128)(2,1)S(1)}, u32[]{:S(2)}, u32[]{:S(2)}) collective-permute-start(bf16[128,128]{1,0:T(8,128)(2,1)S(1)} %get-tuple-element.105.refs_0_), channel_id=1, source_target_pairs={{0,1},{1,0},{2,3},{3,2},{4,5},{5,4},{6,7},{7,6},{8,9},{9,8},{10,11... | collective-permute-start | bytes 98312 | tf_op jit(solution)/shard_map/ppermute | solution.py:81
  136.7 9.3 %collective-permute-start.65 = (bf16[128,128]{1,0:T(8,128)(2,1)S(1)}, bf16[128,128]{1,0:T(8,128)(2,1)S(1)}, u32[]{:S(2)}, u32[]{:S(2)}) collective-permute-start(bf16[128,128]{1,0:T(8,128)(2,1)S(1)} %get-tuple-element.105.refs_0_), channel_id=1, source_target_pairs={{0,2},{1,3},{2,0},{3,1},{4,6},{5,7},{6,4},{7,5},{8,10},{9,11},{10,... | collective-permute-start | bytes 98312 | tf_op jit(solution)/shard_map/ppermute | solution.py:81
  142.5 7.2 %collective-permute-start.29 = (bf16[32,2048]{1,0:T(8,128)(2,1)S(1)}, bf16[32,2048]{1,0:T(8,128)(2,1)S(1)}, u32[]{:S(2)}, u32[]{:S(2)}) collective-permute-start(bf16[32,2048]{1,0:T(8,128)(2,1)S(1)} %get-tuple-element.78), channel_id=1, source_target_pairs={{0,4},{4,0},{8,12},{12,8},{1,5},{5,1},{9,13},{13,9},{2,6},{6,2},{1... | collective-permute-start | bytes 393224 | tf_op jit(solution)/shard_map/ppermute | solution.py:81
  143.4 7.6 %collective-permute-start.30 = (bf16[32,2048]{1,0:T(8,128)(2,1)S(1)}, bf16[32,2048]{1,0:T(8,128)(2,1)S(1)}, u32[]{:S(2)}, u32[]{:S(2)}) collective-permute-start(bf16[32,2048]{1,0:T(8,128)(2,1)S(1)} %get-tuple-element.79), channel_id=1, source_target_pairs={{0,8},{4,12},{8,0},{12,4},{1,9},{5,13},{9,1},{13,5},{2,10},{6,14},... | collective-permute-start | bytes 393224 | tf_op jit(solution)/shard_map/ppermute | solution.py:81
  144.8 7.3 %collective-permute-start.31 = (bf16[32,2048]{1,0:T(8,128)(2,1)S(1)}, bf16[32,2048]{1,0:T(8,128)(2,1)S(1)}, u32[]{:S(2)}, u32[]{:S(2)}) collective-permute-start(bf16[32,2048]{1,0:T(8,128)(2,1)S(1)} %get-tuple-element.80), channel_id=1, source_target_pairs={{0,12},{4,8},{8,4},{12,0},{1,13},{5,9},{9,5},{13,1},{2,14},{6,10},... | collective-permute-start | bytes 393224 | tf_op jit(solution)/shard_map/ppermute | solution.py:81
  148.4 9.2 %collective-permute-start.68 = (bf16[32,2048]{1,0:T(8,128)(2,1)S(1)}, bf16[32,2048]{1,0:T(8,128)(2,1)S(1)}, u32[]{:S(2)}, u32[]{:S(2)}) collective-permute-start(bf16[32,2048]{1,0:T(8,128)(2,1)S(1)} %get-tuple-element.108), channel_id=1, source_target_pairs={{0,8},{4,12},{8,0},{12,4},{1,9},{5,13},{9,1},{13,5},{2,10},{6,14},... | collective-permute-start | bytes 393224 | tf_op jit(solution)/shard_map/ppermute | solution.py:81
  149.7 8.0 %collective-permute-start.69 = (bf16[32,2048]{1,0:T(8,128)(2,1)S(1)}, bf16[32,2048]{1,0:T(8,128)(2,1)S(1)}, u32[]{:S(2)}, u32[]{:S(2)}) collective-permute-start(bf16[32,2048]{1,0:T(8,128)(2,1)S(1)} %get-tuple-element.109), channel_id=1, source_target_pairs={{0,12},{4,8},{8,4},{12,0},{1,13},{5,9},{9,5},{13,1},{2,14},{6,10},... | collective-permute-start | bytes 393224 | tf_op jit(solution)/shard_map/ppermute | solution.py:81
  152.1 8.0 %collective-permute-start.32 = (bf16[32,2048]{1,0:T(8,128)(2,1)S(1)}, bf16[32,2048]{1,0:T(8,128)(2,1)S(1)}, u32[]{:S(2)}, u32[]{:S(2)}) collective-permute-start(bf16[32,2048]{1,0:T(8,128)(2,1)S(1)} %subtract_convert_fusion.1.refs_0_), channel_id=1, source_target_pairs={{0,4},{4,0},{8,12},{12,8},{1,5},{5,1},{9,13},{13,9},{2,6},{6,2},{1... | collective-permute-start | bytes 393224 | tf_op jit(solution)/shard_map/ppermute | solution.py:81
  153.3 9.9 %collective-permute-start.33 = (bf16[32,2048]{1,0:T(8,128)(2,1)S(1)}, bf16[32,2048]{1,0:T(8,128)(2,1)S(1)}, u32[]{:S(2)}, u32[]{:S(2)}) collective-permute-start(bf16[32,2048]{1,0:T(8,128)(2,1)S(1)} %subtract_convert_fusion.1.refs_0_), channel_id=1, source_target_pairs={{0,8},{4,12},{8,0},{12,4},{1,9},{5,13},{9,1},{13,5},{2,10},{6,14},... | collective-permute-start | bytes 393224 | tf_op jit(solution)/shard_map/ppermute | solution.py:81
  154.5 8.8 %collective-permute-start.34 = (bf16[32,2048]{1,0:T(8,128)(2,1)S(1)}, bf16[32,2048]{1,0:T(8,128)(2,1)S(1)}, u32[]{:S(2)}, u32[]{:S(2)}) collective-permute-start(bf16[32,2048]{1,0:T(8,128)(2,1)S(1)} %subtract_convert_fusion.1.refs_0_), channel_id=1, source_target_pairs={{0,12},{4,8},{8,4},{12,0},{1,13},{5,9},{9,5},{13,1},{2,14},{6,10},... | collective-permute-start | bytes 393224 | tf_op jit(solution)/shard_map/ppermute | solution.py:81
  157.8 10.3 %collective-permute-start.70 = (bf16[32,2048]{1,0:T(8,128)(2,1)S(1)}, bf16[32,2048]{1,0:T(8,128)(2,1)S(1)}, u32[]{:S(2)}, u32[]{:S(2)}) collective-permute-start(bf16[32,2048]{1,0:T(8,128)(2,1)S(1)} %subtract_convert_fusion.refs_0_), channel_id=1, source_target_pairs={{0,4},{4,0},{8,12},{12,8},{1,5},{5,1},{9,13},{13,9},{2,6},{6,2},{1... | collective-permute-start | bytes 393224 | tf_op jit(solution)/shard_map/ppermute | solution.py:81
  158.9 11.3 %collective-permute-start.71 = (bf16[32,2048]{1,0:T(8,128)(2,1)S(1)}, bf16[32,2048]{1,0:T(8,128)(2,1)S(1)}, u32[]{:S(2)}, u32[]{:S(2)}) collective-permute-start(bf16[32,2048]{1,0:T(8,128)(2,1)S(1)} %subtract_convert_fusion.refs_0_), channel_id=1, source_target_pairs={{0,8},{4,12},{8,0},{12,4},{1,9},{5,13},{9,1},{13,5},{2,10},{6,14},... | collective-permute-start | bytes 393224 | tf_op jit(solution)/shard_map/ppermute | solution.py:81
  160.1 10.0 %collective-permute-start.72 = (bf16[32,2048]{1,0:T(8,128)(2,1)S(1)}, bf16[32,2048]{1,0:T(8,128)(2,1)S(1)}, u32[]{:S(2)}, u32[]{:S(2)}) collective-permute-start(bf16[32,2048]{1,0:T(8,128)(2,1)S(1)} %subtract_convert_fusion.refs_0_), channel_id=1, source_target_pairs={{0,12},{4,8},{8,4},{12,0},{1,13},{5,9},{9,5},{13,1},{2,14},{6,10},... | collective-permute-start | bytes 393224 | tf_op jit(solution)/shard_map/ppermute | solution.py:81
  164.6 13.7 %collective-permute-start.35 = (bf16[32,2048]{1,0:T(8,128)(2,1)S(1)}, bf16[32,2048]{1,0:T(8,128)(2,1)S(1)}, u32[]{:S(2)}, u32[]{:S(2)}) collective-permute-start(bf16[32,2048]{1,0:T(8,128)(2,1)S(1)} %get-tuple-element.82), channel_id=1, source_target_pairs={{0,1},{1,0},{2,3},{3,2},{4,5},{5,4},{6,7},{7,6},{8,9},{9,8},{10,11... | collective-permute-start | bytes 393224 | tf_op jit(solution)/shard_map/ppermute | solution.py:81
  164.7 14.7 %collective-permute-start.36 = (bf16[32,2048]{1,0:T(8,128)(2,1)S(1)}, bf16[32,2048]{1,0:T(8,128)(2,1)S(1)}, u32[]{:S(2)}, u32[]{:S(2)}) collective-permute-start(bf16[32,2048]{1,0:T(8,128)(2,1)S(1)} %get-tuple-element.83), channel_id=1, source_target_pairs={{0,2},{1,3},{2,0},{3,1},{4,6},{5,7},{6,4},{7,5},{8,10},{9,11},{10,... | collective-permute-start | bytes 393224 | tf_op jit(solution)/shard_map/ppermute | solution.py:81
  168.0 11.3 %collective-permute-start.37 = (bf16[32,2048]{1,0:T(8,128)(2,1)S(1)}, bf16[32,2048]{1,0:T(8,128)(2,1)S(1)}, u32[]{:S(2)}, u32[]{:S(2)}) collective-permute-start(bf16[32,2048]{1,0:T(8,128)(2,1)S(1)} %get-tuple-element.84), channel_id=1, source_target_pairs={{0,3},{1,2},{2,1},{3,0},{4,7},{5,6},{6,5},{7,4},{8,11},{9,10},{10,... | collective-permute-start | bytes 393224 | tf_op jit(solution)/shard_map/ppermute | solution.py:81
  175.0 11.1 %collective-permute-start.74 = (bf16[32,2048]{1,0:T(8,128)(2,1)S(1)}, bf16[32,2048]{1,0:T(8,128)(2,1)S(1)}, u32[]{:S(2)}, u32[]{:S(2)}) collective-permute-start(bf16[32,2048]{1,0:T(8,128)(2,1)S(1)} %get-tuple-element.112), channel_id=1, source_target_pairs={{0,2},{1,3},{2,0},{3,1},{4,6},{5,7},{6,4},{7,5},{8,10},{9,11},{10,... | collective-permute-start | bytes 393224 | tf_op jit(solution)/shard_map/ppermute | solution.py:81
  178.3 7.8 %collective-permute-start.75 = (bf16[32,2048]{1,0:T(8,128)(2,1)S(1)}, bf16[32,2048]{1,0:T(8,128)(2,1)S(1)}, u32[]{:S(2)}, u32[]{:S(2)}) collective-permute-start(bf16[32,2048]{1,0:T(8,128)(2,1)S(1)} %get-tuple-element.113), channel_id=1, source_target_pairs={{0,3},{1,2},{2,1},{3,0},{4,7},{5,6},{6,5},{7,4},{8,11},{9,10},{10,... | collective-permute-start | bytes 393224 | tf_op jit(solution)/shard_map/ppermute | solution.py:81
  (38 other events, 253.6 us)

commit v3 on v2

v3 whole, which is shorter than its diff:
```python
import jax
import jax.numpy as jnp
from jax import lax
from jax.experimental import pallas as pl
from jax.experimental.pallas import tpu as pltpu
from jax.sharding import PartitionSpec as P


PHASES = 1
SHARES = 1, 1
KERNEL_BYTES = 24 << 20
TILE = 256
COVER = 2
SETTLE = 10**10
TOUCH = False, False, False, False
F32 = jnp.float32
BF16 = jnp.bfloat16


def dot_nt(left, right):
    return lax.dot_general(left, right, (((1,), (1,)), ((), ())), preferred_element_type=F32)


def dot_nn(left, right):
    return lax.dot_general(left, right, (((1,), (0,)), ((), ())), preferred_element_type=F32)


def call(kernel, outs, index, operands, scratch, flops):
    moved = sum(a.size * a.dtype.itemsize for a in operands)
    return pl.pallas_call(
        kernel,
        out_shape=outs,
        in_specs=[pl.BlockSpec(memory_space=pltpu.SMEM)]
        + [pl.BlockSpec(memory_space=pltpu.VMEM)] * len(operands),
        out_specs=[pl.BlockSpec(memory_space=pltpu.VMEM)] * len(outs),
        scratch_shapes=scratch,
        cost_estimate=pl.CostEstimate(flops=flops, bytes_accessed=moved, transcendentals=0),
        compiler_params=pltpu.CompilerParams(vmem_limit_bytes=KERNEL_BYTES),
    )(index, *operands)


def after(value, *done):
    return lax.optimization_barrier((value, *done))[0]


def settle(index):
    def kernel(index, out):
        for k in range(index.shape[0]):
            out[k] = index[k]

    return pl.pallas_call(
        kernel,
        out_shape=jax.ShapeDtypeStruct(index.shape, index.dtype),
        in_specs=[pl.BlockSpec(memory_space=pltpu.SMEM)],
        out_specs=pl.BlockSpec(memory_space=pltpu.SMEM),
        cost_estimate=pl.CostEstimate(flops=SETTLE, bytes_accessed=64, transcendentals=0),
        name="settle",
    )(index)


def touch(index, panel, done):
    def kernel(index, panel, done, out):
        for k in range(index.shape[0]):
            out[k] = index[k]

    spaces = pltpu.SMEM, pltpu.VMEM, pl.ANY
    return pl.pallas_call(
        kernel,
        out_shape=jax.ShapeDtypeStruct(index.shape, index.dtype),
        in_specs=[pl.BlockSpec(memory_space=space) for space in spaces],
        out_specs=pl.BlockSpec(memory_space=pltpu.SMEM),
        compiler_params=pltpu.CompilerParams(vmem_limit_bytes=KERNEL_BYTES),
        name="touch",
    )(index, panel, done)


def exchange(pieces, axis):
    size = lax.axis_size(axis)
    out = [pieces[0]]
    for o in range(1, size):
        out.append(lax.ppermute(pieces[o], axis, [(i, i ^ o) for i in range(size)]))
    return out


def relay(near, far, axis):
    size = lax.axis_size(axis)
    if size != 4:
        return exchange([near] + [far] * (size - 1), axis)
    out = [near, None, None, None]
    for o, piece in ((3, far), (1, near), (2, None)):
        piece = out[3] if o == 2 else piece
        out[o] = lax.ppermute(piece, axis, [(i, i ^ {1: 1, 2: 1, 3: 3}[o]) for i in range(size)])
    return out


def spread(piece, axis):
    return exchange([piece] * lax.axis_size(axis), axis)


def add_all(pieces):
    total = pieces[0].astype(F32)
    for piece in pieces[1:]:
        total = total + piece.astype(F32)
    return total


def at(index, step):
    return pl.ds(pl.multiple_of(index * step, step), step)


def shape(*dims, dtype=BF16):
    return jax.ShapeDtypeStruct(dims, dtype)


def shards(sketch_leaf, sketch_sep, leaf_inverse, coupling, sep_inverse, front_map):
    n_leaf, n_row, n_col = (lax.axis_size(a) for a in ("leaf", "row", "col"))
    assert n_row == n_col and n_row & (n_row - 1) == 0 and n_leaf & (n_leaf - 1) == 0
    n = n_row
    section, r, c = (lax.axis_index(a) for a in ("leaf", "row", "col"))
    q = r * n_col + c
    rows, width = leaf_inverse.shape
    wide = sketch_leaf.shape[1]
    blk = coupling.shape[1] * n_row // front_map.shape[1]
    span = coupling.shape[1]
    sep_rows, sep_width = sep_inverse.shape
    group = sketch_sep.shape[0] // blk
    half = rows // PHASES
    assert rows == width

    slots = [
        jnp.clip(front_map[section ^ o, q] - q * group, 0, group - 1) for o in range(n_leaf)
    ]
    index = settle(jnp.stack([r, c] + slots).astype(jnp.int32))

    leaf_t = sketch_leaf.T
    sep_t = sketch_sep.T.reshape(n, wide, sep_width)

    def stream(h, chunk, offset):
        cols = chunk * n

        def needed(row_end, row_parts, col_parts, limit):
            last = (row_end // blk) * row_parts - 1
            return min(limit, (last // col_parts + 1) * blk)

        def first_row(col_start, row_parts, col_parts, limit):
            return min(limit, (col_start // blk) * col_parts // row_parts * blk)

        def forward_leaf(h, index):
            base = h * half
            depth = needed(base + half, n_col, n_row, width)
            assert depth <= (h + 1) * half

            def kernel(idx, inv, *refs):
                count = n * (h + 1)
                pieces, outs, lhs = refs[:count], refs[count : count + n], refs[count + n]
                for k in range(h + 1):
                    for o in range(n):
                        lhs[at(idx[0] ^ o, chunk), k * half : (k + 1) * half] = pieces[k * n + o][...]
                for start in range(0, half, TILE):
                    reach = needed(base + start + TILE, n_col, n_row, width)
                    acc = dot_nt(
                        lhs[:, :reach], inv[base + start : base + start + TILE, :reach]
                    ).astype(BF16)
                    for p in range(n):
                        outs[p][:, start : start + TILE] = acc[p * chunk : (p + 1) * chunk]

            return lambda pieces: call(
                kernel, [shape(chunk, half)] * n, index, [leaf_inverse] + pieces,
                [pltpu.VMEM((cols, (h + 1) * half), BF16)], 2 * cols * half * depth,
            )

        def forward_coupling(pieces):
            def kernel(idx, cpl, *refs):
                count = n * PHASES
                pieces, outs = refs[:count], refs[count : count + n]
                lhs, res = refs[count + n :]
                for k in range(PHASES):
                    for p in range(n):
                        place = at(idx[0] ^ idx[1] ^ p, chunk)
                        lhs[place, k * half : (k + 1) * half] = pieces[k * n + p][...]
                for s in range(0, span, TILE):
                    res[:, s : s + TILE] = dot_nn(lhs[...], cpl[:, s : s + TILE])
                for o in range(n):
                    outs[o][...] = res[:, at(idx[1] ^ o, blk)].astype(BF16)

            return call(
                kernel, [shape(cols, blk)] * n, index, [coupling] + pieces,
                [pltpu.VMEM((cols, rows), BF16), pltpu.VMEM((cols, span), F32)],
                COVER * cols * rows * span,
            )

        def sep_rhs(sketch, blocks):
            def kernel(idx, sketch, *refs):
                blocks, outs, rhs = refs[:n_leaf], refs[n_leaf:-1], refs[-1]
                rhs[...] = sketch[...].astype(F32)
                for o in range(n_leaf):
                    place = at(idx[2 + o], blk)
                    rhs[:, place] = rhs[:, place] - blocks[o][...].astype(F32)
                for k in range(n):
                    rounded = rhs[k * chunk : (k + 1) * chunk, :].astype(BF16)
                    outs[0][at(idx[0] ^ k, chunk), :] = rounded

            return call(
                kernel, [shape(cols, sep_width)], index, [sketch] + blocks,
                [pltpu.VMEM((cols, sep_width), F32)], cols * sep_width,
            )

        def forward_sep(index, base, size, rhs):
            def kernel(idx, inv, lhs, *outs):
                for start in range(0, size, TILE):
                    reach = needed(base + start + TILE, n_leaf, n_row * n_col, sep_width)
                    acc = dot_nt(
                        lhs[:, :reach], inv[base + start : base + start + TILE, :reach]
                    ).astype(BF16)
                    for p in range(n):
                        outs[p][:, start : start + TILE] = acc[p * chunk : (p + 1) * chunk]

            return call(
                kernel, [shape(chunk, size)] * n, index, [sep_inverse, rhs], [],
                2 * cols * size * sep_width,
            )

        def reduce_first(size, second, pieces):
            part = size // n

            def kernel(idx, *refs):
                pieces, outs = refs[:n], refs[n:]
                for o in range(n):
                    place = at(idx[second] ^ o, part)
                    outs[o][...] = add_all([piece[:, place] for piece in pieces]).astype(BF16)

            return call(kernel, [shape(chunk, part)] * n, index, pieces, [], n * chunk * size)

        def backward_sep(base, size, first_axis, pieces, before):
            part = size // n
            given = [] if before is None else [before]

            def kernel(idx, inv, *refs):
                pieces, before, (out, lhs) = refs[:n], refs[n:-2], refs[-2:]
                for p in range(n):
                    for o in range(n):
                        place = at(idx[first_axis] ^ p, chunk), at(idx[1 - first_axis] ^ o, part)
                        lhs[place] = pieces[p][o]
                for start in range(0, sep_width, TILE):
                    first = max(first_row(start, n_leaf, n_row * n_col, sep_rows) - base, 0)
                    stop = start + TILE
                    if first < size:
                        acc = dot_nn(lhs[:, first:], inv[base + first : base + size, start:stop])
                    else:
                        acc = jnp.zeros((cols, TILE), F32)
                    for old in before:
                        acc = acc + old[:, start:stop]
                    out[:, start:stop] = acc

            return call(
                kernel, [shape(cols, sep_width, dtype=F32)], index, [sep_inverse] + pieces + given,
                [pltpu.VMEM((cols, size), BF16)], 2 * cols * size * sep_width,
            )[0]

        def pull(parts):
            def kernel(idx, *refs):
                parts, out, pulled = refs[:n_leaf], refs[n_leaf], refs[n_leaf + 1]
                out[...] = add_all([ref[...] for ref in parts])
                pulled[...] = out[:, at(idx[2], blk)].astype(BF16)

            return call(
                kernel, [shape(cols, sep_width, dtype=F32), shape(cols, blk)], index, parts, [],
                cols * sep_width,
            )

        def backward_coupling(h, pieces):
            base = h * half

            def kernel(idx, cpl, *refs):
                pieces, outs, lhs = refs[:n], refs[n : 2 * n], refs[2 * n]
                for o in range(n):
                    for k in range(n):
                        lhs[at(idx[0] ^ idx[1] ^ k, chunk), at(idx[1] ^ o, blk)] = pieces[o][
                            k * chunk : (k + 1) * chunk, :
                        ]
                for start in range(0, half, TILE):
                    acc = dot_nt(lhs[...], cpl[base + start : base + start + TILE, :]).astype(BF16)
                    for p in range(n):
                        outs[p][:, start : start + TILE] = acc[p * chunk : (p + 1) * chunk]

            return call(
                kernel, [shape(chunk, half)] * n, index, [coupling] + pieces,
                [pltpu.VMEM((cols, span), BF16)], COVER * cols * half * span,
            )

        def backward_leaf(index, h, pieces):
            base = h * half
            later = PHASES - h

            def kernel(idx, inv, *refs):
                count = n * later
                pieces, outs, lhs = refs[:count], refs[count : count + n], refs[count + n]
                for k in range(later):
                    for p in range(n):
                        lhs[at(idx[0] ^ p, chunk), k * half : (k + 1) * half] = pieces[k * n + p][...]
                for start in range(0, half, TILE):
                    first = first_row(base + start, n_col, n_row, rows)
                    assert first >= base
                    acc = dot_nn(
                        lhs[:, first - base :], inv[first:, base + start : base + start + TILE]
                    ).astype(BF16)
                    for o in range(n):
                        outs[o][:, start : start + TILE] = acc[o * chunk : (o + 1) * chunk]

            return call(
                kernel, [shape(chunk, half)] * n, index, [leaf_inverse] + pieces,
                [pltpu.VMEM((cols, later * half), BF16)], 2 * cols * half * half * later,
            )

        source = leaf_t[offset : offset + chunk]
        if h:
            source = after(source, seen["A"][3])
        pieces = relay(source, source, "col")
        if TOUCH[h]:
            own = touch(index, leaf_inverse, seen["L"] if h else pieces[1])
        else:
            own = index
        seen["A"] = pieces
        parts = forward_leaf(0, own)(pieces)
        seen["L"] = parts[0]
        front = add_all(exchange(parts, "row")).astype(BF16)
        parts = forward_coupling(spread(front, "row"))
        coupled = add_all(exchange(parts, "col")).astype(BF16)
        sketch = sep_t[:, offset : offset + chunk].reshape(cols, sep_width)
        rhs = sep_rhs(sketch, spread(coupled, "leaf"))
        parts = exchange(forward_sep(index, 0, sep_rows, rhs[0]), "row")
        if h:
            parts = [after(parts[0], seen["mid"])] + parts[1:]
        parts = exchange(reduce_first(sep_rows, 1, parts), "col")
        if h:
            parts = [after(parts[0], seen["stack"])] + parts[1:]
        mid = add_all(parts).astype(BF16)
        stack = jnp.stack(spread(mid, "col"))
        seen["mid"], seen["stack"] = mid, stack
        pieces = spread(stack, "row")
        total = backward_sep(0, sep_rows, 0, pieces, None)
        out_sep, pulled = pull(spread(total, "leaf"))
        parts = backward_coupling(0, spread(pulled, "col"))
        back = add_all(exchange(parts, "row"))
        leaf_rhs = (front.astype(F32) - back).astype(BF16)
        pieces = spread(leaf_rhs, "row")
        own = touch(index, leaf_inverse, leaf_rhs) if TOUCH[2 + h] else index
        parts = backward_leaf(own, 0, pieces)
        return add_all(exchange(parts, "col")), out_sep

    seen = {}
    sizes = [wide * share // sum(SHARES) for share in SHARES]
    results = [stream(h, size, sum(sizes[:h])) for h, size in enumerate(sizes)]
    out_leaf = jnp.concatenate([leaf for leaf, _ in results], axis=0)
    out_sep = jnp.concatenate(
        [sep.reshape(n, size, sep_width) for size, (_, sep) in zip(sizes, results)], axis=1
    )
    return out_leaf.T, out_sep.reshape(sketch_sep.shape[1], sep_width).T


def solution(mesh):
    placed = (
        P(("leaf", "row"), "col"),
        P(("row", "col"), None),
        P(("leaf", "col"), "row"),
        P(("leaf", "col"), "row"),
        P("leaf", ("row", "col")),
        P(),
    )

    return jax.shard_map(
        shards,
        mesh=mesh,
        in_specs=placed,
        out_specs=(P(("leaf", "row"), "col"), P(("row", "col"), None)),
        check_vma=False,
    )
```

time: 187 us -> 192 us (1.027)
  waiting for transfers between devices: 43.3 us -> 47.7 us
  local copies, waits for them, and re-layouts: 14.3 us -> 12 us
  starting transfers between devices: 101 us -> 103 us
    ppermute x70, waiting for transfers between devices: 42.1 us -> 46.7 us  [exchange(): out.append(lax.ppermute(pieces[o], axis, [(i, i ^ o) for i in range(size)]))]
    unnamed x22 -> x20, local copies, waits for them, and re-layouts: 12 us -> 9.62 us
    ppermute x70, starting transfers between devices: 89.8 us -> 91.9 us  [exchange(): out.append(lax.ppermute(pieces[o], axis, [(i, i ^ o) for i in range(size)]))]
  transfers between devices with their start and end apart: 76 -> 76, of which waited for: 28 -> 26; matrix products, arithmetic and copies ran while one was open for 2% -> 3% of each run, Pallas kernels for 12% -> 11%
where the time goes in v3:
time: 192 us; the launch traced here: 191 us
  starting transfers between devices  103 us (54%)
  waiting for transfers between devices  47.7 us (25%)
  Pallas kernels  22.4 us (12%)
  local copies, waits for them, and re-layouts  12 us (6%)
  other arithmetic  3.19 us (2%)
  between operations  2.42 us (1%)
    ppermute x70, starting transfers between devices, exchange(): out.append(lax.ppermute(pieces[o], axis, [(i, i ^ o) for i in range(size)]))  91.9 us
    ppermute x70, waiting for transfers between devices, exchange(): out.append(lax.ppermute(pieces[o], axis, [(i, i ^ o) for i in range(size)]))  46.7 us
    pallas_call x18, Pallas kernels, call(): pl.pallas_call(kernel, out_shape=outs, in_specs=[pl.BlockSpec(memory_spac...  21.2 us
    ppermute x6, starting transfers between devices, relay(): lax.ppermute(piece, axis, [(i, i ^ {1: 1, 2: 1, 3: 3}[o]) for i in range(...  11.6 us
    unnamed x20, local copies, waits for them, and re-layouts  9.62 us
  transfers between devices with their start and end apart: 76, of which 26 were waited for; matrix products, arithmetic and copies ran while one was open for 3% of the time, Pallas kernels for 11%

profile of v3, /device:TPU:0, one launch (start us, length us, event | category | flops | bytes accessed | tf_op | source)
XLA Modules:
  0.0 191.2 jit_solution(8006130187475461779)
XLA Ops:
  1.6 5.1 %collective-permute-start.1 = (bf16[32,2048]{1,0:T(8,128)(2,1)S(1)}, bf16[32,2048]{1,0:T(8,128)(2,1)S(1)}, u32[]{:S(2)}, u32[]{:S(2)}) collective-permute-start(bf16[32,2048]{1,0:T(8,128)(2,1)S(1)} %get-tuple-element.116.refs_0_), channel_id=1, source_target_pairs={{0,3},{1,2},{2,1},{3,0},{4,7},{5,6},{6,5},{7,4},{8,11},{9,10},{10,... | collective-permute-start | bytes 393224 | tf_op jit(solution)/shard_map/ppermute | solution.py:92
  11.2 1.6 collective-permute-start.2
  14.0 2.3 %collective-permute-start.39 = (bf16[32,2048]{1,0:T(8,128)(2,1)S(1)}, bf16[32,2048]{1,0:T(8,128)(2,1)S(1)}, u32[]{:S(2)}, u32[]{:S(2)}) collective-permute-start(bf16[32,2048]{1,0:T(8,128)(2,1)S(1)} %get-tuple-element.82.refs_0_), channel_id=1, source_target_pairs={{0,3},{1,2},{2,1},{3,0},{4,7},{5,6},{6,5},{7,4},{8,11},{9,10},{10,... | collective-permute-start | bytes 393224 | tf_op jit(solution)/shard_map/ppermute | solution.py:92
  16.3 3.4 %copy-done = bf16[2048,2048]{1,0:T(8,128)(2,1)S(1)} copy-done((bf16[2048,2048]{1,0:T(8,128)(2,1)S(1)}, bf16[2048,2048]{1,0:T(8,128)(2,1)}, u32[]{:S(2)}) %copy-start) | copy-done | bytes 8388632
  20.3 2.2 %shard_map.77 = (bf16[32,2048]{1,0:T(8,128)(2,1)S(1)}, bf16[32,2048]{1,0:T(8,128)(2,1)S(1)}, bf16[32,2048]{1,0:T(8,128)(2,1)S(1)}, bf16[32,2048]{1,0:T(8,128)(2,1)S(1)}) custom-call(s32[4]{0:T(128)S(1)} %copy-done.4, bf16[2048,2048]{1,0:T(8,128)(2,1)S(1)} %copy-done, bf16[32,2048]{1,0:T(8,128)(2,1)S(1)} %get-tuple-element.116.refs_0_, ...), custom_call_target="tpu_custom_call" | custom-call | flops 1073741824 | bytes 8912896 | tf_op jit(solution)/shard_map/pallas_call | solution.py:30
  22.6 1.6 collective-permute-start.3
  24.1 1.5 collective-permute-start.4
  26.1 2.5 %collective-permute-start.38 = (bf16[32,2048]{1,0:T(8,128)(2,1)S(1)}, bf16[32,2048]{1,0:T(8,128)(2,1)S(1)}, u32[]{:S(2)}, u32[]{:S(2)}) collective-permute-start(bf16[32,2048]{1,0:T(8,128)(2,1)S(1)} %get-tuple-element.82.refs_0_), channel_id=1, source_target_pairs={{0,1},{1,0},{2,3},{3,2},{4,5},{5,4},{6,7},{7,6},{8,9},{9,8},{10,11... | collective-permute-start | bytes 393224 | tf_op jit(solution)/shard_map/ppermute | solution.py:92
  29.7 1.8 collective-permute-done.5
  32.7 2.4 %collective-permute-start.8 = (bf16[32,2048]{1,0:T(8,128)(2,1)S(1)}, bf16[32,2048]{1,0:T(8,128)(2,1)S(1)}, u32[]{:S(2)}, u32[]{:S(2)}) collective-permute-start(bf16[32,2048]{1,0:T(8,128)(2,1)S(1)} %add_convert_fusion.1.refs_0_), channel_id=1, source_target_pairs={{0,12},{4,8},{8,4},{12,0},{1,13},{5,9},{9,5},{13,1},{2,14},{6,10},... | collective-permute-start | bytes 393224 | tf_op jit(solution)/shard_map/ppermute | solution.py:81
  35.2 2.2 %shard_map.86 = (bf16[32,2048]{1,0:T(8,128)(2,1)S(1)}, bf16[32,2048]{1,0:T(8,128)(2,1)S(1)}, bf16[32,2048]{1,0:T(8,128)(2,1)S(1)}, bf16[32,2048]{1,0:T(8,128)(2,1)S(1)}) custom-call(s32[4]{0:T(128)S(1)} %copy-done.4, bf16[2048,2048]{1,0:T(8,128)(2,1)S(1)} %copy-done, bf16[32,2048]{1,0:T(8,128)(2,1)S(1)} %get-tuple-element.82.refs_0_, ...), custom_call_target="tpu_custom_call" | custom-call | flops 1073741824 | bytes 8912896 | tf_op jit(solution)/shard_map/pallas_call | solution.py:30
  38.9 2.1 %collective-permute-start.43 = (bf16[32,2048]{1,0:T(8,128)(2,1)S(1)}, bf16[32,2048]{1,0:T(8,128)(2,1)}, u32[]{:S(2)}, u32[]{:S(2)}) collective-permute-start(bf16[32,2048]{1,0:T(8,128)(2,1)S(1)} %get-tuple-element.86), channel_id=1, source_target_pairs={{0,12},{4,8},{8,4},{12,0},{1,13},{5,9},{9,5},{13,1},{2,14},{6,10},... | collective-permute-start | bytes 393224 | tf_op jit(solution)/shard_map/ppermute | solution.py:81
  43.2 4.7 %collective-permute-start.10 = (bf16[128,128]{1,0:T(8,128)(2,1)S(1)}, bf16[128,128]{1,0:T(8,128)(2,1)S(1)}, u32[]{:S(2)}, u32[]{:S(2)}) collective-permute-start(bf16[128,128]{1,0:T(8,128)(2,1)S(1)} %get-tuple-element.63), channel_id=1, source_target_pairs={{0,2},{1,3},{2,0},{3,1},{4,6},{5,7},{6,4},{7,5},{8,10},{9,11},{10,... | collective-permute-start | bytes 98312 | tf_op jit(solution)/shard_map/ppermute | solution.py:81
  47.9 1.8 collective-permute-start.11
  57.8 1.6 collective-permute-done.46.refs_3_
  62.0 2.5 %collective-permute-start.48 = (bf16[128,128]{1,0:T(8,128)(2,1)S(1)}, bf16[128,128]{1,0:T(8,128)(2,1)S(1)}, u32[]{:S(2)}, u32[]{:S(2)}) collective-permute-start(bf16[128,128]{1,0:T(8,128)(2,1)S(1)} %get-tuple-element.89), channel_id=1, source_target_pairs={{0,2},{1,3},{2,0},{3,1},{4,6},{5,7},{6,4},{7,5},{8,10},{9,11},{10,... | collective-permute-start | bytes 98312 | tf_op jit(solution)/shard_map/ppermute | solution.py:81
  65.0 1.5 shard_map.80
  66.5 2.0 %collective-permute-start.13 = (bf16[32,4096]{1,0:T(8,128)(2,1)S(1)}, bf16[32,4096]{1,0:T(8,128)(2,1)S(1)}, u32[]{:S(2)}, u32[]{:S(2)}) collective-permute-start(bf16[32,4096]{1,0:T(8,128)(2,1)S(1)} %get-tuple-element.66), channel_id=1, source_target_pairs={{0,4},{4,0},{8,12},{12,8},{1,5},{5,1},{9,13},{13,9},{2,6},{6,2},{1... | collective-permute-start | bytes 786440 | tf_op jit(solution)/shard_map/ppermute | solution.py:81
  72.0 2.4 %collective-permute-done.13.refs_1_ = bf16[32,4096]{1,0:T(8,128)(2,1)S(1)} collective-permute-done((bf16[32,4096]{1,0:T(8,128)(2,1)S(1)}, bf16[32,4096]{1,0:T(8,128)(2,1)S(1)}, u32[]{:S(2)}, u32[]{:S(2)}) %collective-permute-start.13) | collective-permute-done | bytes 262176 | tf_op jit(solution)/shard_map/ppermute | solution.py:81
  74.5 4.8 %collective-permute-done.14.refs_2_ = bf16[32,4096]{1,0:T(8,128)(2,1)S(1)} collective-permute-done((bf16[32,4096]{1,0:T(8,128)(2,1)S(1)}, bf16[32,4096]{1,0:T(8,128)(2,1)S(1)}, u32[]{:S(2)}, u32[]{:S(2)}) %collective-permute-start.14) | collective-permute-done | bytes 262176 | tf_op jit(solution)/shard_map/ppermute | solution.py:81
  80.5 2.8 %collective-permute-start.17 = (bf16[32,1024]{1,0:T(8,128)(2,1)S(1)}, bf16[32,1024]{1,0:T(8,128)(2,1)S(1)}, u32[]{:S(2)}, u32[]{:S(2)}) collective-permute-start(bf16[32,1024]{1,0:T(8,128)(2,1)S(1)} %get-tuple-element.71), channel_id=1, source_target_pairs={{0,2},{1,3},{2,0},{3,1},{4,6},{5,7},{6,4},{7,5},{8,10},{9,11},{10,... | collective-permute-start | bytes 196616 | tf_op jit(solution)/shard_map/ppermute | solution.py:81
  84.4 1.5 shard_map.89
  86.0 1.7 collective-permute-start.52
  87.7 1.8 collective-permute-start.53
  89.9 3.0 %collective-permute-start.20 = (bf16[32,1024]{1,0:T(8,128)(2,1)S(1)}, bf16[32,1024]{1,0:T(8,128)(2,1)S(1)}, u32[]{:S(2)}, u32[]{:S(2)}) collective-permute-start(bf16[32,1024]{1,0:T(8,128)(2,1)S(1)} %add_convert_fusion.3), channel_id=1, source_target_pairs={{0,2},{1,3},{2,0},{3,1},{4,6},{5,7},{6,4},{7,5},{8,10},{9,11},{10,... | collective-permute-start | bytes 196616 | tf_op jit(solution)/shard_map/ppermute | solution.py:81
  92.9 2.2 %collective-permute-start.21 = (bf16[32,1024]{1,0:T(8,128)(2,1)S(1)}, bf16[32,1024]{1,0:T(8,128)(2,1)S(1)}, u32[]{:S(2)}, u32[]{:S(2)}) collective-permute-start(bf16[32,1024]{1,0:T(8,128)(2,1)S(1)} %add_convert_fusion.3), channel_id=1, source_target_pairs={{0,3},{1,2},{2,1},{3,0},{4,7},{5,6},{6,5},{7,4},{8,11},{9,10},{10,... | collective-permute-start | bytes 196616 | tf_op jit(solution)/shard_map/ppermute | solution.py:81
  96.0 3.6 %collective-permute-start.55 = (bf16[32,1024]{1,0:T(8,128)(2,1)S(1)}, bf16[32,1024]{1,0:T(8,128)(2,1)S(1)}, u32[]{:S(2)}, u32[]{:S(2)}) collective-permute-start(bf16[32,1024]{1,0:T(8,128)(2,1)S(1)} %get-tuple-element.99), channel_id=1, source_target_pairs={{0,2},{1,3},{2,0},{3,1},{4,6},{5,7},{6,4},{7,5},{8,10},{9,11},{10,... | collective-permute-start | bytes 196616 | tf_op jit(solution)/shard_map/ppermute | solution.py:81
  100.4 2.0 %collective-permute-start.22 = (bf16[4,32,1024]{2,1,0:T(8,128)(2,1)S(1)}, bf16[4,32,1024]{2,1,0:T(8,128)(2,1)S(1)}, u32[]{:S(2)}, u32[]{:S(2)}) collective-permute-start(bf16[4,32,1024]{2,1,0:T(8,128)(2,1)S(1)} %pad_maximum_fusion.1.refs_0_), channel_id=1, source_target_pairs={{0,4},{4,0},{8,12},{12,8},{1,5},{5,1},{9,13},{13,9},{2,6},{6,2},{1... | collective-permute-start | bytes 786440 | tf_op jit(solution)/shard_map/ppermute | solution.py:81
  102.4 3.2 %collective-permute-done.56 = bf16[32,1024]{1,0:T(8,128)(2,1)S(1)} collective-permute-done((bf16[32,1024]{1,0:T(8,128)(2,1)S(1)}, bf16[32,1024]{1,0:T(8,128)(2,1)S(1)}, u32[]{:S(2)}, u32[]{:S(2)}) %collective-permute-start.56) | collective-permute-done | bytes 65568 | tf_op jit(solution)/shard_map/ppermute | solution.py:81
  108.1 2.0 %collective-permute-start.59 = (bf16[32,1024]{1,0:T(8,128)(2,1)S(1)}, bf16[32,1024]{1,0:T(8,128)(2,1)S(1)}, u32[]{:S(2)}, u32[]{:S(2)}) collective-permute-start(bf16[32,1024]{1,0:T(8,128)(2,1)S(1)} %add_convert_fusion.2), channel_id=1, source_target_pairs={{0,3},{1,2},{2,1},{3,0},{4,7},{5,6},{6,5},{7,4},{8,11},{9,10},{10,... | collective-permute-start | bytes 196616 | tf_op jit(solution)/shard_map/ppermute | solution.py:81
  110.1 1.9 collective-permute-start.23
  112.0 1.8 collective-permute-start.24
  114.3 2.0 %collective-permute-start.60 = (bf16[4,32,1024]{2,1,0:T(8,128)(2,1)S(1)}, bf16[4,32,1024]{2,1,0:T(8,128)(2,1)S(1)}, u32[]{:S(2)}, u32[]{:S(2)}) collective-permute-start(bf16[4,32,1024]{2,1,0:T(8,128)(2,1)S(1)} %pad_maximum_fusion.2.refs_0_), channel_id=1, source_target_pairs={{0,4},{4,0},{8,12},{12,8},{1,5},{5,1},{9,13},{13,9},{2,6},{6,2},{1... | collective-permute-start | bytes 786440 | tf_op jit(solution)/shard_map/ppermute | solution.py:81
  117.8 4.1 %collective-permute-done.23.refs_2_ = bf16[4,32,1024]{2,1,0:T(8,128)(2,1)S(1)} collective-permute-done((bf16[4,32,1024]{2,1,0:T(8,128)(2,1)S(1)}, bf16[4,32,1024]{2,1,0:T(8,128)(2,1)S(1)}, u32[]{:S(2)}, u32[]{:S(2)}) %collective-permute-start.23) | collective-permute-done | bytes 262176 | tf_op jit(solution)/shard_map/ppermute | solution.py:81
  123.3 4.3 %collective-permute-done.61.refs_2_ = bf16[4,32,1024]{2,1,0:T(8,128)(2,1)S(1)} collective-permute-done((bf16[4,32,1024]{2,1,0:T(8,128)(2,1)S(1)}, bf16[4,32,1024]{2,1,0:T(8,128)(2,1)S(1)}, u32[]{:S(2)}, u32[]{:S(2)}) %collective-permute-start.61) | collective-permute-done | bytes 262176 | tf_op jit(solution)/shard_map/ppermute | solution.py:81
  130.6 2.0 %collective-permute-start.27 = (bf16[128,128]{1,0:T(8,128)(2,1)S(1)}, bf16[128,128]{1,0:T(8,128)(2,1)S(1)}, u32[]{:S(2)}, u32[]{:S(2)}) collective-permute-start(bf16[128,128]{1,0:T(8,128)(2,1)S(1)} %get-tuple-element.73.refs_0_), channel_id=1, source_target_pairs={{0,2},{1,3},{2,0},{3,1},{4,6},{5,7},{6,4},{7,5},{8,10},{9,11},{10,... | collective-permute-start | bytes 98312 | tf_op jit(solution)/shard_map/ppermute | solution.py:81
  133.9 1.6 collective-permute-done.27.refs_2_
  135.6 2.7 %collective-permute-done.28.refs_3_ = bf16[128,128]{1,0:T(8,128)(2,1)S(1)} collective-permute-done((bf16[128,128]{1,0:T(8,128)(2,1)S(1)}, bf16[128,128]{1,0:T(8,128)(2,1)S(1)}, u32[]{:S(2)}, u32[]{:S(2)}) %collective-permute-start.28) | collective-permute-done | bytes 32800 | tf_op jit(solution)/shard_map/ppermute | solution.py:81
  143.9 1.9 collective-permute-start.65
  145.8 2.0 %collective-permute-done.64.refs_1_ = bf16[128,128]{1,0:T(8,128)(2,1)S(1)} collective-permute-done((bf16[128,128]{1,0:T(8,128)(2,1)S(1)}, bf16[128,128]{1,0:T(8,128)(2,1)S(1)}, u32[]{:S(2)}, u32[]{:S(2)}) %collective-permute-start.64) | collective-permute-done | bytes 32800 | tf_op jit(solution)/shard_map/ppermute | solution.py:81
  149.1 4.4 %collective-permute-done.66.refs_3_ = bf16[128,128]{1,0:T(8,128)(2,1)S(1)} collective-permute-done((bf16[128,128]{1,0:T(8,128)(2,1)S(1)}, bf16[128,128]{1,0:T(8,128)(2,1)S(1)}, u32[]{:S(2)}, u32[]{:S(2)}) %collective-permute-start.66) | collective-permute-done | bytes 32800 | tf_op jit(solution)/shard_map/ppermute | solution.py:81
  161.3 1.5 collective-permute-start.34
  170.3 2.3 %collective-permute-start.36 = (bf16[32,2048]{1,0:T(8,128)(2,1)S(1)}, bf16[32,2048]{1,0:T(8,128)(2,1)S(1)}, u32[]{:S(2)}, u32[]{:S(2)}) collective-permute-start(bf16[32,2048]{1,0:T(8,128)(2,1)S(1)} %get-tuple-element.80), channel_id=1, source_target_pairs={{0,2},{1,3},{2,0},{3,1},{4,6},{5,7},{6,4},{7,5},{8,10},{9,11},{10,... | collective-permute-start | bytes 393224 | tf_op jit(solution)/shard_map/ppermute | solution.py:81
  172.6 2.1 %collective-permute-start.37 = (bf16[32,2048]{1,0:T(8,128)(2,1)S(1)}, bf16[32,2048]{1,0:T(8,128)(2,1)S(1)}, u32[]{:S(2)}, u32[]{:S(2)}) collective-permute-start(bf16[32,2048]{1,0:T(8,128)(2,1)S(1)} %get-tuple-element.81), channel_id=1, source_target_pairs={{0,3},{1,2},{2,1},{3,0},{4,7},{5,6},{6,5},{7,4},{8,11},{9,10},{10,... | collective-permute-start | bytes 393224 | tf_op jit(solution)/shard_map/ppermute | solution.py:81
  175.7 3.4 %copy-done.1 = bf16[2048,2048]{1,0:T(8,128)(2,1)S(1)} copy-done((bf16[2048,2048]{1,0:T(8,128)(2,1)S(1)}, bf16[2048,2048]{1,0:T(8,128)(2,1)}, u32[]{:S(2)}) %copy-start.1) | copy-done | bytes 8388632
  180.5 2.3 %collective-permute-start.74 = (bf16[32,2048]{1,0:T(8,128)(2,1)S(1)}, bf16[32,2048]{1,0:T(8,128)(2,1)S(1)}, u32[]{:S(2)}, u32[]{:S(2)}) collective-permute-start(bf16[32,2048]{1,0:T(8,128)(2,1)S(1)} %get-tuple-element.108), channel_id=1, source_target_pairs={{0,2},{1,3},{2,0},{3,1},{4,6},{5,7},{6,4},{7,5},{8,10},{9,11},{10,... | collective-permute-start | bytes 393224 | tf_op jit(solution)/shard_map/ppermute | solution.py:81
  182.9 2.1 %collective-permute-start.75 = (bf16[32,2048]{1,0:T(8,128)(2,1)S(1)}, bf16[32,2048]{1,0:T(8,128)(2,1)S(1)}, u32[]{:S(2)}, u32[]{:S(2)}) collective-permute-start(bf16[32,2048]{1,0:T(8,128)(2,1)S(1)} %get-tuple-element.109), channel_id=1, source_target_pairs={{0,3},{1,2},{2,1},{3,0},{4,7},{5,6},{6,5},{7,4},{8,11},{9,10},{10,... | collective-permute-start | bytes 393224 | tf_op jit(solution)/shard_map/ppermute | solution.py:81
  185.7 4.6 %collective-permute-done.74 = bf16[32,2048]{1,0:T(8,128)(2,1)S(1)} collective-permute-done((bf16[32,2048]{1,0:T(8,128)(2,1)S(1)}, bf16[32,2048]{1,0:T(8,128)(2,1)S(1)}, u32[]{:S(2)}, u32[]{:S(2)}) %collective-permute-start.74) | collective-permute-done | bytes 131104 | tf_op jit(solution)/shard_map/ppermute | solution.py:81
  (162 shorter events, 68.0 us)
Async XLA Ops:
  1.6 9.5 %collective-permute-start.1 = (bf16[32,2048]{1,0:T(8,128)(2,1)S(1)}, bf16[32,2048]{1,0:T(8,128)(2,1)S(1)}, u32[]{:S(2)}, u32[]{:S(2)}) collective-permute-start(bf16[32,2048]{1,0:T(8,128)(2,1)S(1)} %get-tuple-element.116.refs_0_), channel_id=1, source_target_pairs={{0,3},{1,2},{2,1},{3,0},{4,7},{5,6},{6,5},{7,4},{8,11},{9,10},{10,... | collective-permute-start | bytes 393224 | tf_op jit(solution)/shard_map/ppermute | solution.py:92
  6.8 9.5 %collective-permute-start = (bf16[32,2048]{1,0:T(8,128)(2,1)S(1)}, bf16[32,2048]{1,0:T(8,128)(2,1)S(1)}, u32[]{:S(2)}, u32[]{:S(2)}) collective-permute-start(bf16[32,2048]{1,0:T(8,128)(2,1)S(1)} %get-tuple-element.116.refs_0_), channel_id=1, source_target_pairs={{0,1},{1,0},{2,3},{3,2},{4,5},{5,4},{6,7},{7,6},{8,9},{9,8},{10,11... | collective-permute-start | bytes 393224 | tf_op jit(solution)/shard_map/ppermute | solution.py:92
  14.0 14.6 %collective-permute-start.39 = (bf16[32,2048]{1,0:T(8,128)(2,1)S(1)}, bf16[32,2048]{1,0:T(8,128)(2,1)S(1)}, u32[]{:S(2)}, u32[]{:S(2)}) collective-permute-start(bf16[32,2048]{1,0:T(8,128)(2,1)S(1)} %get-tuple-element.82.refs_0_), channel_id=1, source_target_pairs={{0,3},{1,2},{2,1},{3,0},{4,7},{5,6},{6,5},{7,4},{8,11},{9,10},{10,... | collective-permute-start | bytes 393224 | tf_op jit(solution)/shard_map/ppermute | solution.py:92
  26.1 9.1 %collective-permute-start.38 = (bf16[32,2048]{1,0:T(8,128)(2,1)S(1)}, bf16[32,2048]{1,0:T(8,128)(2,1)S(1)}, u32[]{:S(2)}, u32[]{:S(2)}) collective-permute-start(bf16[32,2048]{1,0:T(8,128)(2,1)S(1)} %get-tuple-element.82.refs_0_), channel_id=1, source_target_pairs={{0,1},{1,0},{2,3},{3,2},{4,5},{5,4},{6,7},{7,6},{8,9},{9,8},{10,11... | collective-permute-start | bytes 393224 | tf_op jit(solution)/shard_map/ppermute | solution.py:92
  31.6 7.3 %collective-permute-start.6 = (bf16[32,2048]{1,0:T(8,128)(2,1)S(1)}, bf16[32,2048]{1,0:T(8,128)(2,1)S(1)}, u32[]{:S(2)}, u32[]{:S(2)}) collective-permute-start(bf16[32,2048]{1,0:T(8,128)(2,1)S(1)} %add_convert_fusion.1.refs_0_), channel_id=1, source_target_pairs={{0,4},{4,0},{8,12},{12,8},{1,5},{5,1},{9,13},{13,9},{2,6},{6,2},{1... | collective-permute-start | bytes 393224 | tf_op jit(solution)/shard_map/ppermute | solution.py:81
  32.4 9.6 %collective-permute-start.7 = (bf16[32,2048]{1,0:T(8,128)(2,1)S(1)}, bf16[32,2048]{1,0:T(8,128)(2,1)S(1)}, u32[]{:S(2)}, u32[]{:S(2)}) collective-permute-start(bf16[32,2048]{1,0:T(8,128)(2,1)S(1)} %add_convert_fusion.1.refs_0_), channel_id=1, source_target_pairs={{0,8},{4,12},{8,0},{12,4},{1,9},{5,13},{9,1},{13,5},{2,10},{6,14},... | collective-permute-start | bytes 393224 | tf_op jit(solution)/shard_map/ppermute | solution.py:81
  32.7 9.4 %collective-permute-start.8 = (bf16[32,2048]{1,0:T(8,128)(2,1)S(1)}, bf16[32,2048]{1,0:T(8,128)(2,1)S(1)}, u32[]{:S(2)}, u32[]{:S(2)}) collective-permute-start(bf16[32,2048]{1,0:T(8,128)(2,1)S(1)} %add_convert_fusion.1.refs_0_), channel_id=1, source_target_pairs={{0,12},{4,8},{8,4},{12,0},{1,13},{5,9},{9,5},{13,1},{2,14},{6,10},... | collective-permute-start | bytes 393224 | tf_op jit(solution)/shard_map/ppermute | solution.py:81
  37.4 12.3 %collective-permute-start.41 = (bf16[32,2048]{1,0:T(8,128)(2,1)S(1)}, bf16[32,2048]{1,0:T(8,128)(2,1)S(1)}, u32[]{:S(2)}, u32[]{:S(2)}) collective-permute-start(bf16[32,2048]{1,0:T(8,128)(2,1)S(1)} %get-tuple-element.84), channel_id=1, source_target_pairs={{0,4},{4,0},{8,12},{12,8},{1,5},{5,1},{9,13},{13,9},{2,6},{6,2},{1... | collective-permute-start | bytes 393224 | tf_op jit(solution)/shard_map/ppermute | solution.py:81
  38.2 12.0 %collective-permute-start.42 = (bf16[32,2048]{1,0:T(8,128)(2,1)S(1)}, bf16[32,2048]{1,0:T(8,128)(2,1)}, u32[]{:S(2)}, u32[]{:S(2)}) collective-permute-start(bf16[32,2048]{1,0:T(8,128)(2,1)S(1)} %get-tuple-element.85), channel_id=1, source_target_pairs={{0,8},{4,12},{8,0},{12,4},{1,9},{5,13},{9,1},{13,5},{2,10},{6,14},... | collective-permute-start | bytes 393224 | tf_op jit(solution)/shard_map/ppermute | solution.py:81
  38.9 11.4 %collective-permute-start.43 = (bf16[32,2048]{1,0:T(8,128)(2,1)S(1)}, bf16[32,2048]{1,0:T(8,128)(2,1)}, u32[]{:S(2)}, u32[]{:S(2)}) collective-permute-start(bf16[32,2048]{1,0:T(8,128)(2,1)S(1)} %get-tuple-element.86), channel_id=1, source_target_pairs={{0,12},{4,8},{8,4},{12,0},{1,13},{5,9},{9,5},{13,1},{2,14},{6,10},... | collective-permute-start | bytes 393224 | tf_op jit(solution)/shard_map/ppermute | solution.py:81
  43.2 10.4 %collective-permute-start.10 = (bf16[128,128]{1,0:T(8,128)(2,1)S(1)}, bf16[128,128]{1,0:T(8,128)(2,1)S(1)}, u32[]{:S(2)}, u32[]{:S(2)}) collective-permute-start(bf16[128,128]{1,0:T(8,128)(2,1)S(1)} %get-tuple-element.63), channel_id=1, source_target_pairs={{0,2},{1,3},{2,0},{3,1},{4,6},{5,7},{6,4},{7,5},{8,10},{9,11},{10,... | collective-permute-start | bytes 98312 | tf_op jit(solution)/shard_map/ppermute | solution.py:81
  47.9 7.1 %collective-permute-start.11 = (bf16[128,128]{1,0:T(8,128)(2,1)S(1)}, bf16[128,128]{1,0:T(8,128)(2,1)S(1)}, u32[]{:S(2)}, u32[]{:S(2)}) collective-permute-start(bf16[128,128]{1,0:T(8,128)(2,1)S(1)} %get-tuple-element.64), channel_id=1, source_target_pairs={{0,3},{1,2},{2,1},{3,0},{4,7},{5,6},{6,5},{7,4},{8,11},{9,10},{10,... | collective-permute-start | bytes 98312 | tf_op jit(solution)/shard_map/ppermute | solution.py:81
  60.5 8.5 %collective-permute-start.47 = (bf16[128,128]{1,0:T(8,128)(2,1)S(1)}, bf16[128,128]{1,0:T(8,128)(2,1)S(1)}, u32[]{:S(2)}, u32[]{:S(2)}) collective-permute-start(bf16[128,128]{1,0:T(8,128)(2,1)S(1)} %get-tuple-element.88), channel_id=1, source_target_pairs={{0,1},{1,0},{2,3},{3,2},{4,5},{5,4},{6,7},{7,6},{8,9},{9,8},{10,11... | collective-permute-start | bytes 98312 | tf_op jit(solution)/shard_map/ppermute | solution.py:81
  62.0 8.1 %collective-permute-start.48 = (bf16[128,128]{1,0:T(8,128)(2,1)S(1)}, bf16[128,128]{1,0:T(8,128)(2,1)S(1)}, u32[]{:S(2)}, u32[]{:S(2)}) collective-permute-start(bf16[128,128]{1,0:T(8,128)(2,1)S(1)} %get-tuple-element.89), channel_id=1, source_target_pairs={{0,2},{1,3},{2,0},{3,1},{4,6},{5,7},{6,4},{7,5},{8,10},{9,11},{10,... | collective-permute-start | bytes 98312 | tf_op jit(solution)/shard_map/ppermute | solution.py:81
  66.5 8.0 %collective-permute-start.13 = (bf16[32,4096]{1,0:T(8,128)(2,1)S(1)}, bf16[32,4096]{1,0:T(8,128)(2,1)S(1)}, u32[]{:S(2)}, u32[]{:S(2)}) collective-permute-start(bf16[32,4096]{1,0:T(8,128)(2,1)S(1)} %get-tuple-element.66), channel_id=1, source_target_pairs={{0,4},{4,0},{8,12},{12,8},{1,5},{5,1},{9,13},{13,9},{2,6},{6,2},{1... | collective-permute-start | bytes 786440 | tf_op jit(solution)/shard_map/ppermute | solution.py:81
  68.5 10.7 %collective-permute-start.14 = (bf16[32,4096]{1,0:T(8,128)(2,1)S(1)}, bf16[32,4096]{1,0:T(8,128)(2,1)S(1)}, u32[]{:S(2)}, u32[]{:S(2)}) collective-permute-start(bf16[32,4096]{1,0:T(8,128)(2,1)S(1)} %get-tuple-element.67), channel_id=1, source_target_pairs={{0,8},{4,12},{8,0},{12,4},{1,9},{5,13},{9,1},{13,5},{2,10},{6,14},... | collective-permute-start | bytes 786440 | tf_op jit(solution)/shard_map/ppermute | solution.py:81
  69.0 10.2 %collective-permute-start.15 = (bf16[32,4096]{1,0:T(8,128)(2,1)S(1)}, bf16[32,4096]{1,0:T(8,128)(2,1)S(1)}, u32[]{:S(2)}, u32[]{:S(2)}) collective-permute-start(bf16[32,4096]{1,0:T(8,128)(2,1)S(1)} %get-tuple-element.68), channel_id=1, source_target_pairs={{0,12},{4,8},{8,4},{12,0},{1,13},{5,9},{9,5},{13,1},{2,14},{6,10},... | collective-permute-start | bytes 786440 | tf_op jit(solution)/shard_map/ppermute | solution.py:81
  79.9 7.8 %collective-permute-start.16 = (bf16[32,1024]{1,0:T(8,128)(2,1)S(1)}, bf16[32,1024]{1,0:T(8,128)(2,1)S(1)}, u32[]{:S(2)}, u32[]{:S(2)}) collective-permute-start(bf16[32,1024]{1,0:T(8,128)(2,1)S(1)} %get-tuple-element.70), channel_id=1, source_target_pairs={{0,1},{1,0},{2,3},{3,2},{4,5},{5,4},{6,7},{7,6},{8,9},{9,8},{10,11... | collective-permute-start | bytes 196616 | tf_op jit(solution)/shard_map/ppermute | solution.py:81
  80.5 9.0 %collective-permute-start.17 = (bf16[32,1024]{1,0:T(8,128)(2,1)S(1)}, bf16[32,1024]{1,0:T(8,128)(2,1)S(1)}, u32[]{:S(2)}, u32[]{:S(2)}) collective-permute-start(bf16[32,1024]{1,0:T(8,128)(2,1)S(1)} %get-tuple-element.71), channel_id=1, source_target_pairs={{0,2},{1,3},{2,0},{3,1},{4,6},{5,7},{6,4},{7,5},{8,10},{9,11},{10,... | collective-permute-start | bytes 196616 | tf_op jit(solution)/shard_map/ppermute | solution.py:81
  85.9 7.0 %collective-permute-start.51 = (bf16[32,4096]{1,0:T(8,128)(2,1)S(1)}, bf16[32,4096]{1,0:T(8,128)(2,1)S(1)}, u32[]{:S(2)}, u32[]{:S(2)}) collective-permute-start(bf16[32,4096]{1,0:T(8,128)(2,1)S(1)} %get-tuple-element.93), channel_id=1, source_target_pairs={{0,4},{4,0},{8,12},{12,8},{1,5},{5,1},{9,13},{13,9},{2,6},{6,2},{1... | collective-permute-start | bytes 786440 | tf_op jit(solution)/shard_map/ppermute | solution.py:81
  86.0 9.2 %collective-permute-start.52 = (bf16[32,4096]{1,0:T(8,128)(2,1)S(1)}, bf16[32,4096]{1,0:T(8,128)(2,1)S(1)}, u32[]{:S(2)}, u32[]{:S(2)}) collective-permute-start(bf16[32,4096]{1,0:T(8,128)(2,1)S(1)} %get-tuple-element.94), channel_id=1, source_target_pairs={{0,8},{4,12},{8,0},{12,4},{1,9},{5,13},{9,1},{13,5},{2,10},{6,14},... | collective-permute-start | bytes 786440 | tf_op jit(solution)/shard_map/ppermute | solution.py:81
  87.7 7.5 %collective-permute-start.53 = (bf16[32,4096]{1,0:T(8,128)(2,1)S(1)}, bf16[32,4096]{1,0:T(8,128)(2,1)S(1)}, u32[]{:S(2)}, u32[]{:S(2)}) collective-permute-start(bf16[32,4096]{1,0:T(8,128)(2,1)S(1)} %get-tuple-element.95), channel_id=1, source_target_pairs={{0,12},{4,8},{8,4},{12,0},{1,13},{5,9},{9,5},{13,1},{2,14},{6,10},... | collective-permute-start | bytes 786440 | tf_op jit(solution)/shard_map/ppermute | solution.py:81
  89.8 9.7 %collective-permute-start.19 = (bf16[32,1024]{1,0:T(8,128)(2,1)S(1)}, bf16[32,1024]{1,0:T(8,128)(2,1)S(1)}, u32[]{:S(2)}, u32[]{:S(2)}) collective-permute-start(bf16[32,1024]{1,0:T(8,128)(2,1)S(1)} %add_convert_fusion.3), channel_id=1, source_target_pairs={{0,1},{1,0},{2,3},{3,2},{4,5},{5,4},{6,7},{7,6},{8,9},{9,8},{10,11... | collective-permute-start | bytes 196616 | tf_op jit(solution)/shard_map/ppermute | solution.py:81
  89.9 10.4 %collective-permute-start.20 = (bf16[32,1024]{1,0:T(8,128)(2,1)S(1)}, bf16[32,1024]{1,0:T(8,128)(2,1)S(1)}, u32[]{:S(2)}, u32[]{:S(2)}) collective-permute-start(bf16[32,1024]{1,0:T(8,128)(2,1)S(1)} %add_convert_fusion.3), channel_id=1, source_target_pairs={{0,2},{1,3},{2,0},{3,1},{4,6},{5,7},{6,4},{7,5},{8,10},{9,11},{10,... | collective-permute-start | bytes 196616 | tf_op jit(solution)/shard_map/ppermute | solution.py:81
  92.9 7.5 %collective-permute-start.21 = (bf16[32,1024]{1,0:T(8,128)(2,1)S(1)}, bf16[32,1024]{1,0:T(8,128)(2,1)S(1)}, u32[]{:S(2)}, u32[]{:S(2)}) collective-permute-start(bf16[32,1024]{1,0:T(8,128)(2,1)S(1)} %add_convert_fusion.3), channel_id=1, source_target_pairs={{0,3},{1,2},{2,1},{3,0},{4,7},{5,6},{6,5},{7,4},{8,11},{9,10},{10,... | collective-permute-start | bytes 196616 | tf_op jit(solution)/shard_map/ppermute | solution.py:81
  100.4 16.2 %collective-permute-start.22 = (bf16[4,32,1024]{2,1,0:T(8,128)(2,1)S(1)}, bf16[4,32,1024]{2,1,0:T(8,128)(2,1)S(1)}, u32[]{:S(2)}, u32[]{:S(2)}) collective-permute-start(bf16[4,32,1024]{2,1,0:T(8,128)(2,1)S(1)} %pad_maximum_fusion.1.refs_0_), channel_id=1, source_target_pairs={{0,4},{4,0},{8,12},{12,8},{1,5},{5,1},{9,13},{13,9},{2,6},{6,2},{1... | collective-permute-start | bytes 786440 | tf_op jit(solution)/shard_map/ppermute | solution.py:81
  110.1 11.9 %collective-permute-start.23 = (bf16[4,32,1024]{2,1,0:T(8,128)(2,1)S(1)}, bf16[4,32,1024]{2,1,0:T(8,128)(2,1)S(1)}, u32[]{:S(2)}, u32[]{:S(2)}) collective-permute-start(bf16[4,32,1024]{2,1,0:T(8,128)(2,1)S(1)} %pad_maximum_fusion.1.refs_0_), channel_id=1, source_target_pairs={{0,8},{4,12},{8,0},{12,4},{1,9},{5,13},{9,1},{13,5},{2,10},{6,14},... | collective-permute-start | bytes 786440 | tf_op jit(solution)/shard_map/ppermute | solution.py:81
  112.0 10.0 %collective-permute-start.24 = (bf16[4,32,1024]{2,1,0:T(8,128)(2,1)S(1)}, bf16[4,32,1024]{2,1,0:T(8,128)(2,1)S(1)}, u32[]{:S(2)}, u32[]{:S(2)}) collective-permute-start(bf16[4,32,1024]{2,1,0:T(8,128)(2,1)S(1)} %pad_maximum_fusion.1.refs_0_), channel_id=1, source_target_pairs={{0,12},{4,8},{8,4},{12,0},{1,13},{5,9},{9,5},{13,1},{2,14},{6,10},... | collective-permute-start | bytes 786440 | tf_op jit(solution)/shard_map/ppermute | solution.py:81
  114.3 9.0 %collective-permute-start.60 = (bf16[4,32,1024]{2,1,0:T(8,128)(2,1)S(1)}, bf16[4,32,1024]{2,1,0:T(8,128)(2,1)S(1)}, u32[]{:S(2)}, u32[]{:S(2)}) collective-permute-start(bf16[4,32,1024]{2,1,0:T(8,128)(2,1)S(1)} %pad_maximum_fusion.2.refs_0_), channel_id=1, source_target_pairs={{0,4},{4,0},{8,12},{12,8},{1,5},{5,1},{9,13},{13,9},{2,6},{6,2},{1... | collective-permute-start | bytes 786440 | tf_op jit(solution)/shard_map/ppermute | solution.py:81
  116.2 11.3 %collective-permute-start.61 = (bf16[4,32,1024]{2,1,0:T(8,128)(2,1)S(1)}, bf16[4,32,1024]{2,1,0:T(8,128)(2,1)S(1)}, u32[]{:S(2)}, u32[]{:S(2)}) collective-permute-start(bf16[4,32,1024]{2,1,0:T(8,128)(2,1)S(1)} %pad_maximum_fusion.2.refs_0_), channel_id=1, source_target_pairs={{0,8},{4,12},{8,0},{12,4},{1,9},{5,13},{9,1},{13,5},{2,10},{6,14},... | collective-permute-start | bytes 786440 | tf_op jit(solution)/shard_map/ppermute | solution.py:81
  116.6 11.0 %collective-permute-start.62 = (bf16[4,32,1024]{2,1,0:T(8,128)(2,1)S(1)}, bf16[4,32,1024]{2,1,0:T(8,128)(2,1)S(1)}, u32[]{:S(2)}, u32[]{:S(2)}) collective-permute-start(bf16[4,32,1024]{2,1,0:T(8,128)(2,1)S(1)} %pad_maximum_fusion.2.refs_0_), channel_id=1, source_target_pairs={{0,12},{4,8},{8,4},{12,0},{1,13},{5,9},{9,5},{13,1},{2,14},{6,10},... | collective-permute-start | bytes 786440 | tf_op jit(solution)/shard_map/ppermute | solution.py:81
  128.8 14.4 %collective-permute-start.63 = (f32[128,512]{1,0:T(8,128)S(1)}, f32[128,512]{1,0:T(8,128)S(1)}, u32[]{:S(2)}, u32[]{:S(2)}) collective-permute-start(f32[128,512]{1,0:T(8,128)S(1)} %shard_map.91.refs_0_), channel_id=1, source_target_pairs={{0,16},{16,0},{1,17},{17,1},{2,18},{18,2},{3,19},{19,3},{4,20},{20... | collective-permute-start | bytes 786440 | tf_op jit(solution)/shard_map/ppermute | solution.py:81
  139.7 17.3 %collective-permute-start.29 = (bf16[32,2048]{1,0:T(8,128)(2,1)S(1)}, bf16[32,2048]{1,0:T(8,128)(2,1)S(1)}, u32[]{:S(2)}, u32[]{:S(2)}) collective-permute-start(bf16[32,2048]{1,0:T(8,128)(2,1)S(1)} %get-tuple-element.75), channel_id=1, source_target_pairs={{0,4},{4,0},{8,12},{12,8},{1,5},{5,1},{9,13},{13,9},{2,6},{6,2},{1... | collective-permute-start | bytes 393224 | tf_op jit(solution)/shard_map/ppermute | solution.py:81
  140.7 17.8 %collective-permute-start.30 = (bf16[32,2048]{1,0:T(8,128)(2,1)S(1)}, bf16[32,2048]{1,0:T(8,128)(2,1)S(1)}, u32[]{:S(2)}, u32[]{:S(2)}) collective-permute-start(bf16[32,2048]{1,0:T(8,128)(2,1)S(1)} %get-tuple-element.76), channel_id=1, source_target_pairs={{0,8},{4,12},{8,0},{12,4},{1,9},{5,13},{9,1},{13,5},{2,10},{6,14},... | collective-permute-start | bytes 393224 | tf_op jit(solution)/shard_map/ppermute | solution.py:81
  141.8 16.6 %collective-permute-start.31 = (bf16[32,2048]{1,0:T(8,128)(2,1)S(1)}, bf16[32,2048]{1,0:T(8,128)(2,1)S(1)}, u32[]{:S(2)}, u32[]{:S(2)}) collective-permute-start(bf16[32,2048]{1,0:T(8,128)(2,1)S(1)} %get-tuple-element.77), channel_id=1, source_target_pairs={{0,12},{4,8},{8,4},{12,0},{1,13},{5,9},{9,5},{13,1},{2,14},{6,10},... | collective-permute-start | bytes 393224 | tf_op jit(solution)/shard_map/ppermute | solution.py:81
  155.9 7.9 %collective-permute-start.68 = (bf16[32,2048]{1,0:T(8,128)(2,1)S(1)}, bf16[32,2048]{1,0:T(8,128)(2,1)S(1)}, u32[]{:S(2)}, u32[]{:S(2)}) collective-permute-start(bf16[32,2048]{1,0:T(8,128)(2,1)S(1)} %get-tuple-element.104), channel_id=1, source_target_pairs={{0,8},{4,12},{8,0},{12,4},{1,9},{5,13},{9,1},{13,5},{2,10},{6,14},... | collective-permute-start | bytes 393224 | tf_op jit(solution)/shard_map/ppermute | solution.py:81
  157.0 7.5 %collective-permute-start.69 = (bf16[32,2048]{1,0:T(8,128)(2,1)S(1)}, bf16[32,2048]{1,0:T(8,128)(2,1)S(1)}, u32[]{:S(2)}, u32[]{:S(2)}) collective-permute-start(bf16[32,2048]{1,0:T(8,128)(2,1)S(1)} %get-tuple-element.105), channel_id=1, source_target_pairs={{0,12},{4,8},{8,4},{12,0},{1,13},{5,9},{9,5},{13,1},{2,14},{6,10},... | collective-permute-start | bytes 393224 | tf_op jit(solution)/shard_map/ppermute | solution.py:81
  158.5 8.2 %collective-permute-start.32 = (bf16[32,2048]{1,0:T(8,128)(2,1)S(1)}, bf16[32,2048]{1,0:T(8,128)(2,1)S(1)}, u32[]{:S(2)}, u32[]{:S(2)}) collective-permute-start(bf16[32,2048]{1,0:T(8,128)(2,1)S(1)} %subtract_convert_fusion.1.refs_0_), channel_id=1, source_target_pairs={{0,4},{4,0},{8,12},{12,8},{1,5},{5,1},{9,13},{13,9},{2,6},{6,2},{1... | collective-permute-start | bytes 393224 | tf_op jit(solution)/shard_map/ppermute | solution.py:81
  159.5 9.3 %collective-permute-start.33 = (bf16[32,2048]{1,0:T(8,128)(2,1)S(1)}, bf16[32,2048]{1,0:T(8,128)(2,1)S(1)}, u32[]{:S(2)}, u32[]{:S(2)}) collective-permute-start(bf16[32,2048]{1,0:T(8,128)(2,1)S(1)} %subtract_convert_fusion.1.refs_0_), channel_id=1, source_target_pairs={{0,8},{4,12},{8,0},{12,4},{1,9},{5,13},{9,1},{13,5},{2,10},{6,14},... | collective-permute-start | bytes 393224 | tf_op jit(solution)/shard_map/ppermute | solution.py:81
  161.3 7.5 %collective-permute-start.34 = (bf16[32,2048]{1,0:T(8,128)(2,1)S(1)}, bf16[32,2048]{1,0:T(8,128)(2,1)S(1)}, u32[]{:S(2)}, u32[]{:S(2)}) collective-permute-start(bf16[32,2048]{1,0:T(8,128)(2,1)S(1)} %subtract_convert_fusion.1.refs_0_), channel_id=1, source_target_pairs={{0,12},{4,8},{8,4},{12,0},{1,13},{5,9},{9,5},{13,1},{2,14},{6,10},... | collective-permute-start | bytes 393224 | tf_op jit(solution)/shard_map/ppermute | solution.py:81
  164.6 8.0 %collective-permute-start.70 = (bf16[32,2048]{1,0:T(8,128)(2,1)S(1)}, bf16[32,2048]{1,0:T(8,128)(2,1)S(1)}, u32[]{:S(2)}, u32[]{:S(2)}) collective-permute-start(bf16[32,2048]{1,0:T(8,128)(2,1)S(1)} %subtract_convert_fusion.refs_0_), channel_id=1, source_target_pairs={{0,4},{4,0},{8,12},{12,8},{1,5},{5,1},{9,13},{13,9},{2,6},{6,2},{1... | collective-permute-start | bytes 393224 | tf_op jit(solution)/shard_map/ppermute | solution.py:81
  165.9 9.8 %collective-permute-start.71 = (bf16[32,2048]{1,0:T(8,128)(2,1)S(1)}, bf16[32,2048]{1,0:T(8,128)(2,1)S(1)}, u32[]{:S(2)}, u32[]{:S(2)}) collective-permute-start(bf16[32,2048]{1,0:T(8,128)(2,1)S(1)} %subtract_convert_fusion.refs_0_), channel_id=1, source_target_pairs={{0,8},{4,12},{8,0},{12,4},{1,9},{5,13},{9,1},{13,5},{2,10},{6,14},... | collective-permute-start | bytes 393224 | tf_op jit(solution)/shard_map/ppermute | solution.py:81
  166.8 9.0 %collective-permute-start.72 = (bf16[32,2048]{1,0:T(8,128)(2,1)S(1)}, bf16[32,2048]{1,0:T(8,128)(2,1)S(1)}, u32[]{:S(2)}, u32[]{:S(2)}) collective-permute-start(bf16[32,2048]{1,0:T(8,128)(2,1)S(1)} %subtract_convert_fusion.refs_0_), channel_id=1, source_target_pairs={{0,12},{4,8},{8,4},{12,0},{1,13},{5,9},{9,5},{13,1},{2,14},{6,10},... | collective-permute-start | bytes 393224 | tf_op jit(solution)/shard_map/ppermute | solution.py:81
  170.2 12.6 %collective-permute-start.35 = (bf16[32,2048]{1,0:T(8,128)(2,1)S(1)}, bf16[32,2048]{1,0:T(8,128)(2,1)S(1)}, u32[]{:S(2)}, u32[]{:S(2)}) collective-permute-start(bf16[32,2048]{1,0:T(8,128)(2,1)S(1)} %get-tuple-element.79), channel_id=1, source_target_pairs={{0,1},{1,0},{2,3},{3,2},{4,5},{5,4},{6,7},{7,6},{8,9},{9,8},{10,11... | collective-permute-start | bytes 393224 | tf_op jit(solution)/shard_map/ppermute | solution.py:81
  170.3 14.6 %collective-permute-start.36 = (bf16[32,2048]{1,0:T(8,128)(2,1)S(1)}, bf16[32,2048]{1,0:T(8,128)(2,1)S(1)}, u32[]{:S(2)}, u32[]{:S(2)}) collective-permute-start(bf16[32,2048]{1,0:T(8,128)(2,1)S(1)} %get-tuple-element.80), channel_id=1, source_target_pairs={{0,2},{1,3},{2,0},{3,1},{4,6},{5,7},{6,4},{7,5},{8,10},{9,11},{10,... | collective-permute-start | bytes 393224 | tf_op jit(solution)/shard_map/ppermute | solution.py:81
  172.6 12.3 %collective-permute-start.37 = (bf16[32,2048]{1,0:T(8,128)(2,1)S(1)}, bf16[32,2048]{1,0:T(8,128)(2,1)S(1)}, u32[]{:S(2)}, u32[]{:S(2)}) collective-permute-start(bf16[32,2048]{1,0:T(8,128)(2,1)S(1)} %get-tuple-element.81), channel_id=1, source_target_pairs={{0,3},{1,2},{2,1},{3,0},{4,7},{5,6},{6,5},{7,4},{8,11},{9,10},{10,... | collective-permute-start | bytes 393224 | tf_op jit(solution)/shard_map/ppermute | solution.py:81
  180.5 9.8 %collective-permute-start.74 = (bf16[32,2048]{1,0:T(8,128)(2,1)S(1)}, bf16[32,2048]{1,0:T(8,128)(2,1)S(1)}, u32[]{:S(2)}, u32[]{:S(2)}) collective-permute-start(bf16[32,2048]{1,0:T(8,128)(2,1)S(1)} %get-tuple-element.108), channel_id=1, source_target_pairs={{0,2},{1,3},{2,0},{3,1},{4,6},{5,7},{6,4},{7,5},{8,10},{9,11},{10,... | collective-permute-start | bytes 393224 | tf_op jit(solution)/shard_map/ppermute | solution.py:81
  182.9 7.5 %collective-permute-start.75 = (bf16[32,2048]{1,0:T(8,128)(2,1)S(1)}, bf16[32,2048]{1,0:T(8,128)(2,1)S(1)}, u32[]{:S(2)}, u32[]{:S(2)}) collective-permute-start(bf16[32,2048]{1,0:T(8,128)(2,1)S(1)} %get-tuple-element.109), channel_id=1, source_target_pairs={{0,3},{1,2},{2,1},{3,0},{4,7},{5,6},{6,5},{7,4},{8,11},{9,10},{10,... | collective-permute-start | bytes 393224 | tf_op jit(solution)/shard_map/ppermute | solution.py:81
  (37 other events, 296.0 us)

commit v4 on v3

--- a/solution.py
+++ b/solution.py
@@ -11,8 +11,6 @@
 KERNEL_BYTES = 24 << 20
 TILE = 256
 COVER = 2
-SETTLE = 10**10
-TOUCH = False, False, False, False
 F32 = jnp.float32
 BF16 = jnp.bfloat16
 
@@ -41,37 +39,6 @@
 
 def after(value, *done):
     return lax.optimization_barrier((value, *done))[0]
-
-
-def settle(index):
-    def kernel(index, out):
-        for k in range(index.shape[0]):
-            out[k] = index[k]
-
-    return pl.pallas_call(
-        kernel,
-        out_shape=jax.ShapeDtypeStruct(index.shape, index.dtype),
-        in_specs=[pl.BlockSpec(memory_space=pltpu.SMEM)],
-        out_specs=pl.BlockSpec(memory_space=pltpu.SMEM),
-        cost_estimate=pl.CostEstimate(flops=SETTLE, bytes_accessed=64, transcendentals=0),
-        name="settle",
-    )(index)
-
-
-def touch(index, panel, done):
-    def kernel(index, panel, done, out):
-        for k in range(index.shape[0]):
-            out[k] = index[k]
-
-    spaces = pltpu.SMEM, pltpu.VMEM, pl.ANY
-    return pl.pallas_call(
-        kernel,
-        out_shape=jax.ShapeDtypeStruct(index.shape, index.dtype),
-        in_specs=[pl.BlockSpec(memory_space=space) for space in spaces],
-        out_specs=pl.BlockSpec(memory_space=pltpu.SMEM),
-        compiler_params=pltpu.CompilerParams(vmem_limit_bytes=KERNEL_BYTES),
-        name="touch",
-    )(index, panel, done)
 
 
 def exchange(pieces, axis):
@@ -130,7 +97,7 @@
     slots = [
         jnp.clip(front_map[section ^ o, q] - q * group, 0, group - 1) for o in range(n_leaf)
     ]
-    index = settle(jnp.stack([r, c] + slots).astype(jnp.int32))
+    index = jnp.stack([r, c] + slots).astype(jnp.int32)
 
     leaf_t = sketch_leaf.T
     sep_t = sketch_sep.T.reshape(n, wide, sep_width)
@@ -316,13 +283,8 @@
         if h:
             source = after(source, seen["A"][3])
         pieces = relay(source, source, "col")
-        if TOUCH[h]:
-            own = touch(index, leaf_inverse, seen["L"] if h else pieces[1])
-        else:
-            own = index
         seen["A"] = pieces
-        parts = forward_leaf(0, own)(pieces)
-        seen["L"] = parts[0]
+        parts = forward_leaf(0, index)(pieces)
         front = add_all(exchange(parts, "row")).astype(BF16)
         parts = forward_coupling(spread(front, "row"))
         coupled = add_all(exchange(parts, "col")).astype(BF16)
@@ -344,8 +306,7 @@
         back = add_all(exchange(parts, "row"))
         leaf_rhs = (front.astype(F32) - back).astype(BF16)
         pieces = spread(leaf_rhs, "row")
-        own = touch(index, leaf_inverse, leaf_rhs) if TOUCH[2 + h] else index
-        parts = backward_leaf(own, 0, pieces)
+        parts = backward_leaf(index, 0, pieces)
         return add_all(exchange(parts, "col")), out_sep
 
     seen = {}

time: 192 us -> 188 us (0.979)
  starting transfers between devices: 103 us -> 97.5 us
  waiting for transfers between devices: 47.7 us -> 52.7 us
    ppermute x70, starting transfers between devices: 91.9 us -> 86.5 us  [exchange(): out.append(lax.ppermute(pieces[o], axis, [(i, i ^ o) for i in range(size)]))]
    ppermute x6, waiting for transfers between devices: 1.03 us -> 4.4 us  [relay(): lax.ppermute(piece, axis, [(i, i ^ {1: 1, 2: 1, 3: 3}[o]) for i in range(...]
    unnamed x20 -> x14, local copies, waits for them, and re-layouts: 9.62 us -> 8.87 us
  transfers between devices with their start and end apart: 76 -> 76, of which waited for: 26 -> 26; matrix products, arithmetic and copies ran while one was open for 3% -> 3% of each run, Pallas kernels for 11% -> 10%
where the time goes in v4:
time: 188 us
  starting transfers between devices  97.5 us (52%)
  waiting for transfers between devices  52.7 us (28%)
  Pallas kernels  21 us (11%)
  local copies, waits for them, and re-layouts  11.3 us (6%)
  other arithmetic  2.56 us (1%)
  between operations  2.41 us (1%)
    ppermute x70, starting transfers between devices, exchange(): out.append(lax.ppermute(pieces[o], axis, [(i, i ^ o) for i in range(size)]))  86.5 us
    ppermute x70, waiting for transfers between devices, exchange(): out.append(lax.ppermute(pieces[o], axis, [(i, i ^ o) for i in range(size)]))  48.3 us
    pallas_call x18, Pallas kernels, call(): pl.pallas_call(kernel, out_shape=outs, in_specs=[pl.BlockSpec(memory_spac...  21 us
    ppermute x6, starting transfers between devices, relay(): lax.ppermute(piece, axis, [(i, i ^ {1: 1, 2: 1, 3: 3}[o]) for i in range(...  11 us
    unnamed x14, local copies, waits for them, and re-layouts  8.87 us
    ppermute x6, waiting for transfers between devices, relay(): lax.ppermute(piece, axis, [(i, i ^ {1: 1, 2: 1, 3: 3}[o]) for i in range(...  4.4 us
  transfers between devices with their start and end apart: 76, of which 26 were waited for; matrix products, arithmetic and copies ran while one was open for 3% of the time, Pallas kernels for 10%

profile of v4, /device:TPU:0, one launch (start us, length us, event | category | flops | bytes accessed | tf_op | source)
XLA Modules:
  0.0 187.5 jit_solution(14941012443156945742)
XLA Ops:
  1.6 5.1 %collective-permute-start.1 = (bf16[32,2048]{1,0:T(8,128)(2,1)S(1)}, bf16[32,2048]{1,0:T(8,128)(2,1)S(1)}, u32[]{:S(2)}, u32[]{:S(2)}) collective-permute-start(bf16[32,2048]{1,0:T(8,128)(2,1)S(1)} %get-tuple-element.116.refs_0_), channel_id=1, source_target_pairs={{0,3},{1,2},{2,1},{3,0},{4,7},{5,6},{6,5},{7,4},{8,11},{9,10},{10,... | collective-permute-start | bytes 393224 | tf_op jit(solution)/shard_map/ppermute | solution.py:59
  6.8 4.4 %collective-permute-done.1.refs_3_ = bf16[32,2048]{1,0:T(8,128)(2,1)S(1)} collective-permute-done((bf16[32,2048]{1,0:T(8,128)(2,1)S(1)}, bf16[32,2048]{1,0:T(8,128)(2,1)S(1)}, u32[]{:S(2)}, u32[]{:S(2)}) %collective-permute-start.1) | collective-permute-done | bytes 131104 | tf_op jit(solution)/shard_map/ppermute | solution.py:59
  11.2 1.6 collective-permute-start.2
  15.6 2.2 %collective-permute-start.39 = (bf16[32,2048]{1,0:T(8,128)(2,1)S(1)}, bf16[32,2048]{1,0:T(8,128)(2,1)S(1)}, u32[]{:S(2)}, u32[]{:S(2)}) collective-permute-start(bf16[32,2048]{1,0:T(8,128)(2,1)S(1)} %get-tuple-element.82.refs_0_), channel_id=1, source_target_pairs={{0,3},{1,2},{2,1},{3,0},{4,7},{5,6},{6,5},{7,4},{8,11},{9,10},{10,... | collective-permute-start | bytes 393224 | tf_op jit(solution)/shard_map/ppermute | solution.py:59
  17.9 3.4 %copy-done = bf16[2048,2048]{1,0:T(8,128)(2,1)S(1)} copy-done((bf16[2048,2048]{1,0:T(8,128)(2,1)S(1)}, bf16[2048,2048]{1,0:T(8,128)(2,1)}, u32[]{:S(2)}) %copy-start) | copy-done | bytes 8388632
  21.2 2.2 %shard_map.77 = (bf16[32,2048]{1,0:T(8,128)(2,1)S(1)}, bf16[32,2048]{1,0:T(8,128)(2,1)S(1)}, bf16[32,2048]{1,0:T(8,128)(2,1)S(1)}, bf16[32,2048]{1,0:T(8,128)(2,1)S(1)}) custom-call(s32[4]{0:T(128)S(1)} %pad_add_fusion.idx, bf16[2048,2048]{1,0:T(8,128)(2,1)S(1)} %copy-done, bf16[32,2048]{1,0:T(8,128)(2,1)S(1)} %get-tuple-element.116.refs_0_, ...), custom_call_target="tpu_custom_call" | custom-call | flops 1073741824 | bytes 8912896 | tf_op jit(solution)/shard_map/pallas_call | solution.py:28
  23.4 1.6 collective-permute-start.3
  25.0 1.5 collective-permute-start.4
  30.1 3.2 %collective-permute-done.5 = bf16[32,2048]{1,0:T(8,128)(2,1)S(1)} collective-permute-done((bf16[32,2048]{1,0:T(8,128)(2,1)S(1)}, bf16[32,2048]{1,0:T(8,128)(2,1)S(1)}, u32[]{:S(2)}, u32[]{:S(2)}) %collective-permute-start.5) | collective-permute-done | bytes 131104 | tf_op jit(solution)/shard_map/ppermute | solution.py:48
  34.2 2.8 %collective-permute-start.8 = (bf16[32,2048]{1,0:T(8,128)(2,1)S(1)}, bf16[32,2048]{1,0:T(8,128)(2,1)S(1)}, u32[]{:S(2)}, u32[]{:S(2)}) collective-permute-start(bf16[32,2048]{1,0:T(8,128)(2,1)S(1)} %add_convert_fusion.1.refs_0_), channel_id=1, source_target_pairs={{0,12},{4,8},{8,4},{12,0},{1,13},{5,9},{9,5},{13,1},{2,14},{6,10},... | collective-permute-start | bytes 393224 | tf_op jit(solution)/shard_map/ppermute | solution.py:48
  37.0 2.2 %shard_map.86 = (bf16[32,2048]{1,0:T(8,128)(2,1)S(1)}, bf16[32,2048]{1,0:T(8,128)(2,1)S(1)}, bf16[32,2048]{1,0:T(8,128)(2,1)S(1)}, bf16[32,2048]{1,0:T(8,128)(2,1)S(1)}) custom-call(s32[4]{0:T(128)S(1)} %pad_add_fusion.idx, bf16[2048,2048]{1,0:T(8,128)(2,1)S(1)} %copy-done, bf16[32,2048]{1,0:T(8,128)(2,1)S(1)} %get-tuple-element.82.refs_0_, ...), custom_call_target="tpu_custom_call" | custom-call | flops 1073741824 | bytes 8912896 | tf_op jit(solution)/shard_map/pallas_call | solution.py:28
  40.0 2.8 %collective-permute-start.43 = (bf16[32,2048]{1,0:T(8,128)(2,1)S(1)}, bf16[32,2048]{1,0:T(8,128)(2,1)}, u32[]{:S(2)}, u32[]{:S(2)}) collective-permute-start(bf16[32,2048]{1,0:T(8,128)(2,1)S(1)} %get-tuple-element.86), channel_id=1, source_target_pairs={{0,12},{4,8},{8,4},{12,0},{1,13},{5,9},{9,5},{13,1},{2,14},{6,10},... | collective-permute-start | bytes 393224 | tf_op jit(solution)/shard_map/ppermute | solution.py:48
  45.8 2.7 %collective-permute-start.11 = (bf16[128,128]{1,0:T(8,128)(2,1)S(1)}, bf16[128,128]{1,0:T(8,128)(2,1)S(1)}, u32[]{:S(2)}, u32[]{:S(2)}) collective-permute-start(bf16[128,128]{1,0:T(8,128)(2,1)S(1)} %get-tuple-element.64), channel_id=1, source_target_pairs={{0,3},{1,2},{2,1},{3,0},{4,7},{5,6},{6,5},{7,4},{8,11},{9,10},{10,... | collective-permute-start | bytes 98312 | tf_op jit(solution)/shard_map/ppermute | solution.py:48
  51.7 1.5 collective-permute-start.46
  55.4 2.1 %collective-permute-done.46.refs_3_ = bf16[32,2048]{1,0:T(8,128)(2,1)S(1)} collective-permute-done((bf16[32,2048]{1,0:T(8,128)(2,1)S(1)}, bf16[32,2048]{1,0:T(8,128)(2,1)S(1)}, u32[]{:S(2)}, u32[]{:S(2)}) %collective-permute-start.46) | collective-permute-done | bytes 131104 | tf_op jit(solution)/shard_map/ppermute | solution.py:48
  60.1 3.0 %collective-permute-start.49 = (bf16[128,128]{1,0:T(8,128)(2,1)S(1)}, bf16[128,128]{1,0:T(8,128)(2,1)S(1)}, u32[]{:S(2)}, u32[]{:S(2)}) collective-permute-start(bf16[128,128]{1,0:T(8,128)(2,1)S(1)} %get-tuple-element.90), channel_id=1, source_target_pairs={{0,3},{1,2},{2,1},{3,0},{4,7},{5,6},{6,5},{7,4},{8,11},{9,10},{10,... | collective-permute-start | bytes 98312 | tf_op jit(solution)/shard_map/ppermute | solution.py:48
  63.0 1.5 shard_map.80
  65.2 1.5 collective-permute-start.14
  70.0 2.9 %collective-permute-done.13.refs_1_ = bf16[32,4096]{1,0:T(8,128)(2,1)S(1)} collective-permute-done((bf16[32,4096]{1,0:T(8,128)(2,1)S(1)}, bf16[32,4096]{1,0:T(8,128)(2,1)S(1)}, u32[]{:S(2)}, u32[]{:S(2)}) %collective-permute-start.13) | collective-permute-done | bytes 262176 | tf_op jit(solution)/shard_map/ppermute | solution.py:48
  72.9 3.3 %collective-permute-done.14.refs_2_ = bf16[32,4096]{1,0:T(8,128)(2,1)S(1)} collective-permute-done((bf16[32,4096]{1,0:T(8,128)(2,1)S(1)}, bf16[32,4096]{1,0:T(8,128)(2,1)S(1)}, u32[]{:S(2)}, u32[]{:S(2)}) %collective-permute-start.14) | collective-permute-done | bytes 262176 | tf_op jit(solution)/shard_map/ppermute | solution.py:48
  78.9 2.4 %collective-permute-start.18 = (bf16[32,1024]{1,0:T(8,128)(2,1)S(1)}, bf16[32,1024]{1,0:T(8,128)(2,1)S(1)}, u32[]{:S(2)}, u32[]{:S(2)}) collective-permute-start(bf16[32,1024]{1,0:T(8,128)(2,1)S(1)} %get-tuple-element.72), channel_id=1, source_target_pairs={{0,3},{1,2},{2,1},{3,0},{4,7},{5,6},{6,5},{7,4},{8,11},{9,10},{10,... | collective-permute-start | bytes 196616 | tf_op jit(solution)/shard_map/ppermute | solution.py:48
  81.3 1.5 shard_map.89
  86.6 2.2 %collective-permute-start.20 = (bf16[32,1024]{1,0:T(8,128)(2,1)S(1)}, bf16[32,1024]{1,0:T(8,128)(2,1)S(1)}, u32[]{:S(2)}, u32[]{:S(2)}) collective-permute-start(bf16[32,1024]{1,0:T(8,128)(2,1)S(1)} %add_convert_fusion.3), channel_id=1, source_target_pairs={{0,2},{1,3},{2,0},{3,1},{4,6},{5,7},{6,4},{7,5},{8,10},{9,11},{10,... | collective-permute-start | bytes 196616 | tf_op jit(solution)/shard_map/ppermute | solution.py:48
  89.3 1.6 collective-permute-start.21
  90.9 2.4 %collective-permute-done.52.refs_2_ = bf16[32,4096]{1,0:T(8,128)(2,1)S(1)} collective-permute-done((bf16[32,4096]{1,0:T(8,128)(2,1)S(1)}, bf16[32,4096]{1,0:T(8,128)(2,1)S(1)}, u32[]{:S(2)}, u32[]{:S(2)}) %collective-permute-start.52) | collective-permute-done | bytes 262176 | tf_op jit(solution)/shard_map/ppermute | solution.py:48
  94.1 1.9 %collective-permute-start.55 = (bf16[32,1024]{1,0:T(8,128)(2,1)S(1)}, bf16[32,1024]{1,0:T(8,128)(2,1)S(1)}, u32[]{:S(2)}, u32[]{:S(2)}) collective-permute-start(bf16[32,1024]{1,0:T(8,128)(2,1)S(1)} %get-tuple-element.99), channel_id=1, source_target_pairs={{0,2},{1,3},{2,0},{3,1},{4,6},{5,7},{6,4},{7,5},{8,10},{9,11},{10,... | collective-permute-start | bytes 196616 | tf_op jit(solution)/shard_map/ppermute | solution.py:48
  96.0 2.5 %collective-permute-start.56 = (bf16[32,1024]{1,0:T(8,128)(2,1)S(1)}, bf16[32,1024]{1,0:T(8,128)(2,1)S(1)}, u32[]{:S(2)}, u32[]{:S(2)}) collective-permute-start(bf16[32,1024]{1,0:T(8,128)(2,1)S(1)} %get-tuple-element.100), channel_id=1, source_target_pairs={{0,3},{1,2},{2,1},{3,0},{4,7},{5,6},{6,5},{7,4},{8,11},{9,10},{10,... | collective-permute-start | bytes 196616 | tf_op jit(solution)/shard_map/ppermute | solution.py:48
  99.4 3.5 %collective-permute-done.56 = bf16[32,1024]{1,0:T(8,128)(2,1)S(1)} collective-permute-done((bf16[32,1024]{1,0:T(8,128)(2,1)S(1)}, bf16[32,1024]{1,0:T(8,128)(2,1)S(1)}, u32[]{:S(2)}, u32[]{:S(2)}) %collective-permute-start.56) | collective-permute-done | bytes 65568 | tf_op jit(solution)/shard_map/ppermute | solution.py:48
  103.1 2.8 %collective-permute-start.58 = (bf16[32,1024]{1,0:T(8,128)(2,1)S(1)}, bf16[32,1024]{1,0:T(8,128)(2,1)S(1)}, u32[]{:S(2)}, u32[]{:S(2)}) collective-permute-start(bf16[32,1024]{1,0:T(8,128)(2,1)S(1)} %add_convert_fusion.2), channel_id=1, source_target_pairs={{0,2},{1,3},{2,0},{3,1},{4,6},{5,7},{6,4},{7,5},{8,10},{9,11},{10,... | collective-permute-start | bytes 196616 | tf_op jit(solution)/shard_map/ppermute | solution.py:48
  105.8 1.6 collective-permute-start.59
  109.6 2.3 %collective-permute-done.59 = bf16[32,1024]{1,0:T(8,128)(2,1)S(1)} collective-permute-done((bf16[32,1024]{1,0:T(8,128)(2,1)S(1)}, bf16[32,1024]{1,0:T(8,128)(2,1)S(1)}, u32[]{:S(2)}, u32[]{:S(2)}) %collective-permute-start.59) | collective-permute-done | bytes 65568 | tf_op jit(solution)/shard_map/ppermute | solution.py:48
  115.5 3.9 %collective-permute-done.23.refs_2_ = bf16[4,32,1024]{2,1,0:T(8,128)(2,1)S(1)} collective-permute-done((bf16[4,32,1024]{2,1,0:T(8,128)(2,1)S(1)}, bf16[4,32,1024]{2,1,0:T(8,128)(2,1)S(1)}, u32[]{:S(2)}, u32[]{:S(2)}) %collective-permute-start.23) | collective-permute-done | bytes 262176 | tf_op jit(solution)/shard_map/ppermute | solution.py:48
  120.7 4.3 %collective-permute-done.61.refs_2_ = bf16[4,32,1024]{2,1,0:T(8,128)(2,1)S(1)} collective-permute-done((bf16[4,32,1024]{2,1,0:T(8,128)(2,1)S(1)}, bf16[4,32,1024]{2,1,0:T(8,128)(2,1)S(1)}, u32[]{:S(2)}, u32[]{:S(2)}) %collective-permute-start.61) | collective-permute-done | bytes 262176 | tf_op jit(solution)/shard_map/ppermute | solution.py:48
  127.0 1.9 %collective-permute-start.27 = (bf16[128,128]{1,0:T(8,128)(2,1)S(1)}, bf16[128,128]{1,0:T(8,128)(2,1)S(1)}, u32[]{:S(2)}, u32[]{:S(2)}) collective-permute-start(bf16[128,128]{1,0:T(8,128)(2,1)S(1)} %get-tuple-element.73.refs_0_), channel_id=1, source_target_pairs={{0,2},{1,3},{2,0},{3,1},{4,6},{5,7},{6,4},{7,5},{8,10},{9,11},{10,... | collective-permute-start | bytes 98312 | tf_op jit(solution)/shard_map/ppermute | solution.py:48
  128.9 2.5 %collective-permute-start.28 = (bf16[128,128]{1,0:T(8,128)(2,1)S(1)}, bf16[128,128]{1,0:T(8,128)(2,1)S(1)}, u32[]{:S(2)}, u32[]{:S(2)}) collective-permute-start(bf16[128,128]{1,0:T(8,128)(2,1)S(1)} %get-tuple-element.73.refs_0_), channel_id=1, source_target_pairs={{0,3},{1,2},{2,1},{3,0},{4,7},{5,6},{6,5},{7,4},{8,11},{9,10},{10,... | collective-permute-start | bytes 98312 | tf_op jit(solution)/shard_map/ppermute | solution.py:48
  132.1 2.5 %collective-permute-done.28.refs_3_ = bf16[128,128]{1,0:T(8,128)(2,1)S(1)} collective-permute-done((bf16[128,128]{1,0:T(8,128)(2,1)S(1)}, bf16[128,128]{1,0:T(8,128)(2,1)S(1)}, u32[]{:S(2)}, u32[]{:S(2)}) %collective-permute-start.28) | collective-permute-done | bytes 32800 | tf_op jit(solution)/shard_map/ppermute | solution.py:48
  137.9 1.6 collective-permute-start.31
  140.2 3.0 %collective-permute-start.65 = (bf16[128,128]{1,0:T(8,128)(2,1)S(1)}, bf16[128,128]{1,0:T(8,128)(2,1)S(1)}, u32[]{:S(2)}, u32[]{:S(2)}) collective-permute-start(bf16[128,128]{1,0:T(8,128)(2,1)S(1)} %get-tuple-element.101.refs_0_), channel_id=1, source_target_pairs={{0,2},{1,3},{2,0},{3,1},{4,6},{5,7},{6,4},{7,5},{8,10},{9,11},{10,... | collective-permute-start | bytes 98312 | tf_op jit(solution)/shard_map/ppermute | solution.py:48
  144.1 2.5 %collective-permute-start.66 = (bf16[128,128]{1,0:T(8,128)(2,1)S(1)}, bf16[128,128]{1,0:T(8,128)(2,1)S(1)}, u32[]{:S(2)}, u32[]{:S(2)}) collective-permute-start(bf16[128,128]{1,0:T(8,128)(2,1)S(1)} %get-tuple-element.101.refs_0_), channel_id=1, source_target_pairs={{0,3},{1,2},{2,1},{3,0},{4,7},{5,6},{6,5},{7,4},{8,11},{9,10},{10,... | collective-permute-start | bytes 98312 | tf_op jit(solution)/shard_map/ppermute | solution.py:48
  146.6 3.2 %collective-permute-done.66.refs_3_ = bf16[128,128]{1,0:T(8,128)(2,1)S(1)} collective-permute-done((bf16[128,128]{1,0:T(8,128)(2,1)S(1)}, bf16[128,128]{1,0:T(8,128)(2,1)S(1)}, u32[]{:S(2)}, u32[]{:S(2)}) %collective-permute-start.66) | collective-permute-done | bytes 32800 | tf_op jit(solution)/shard_map/ppermute | solution.py:48
  153.1 1.6 collective-permute-start.69
  162.0 1.5 collective-permute-start.71
  166.6 2.8 %collective-permute-start.36 = (bf16[32,2048]{1,0:T(8,128)(2,1)S(1)}, bf16[32,2048]{1,0:T(8,128)(2,1)S(1)}, u32[]{:S(2)}, u32[]{:S(2)}) collective-permute-start(bf16[32,2048]{1,0:T(8,128)(2,1)S(1)} %get-tuple-element.80), channel_id=1, source_target_pairs={{0,2},{1,3},{2,0},{3,1},{4,6},{5,7},{6,4},{7,5},{8,10},{9,11},{10,... | collective-permute-start | bytes 393224 | tf_op jit(solution)/shard_map/ppermute | solution.py:48
  169.4 1.6 collective-permute-start.37
  172.0 3.4 %copy-done.1 = bf16[2048,2048]{1,0:T(8,128)(2,1)S(1)} copy-done((bf16[2048,2048]{1,0:T(8,128)(2,1)S(1)}, bf16[2048,2048]{1,0:T(8,128)(2,1)}, u32[]{:S(2)}) %copy-start.1) | copy-done | bytes 8388632
  176.8 2.8 %collective-permute-start.74 = (bf16[32,2048]{1,0:T(8,128)(2,1)S(1)}, bf16[32,2048]{1,0:T(8,128)(2,1)S(1)}, u32[]{:S(2)}, u32[]{:S(2)}) collective-permute-start(bf16[32,2048]{1,0:T(8,128)(2,1)S(1)} %get-tuple-element.108), channel_id=1, source_target_pairs={{0,2},{1,3},{2,0},{3,1},{4,6},{5,7},{6,4},{7,5},{8,10},{9,11},{10,... | collective-permute-start | bytes 393224 | tf_op jit(solution)/shard_map/ppermute | solution.py:48
  179.6 1.6 collective-permute-start.75
  181.8 4.8 %collective-permute-done.74 = bf16[32,2048]{1,0:T(8,128)(2,1)S(1)} collective-permute-done((bf16[32,2048]{1,0:T(8,128)(2,1)S(1)}, bf16[32,2048]{1,0:T(8,128)(2,1)S(1)}, u32[]{:S(2)}, u32[]{:S(2)}) %collective-permute-start.74) | collective-permute-done | bytes 131104 | tf_op jit(solution)/shard_map/ppermute | solution.py:48
  (155 shorter events, 63.4 us)
Async XLA Ops:
  1.6 9.5 %collective-permute-start.1 = (bf16[32,2048]{1,0:T(8,128)(2,1)S(1)}, bf16[32,2048]{1,0:T(8,128)(2,1)S(1)}, u32[]{:S(2)}, u32[]{:S(2)}) collective-permute-start(bf16[32,2048]{1,0:T(8,128)(2,1)S(1)} %get-tuple-element.116.refs_0_), channel_id=1, source_target_pairs={{0,3},{1,2},{2,1},{3,0},{4,7},{5,6},{6,5},{7,4},{8,11},{9,10},{10,... | collective-permute-start | bytes 393224 | tf_op jit(solution)/shard_map/ppermute | solution.py:59
  6.8 11.1 %collective-permute-start = (bf16[32,2048]{1,0:T(8,128)(2,1)S(1)}, bf16[32,2048]{1,0:T(8,128)(2,1)S(1)}, u32[]{:S(2)}, u32[]{:S(2)}) collective-permute-start(bf16[32,2048]{1,0:T(8,128)(2,1)S(1)} %get-tuple-element.116.refs_0_), channel_id=1, source_target_pairs={{0,1},{1,0},{2,3},{3,2},{4,5},{5,4},{6,7},{7,6},{8,9},{9,8},{10,11... | collective-permute-start | bytes 393224 | tf_op jit(solution)/shard_map/ppermute | solution.py:59
  15.6 12.4 %collective-permute-start.39 = (bf16[32,2048]{1,0:T(8,128)(2,1)S(1)}, bf16[32,2048]{1,0:T(8,128)(2,1)S(1)}, u32[]{:S(2)}, u32[]{:S(2)}) collective-permute-start(bf16[32,2048]{1,0:T(8,128)(2,1)S(1)} %get-tuple-element.82.refs_0_), channel_id=1, source_target_pairs={{0,3},{1,2},{2,1},{3,0},{4,7},{5,6},{6,5},{7,4},{8,11},{9,10},{10,... | collective-permute-start | bytes 393224 | tf_op jit(solution)/shard_map/ppermute | solution.py:59
  27.0 10.0 %collective-permute-start.38 = (bf16[32,2048]{1,0:T(8,128)(2,1)S(1)}, bf16[32,2048]{1,0:T(8,128)(2,1)S(1)}, u32[]{:S(2)}, u32[]{:S(2)}) collective-permute-start(bf16[32,2048]{1,0:T(8,128)(2,1)S(1)} %get-tuple-element.82.refs_0_), channel_id=1, source_target_pairs={{0,1},{1,0},{2,3},{3,2},{4,5},{5,4},{6,7},{7,6},{8,9},{9,8},{10,11... | collective-permute-start | bytes 393224 | tf_op jit(solution)/shard_map/ppermute | solution.py:59
  28.0 9.0 %collective-permute-start.40 = (bf16[32,2048]{1,0:T(8,128)(2,1)S(1)}, bf16[32,2048]{1,0:T(8,128)(2,1)S(1)}, u32[]{:S(2)}, u32[]{:S(2)}) collective-permute-start(bf16[32,2048]{1,0:T(8,128)(2,1)S(1)} %collective-permute-done.39.refs_3_), channel_id=1, source_target_pairs={{0,1},{1,0},{2,3},{3,2},{4,5},{5,4},{6,7},{7,6},{8,9},{9,8},{10,11... | collective-permute-start | bytes 393224 | tf_op jit(solution)/shard_map/ppermute | solution.py:59
  34.2 9.7 %collective-permute-start.7 = (bf16[32,2048]{1,0:T(8,128)(2,1)S(1)}, bf16[32,2048]{1,0:T(8,128)(2,1)S(1)}, u32[]{:S(2)}, u32[]{:S(2)}) collective-permute-start(bf16[32,2048]{1,0:T(8,128)(2,1)S(1)} %add_convert_fusion.1.refs_0_), channel_id=1, source_target_pairs={{0,8},{4,12},{8,0},{12,4},{1,9},{5,13},{9,1},{13,5},{2,10},{6,14},... | collective-permute-start | bytes 393224 | tf_op jit(solution)/shard_map/ppermute | solution.py:48
  34.2 9.7 %collective-permute-start.8 = (bf16[32,2048]{1,0:T(8,128)(2,1)S(1)}, bf16[32,2048]{1,0:T(8,128)(2,1)S(1)}, u32[]{:S(2)}, u32[]{:S(2)}) collective-permute-start(bf16[32,2048]{1,0:T(8,128)(2,1)S(1)} %add_convert_fusion.1.refs_0_), channel_id=1, source_target_pairs={{0,12},{4,8},{8,4},{12,0},{1,13},{5,9},{9,5},{13,1},{2,14},{6,10},... | collective-permute-start | bytes 393224 | tf_op jit(solution)/shard_map/ppermute | solution.py:48
  39.2 9.3 %collective-permute-start.41 = (bf16[32,2048]{1,0:T(8,128)(2,1)S(1)}, bf16[32,2048]{1,0:T(8,128)(2,1)S(1)}, u32[]{:S(2)}, u32[]{:S(2)}) collective-permute-start(bf16[32,2048]{1,0:T(8,128)(2,1)S(1)} %get-tuple-element.84), channel_id=1, source_target_pairs={{0,4},{4,0},{8,12},{12,8},{1,5},{5,1},{9,13},{13,9},{2,6},{6,2},{1... | collective-permute-start | bytes 393224 | tf_op jit(solution)/shard_map/ppermute | solution.py:48
  40.0 8.5 %collective-permute-start.42 = (bf16[32,2048]{1,0:T(8,128)(2,1)S(1)}, bf16[32,2048]{1,0:T(8,128)(2,1)}, u32[]{:S(2)}, u32[]{:S(2)}) collective-permute-start(bf16[32,2048]{1,0:T(8,128)(2,1)S(1)} %get-tuple-element.85), channel_id=1, source_target_pairs={{0,8},{4,12},{8,0},{12,4},{1,9},{5,13},{9,1},{13,5},{2,10},{6,14},... | collective-permute-start | bytes 393224 | tf_op jit(solution)/shard_map/ppermute | solution.py:48
  40.0 8.5 %collective-permute-start.43 = (bf16[32,2048]{1,0:T(8,128)(2,1)S(1)}, bf16[32,2048]{1,0:T(8,128)(2,1)}, u32[]{:S(2)}, u32[]{:S(2)}) collective-permute-start(bf16[32,2048]{1,0:T(8,128)(2,1)S(1)} %get-tuple-element.86), channel_id=1, source_target_pairs={{0,12},{4,8},{8,4},{12,0},{1,13},{5,9},{9,5},{13,1},{2,14},{6,10},... | collective-permute-start | bytes 393224 | tf_op jit(solution)/shard_map/ppermute | solution.py:48
  45.8 7.4 %collective-permute-start.11 = (bf16[128,128]{1,0:T(8,128)(2,1)S(1)}, bf16[128,128]{1,0:T(8,128)(2,1)S(1)}, u32[]{:S(2)}, u32[]{:S(2)}) collective-permute-start(bf16[128,128]{1,0:T(8,128)(2,1)S(1)} %get-tuple-element.64), channel_id=1, source_target_pairs={{0,3},{1,2},{2,1},{3,0},{4,7},{5,6},{6,5},{7,4},{8,11},{9,10},{10,... | collective-permute-start | bytes 98312 | tf_op jit(solution)/shard_map/ppermute | solution.py:48
  58.6 8.2 %collective-permute-start.47 = (bf16[128,128]{1,0:T(8,128)(2,1)S(1)}, bf16[128,128]{1,0:T(8,128)(2,1)S(1)}, u32[]{:S(2)}, u32[]{:S(2)}) collective-permute-start(bf16[128,128]{1,0:T(8,128)(2,1)S(1)} %get-tuple-element.88), channel_id=1, source_target_pairs={{0,1},{1,0},{2,3},{3,2},{4,5},{5,4},{6,7},{7,6},{8,9},{9,8},{10,11... | collective-permute-start | bytes 98312 | tf_op jit(solution)/shard_map/ppermute | solution.py:48
  60.1 8.0 %collective-permute-start.48 = (bf16[128,128]{1,0:T(8,128)(2,1)S(1)}, bf16[128,128]{1,0:T(8,128)(2,1)S(1)}, u32[]{:S(2)}, u32[]{:S(2)}) collective-permute-start(bf16[128,128]{1,0:T(8,128)(2,1)S(1)} %get-tuple-element.89), channel_id=1, source_target_pairs={{0,2},{1,3},{2,0},{3,1},{4,6},{5,7},{6,4},{7,5},{8,10},{9,11},{10,... | collective-permute-start | bytes 98312 | tf_op jit(solution)/shard_map/ppermute | solution.py:48
  60.1 8.0 %collective-permute-start.49 = (bf16[128,128]{1,0:T(8,128)(2,1)S(1)}, bf16[128,128]{1,0:T(8,128)(2,1)S(1)}, u32[]{:S(2)}, u32[]{:S(2)}) collective-permute-start(bf16[128,128]{1,0:T(8,128)(2,1)S(1)} %get-tuple-element.90), channel_id=1, source_target_pairs={{0,3},{1,2},{2,1},{3,0},{4,7},{5,6},{6,5},{7,4},{8,11},{9,10},{10,... | collective-permute-start | bytes 98312 | tf_op jit(solution)/shard_map/ppermute | solution.py:48
  64.5 8.3 %collective-permute-start.13 = (bf16[32,4096]{1,0:T(8,128)(2,1)S(1)}, bf16[32,4096]{1,0:T(8,128)(2,1)S(1)}, u32[]{:S(2)}, u32[]{:S(2)}) collective-permute-start(bf16[32,4096]{1,0:T(8,128)(2,1)S(1)} %get-tuple-element.66), channel_id=1, source_target_pairs={{0,4},{4,0},{8,12},{12,8},{1,5},{5,1},{9,13},{13,9},{2,6},{6,2},{1... | collective-permute-start | bytes 786440 | tf_op jit(solution)/shard_map/ppermute | solution.py:48
  65.2 11.0 %collective-permute-start.14 = (bf16[32,4096]{1,0:T(8,128)(2,1)S(1)}, bf16[32,4096]{1,0:T(8,128)(2,1)S(1)}, u32[]{:S(2)}, u32[]{:S(2)}) collective-permute-start(bf16[32,4096]{1,0:T(8,128)(2,1)S(1)} %get-tuple-element.67), channel_id=1, source_target_pairs={{0,8},{4,12},{8,0},{12,4},{1,9},{5,13},{9,1},{13,5},{2,10},{6,14},... | collective-permute-start | bytes 786440 | tf_op jit(solution)/shard_map/ppermute | solution.py:48
  66.7 9.5 %collective-permute-start.15 = (bf16[32,4096]{1,0:T(8,128)(2,1)S(1)}, bf16[32,4096]{1,0:T(8,128)(2,1)S(1)}, u32[]{:S(2)}, u32[]{:S(2)}) collective-permute-start(bf16[32,4096]{1,0:T(8,128)(2,1)S(1)} %get-tuple-element.68), channel_id=1, source_target_pairs={{0,12},{4,8},{8,4},{12,0},{1,13},{5,9},{9,5},{13,1},{2,14},{6,10},... | collective-permute-start | bytes 786440 | tf_op jit(solution)/shard_map/ppermute | solution.py:48
  76.9 8.2 %collective-permute-start.16 = (bf16[32,1024]{1,0:T(8,128)(2,1)S(1)}, bf16[32,1024]{1,0:T(8,128)(2,1)S(1)}, u32[]{:S(2)}, u32[]{:S(2)}) collective-permute-start(bf16[32,1024]{1,0:T(8,128)(2,1)S(1)} %get-tuple-element.70), channel_id=1, source_target_pairs={{0,1},{1,0},{2,3},{3,2},{4,5},{5,4},{6,7},{7,6},{8,9},{9,8},{10,11... | collective-permute-start | bytes 196616 | tf_op jit(solution)/shard_map/ppermute | solution.py:48
  77.7 8.7 %collective-permute-start.17 = (bf16[32,1024]{1,0:T(8,128)(2,1)S(1)}, bf16[32,1024]{1,0:T(8,128)(2,1)S(1)}, u32[]{:S(2)}, u32[]{:S(2)}) collective-permute-start(bf16[32,1024]{1,0:T(8,128)(2,1)S(1)} %get-tuple-element.71), channel_id=1, source_target_pairs={{0,2},{1,3},{2,0},{3,1},{4,6},{5,7},{6,4},{7,5},{8,10},{9,11},{10,... | collective-permute-start | bytes 196616 | tf_op jit(solution)/shard_map/ppermute | solution.py:48
  78.9 7.5 %collective-permute-start.18 = (bf16[32,1024]{1,0:T(8,128)(2,1)S(1)}, bf16[32,1024]{1,0:T(8,128)(2,1)S(1)}, u32[]{:S(2)}, u32[]{:S(2)}) collective-permute-start(bf16[32,1024]{1,0:T(8,128)(2,1)S(1)} %get-tuple-element.72), channel_id=1, source_target_pairs={{0,3},{1,2},{2,1},{3,0},{4,7},{5,6},{6,5},{7,4},{8,11},{9,10},{10,... | collective-permute-start | bytes 196616 | tf_op jit(solution)/shard_map/ppermute | solution.py:48
  84.2 9.2 %collective-permute-start.52 = (bf16[32,4096]{1,0:T(8,128)(2,1)S(1)}, bf16[32,4096]{1,0:T(8,128)(2,1)S(1)}, u32[]{:S(2)}, u32[]{:S(2)}) collective-permute-start(bf16[32,4096]{1,0:T(8,128)(2,1)S(1)} %get-tuple-element.94), channel_id=1, source_target_pairs={{0,8},{4,12},{8,0},{12,4},{1,9},{5,13},{9,1},{13,5},{2,10},{6,14},... | collective-permute-start | bytes 786440 | tf_op jit(solution)/shard_map/ppermute | solution.py:48
  85.1 8.3 %collective-permute-start.53 = (bf16[32,4096]{1,0:T(8,128)(2,1)S(1)}, bf16[32,4096]{1,0:T(8,128)(2,1)S(1)}, u32[]{:S(2)}, u32[]{:S(2)}) collective-permute-start(bf16[32,4096]{1,0:T(8,128)(2,1)S(1)} %get-tuple-element.95), channel_id=1, source_target_pairs={{0,12},{4,8},{8,4},{12,0},{1,13},{5,9},{9,5},{13,1},{2,14},{6,10},... | collective-permute-start | bytes 786440 | tf_op jit(solution)/shard_map/ppermute | solution.py:48
  86.5 9.6 %collective-permute-start.19 = (bf16[32,1024]{1,0:T(8,128)(2,1)S(1)}, bf16[32,1024]{1,0:T(8,128)(2,1)S(1)}, u32[]{:S(2)}, u32[]{:S(2)}) collective-permute-start(bf16[32,1024]{1,0:T(8,128)(2,1)S(1)} %add_convert_fusion.3), channel_id=1, source_target_pairs={{0,1},{1,0},{2,3},{3,2},{4,5},{5,4},{6,7},{7,6},{8,9},{9,8},{10,11... | collective-permute-start | bytes 196616 | tf_op jit(solution)/shard_map/ppermute | solution.py:48
  86.6 11.8 %collective-permute-start.20 = (bf16[32,1024]{1,0:T(8,128)(2,1)S(1)}, bf16[32,1024]{1,0:T(8,128)(2,1)S(1)}, u32[]{:S(2)}, u32[]{:S(2)}) collective-permute-start(bf16[32,1024]{1,0:T(8,128)(2,1)S(1)} %add_convert_fusion.3), channel_id=1, source_target_pairs={{0,2},{1,3},{2,0},{3,1},{4,6},{5,7},{6,4},{7,5},{8,10},{9,11},{10,... | collective-permute-start | bytes 196616 | tf_op jit(solution)/shard_map/ppermute | solution.py:48
  89.3 9.2 %collective-permute-start.21 = (bf16[32,1024]{1,0:T(8,128)(2,1)S(1)}, bf16[32,1024]{1,0:T(8,128)(2,1)S(1)}, u32[]{:S(2)}, u32[]{:S(2)}) collective-permute-start(bf16[32,1024]{1,0:T(8,128)(2,1)S(1)} %add_convert_fusion.3), channel_id=1, source_target_pairs={{0,3},{1,2},{2,1},{3,0},{4,7},{5,6},{6,5},{7,4},{8,11},{9,10},{10,... | collective-permute-start | bytes 196616 | tf_op jit(solution)/shard_map/ppermute | solution.py:48
  98.5 15.5 %collective-permute-start.22 = (bf16[4,32,1024]{2,1,0:T(8,128)(2,1)S(1)}, bf16[4,32,1024]{2,1,0:T(8,128)(2,1)S(1)}, u32[]{:S(2)}, u32[]{:S(2)}) collective-permute-start(bf16[4,32,1024]{2,1,0:T(8,128)(2,1)S(1)} %pad_maximum_fusion.1.refs_0_), channel_id=1, source_target_pairs={{0,4},{4,0},{8,12},{12,8},{1,5},{5,1},{9,13},{13,9},{2,6},{6,2},{1... | collective-permute-start | bytes 786440 | tf_op jit(solution)/shard_map/ppermute | solution.py:48
  107.4 12.0 %collective-permute-start.23 = (bf16[4,32,1024]{2,1,0:T(8,128)(2,1)S(1)}, bf16[4,32,1024]{2,1,0:T(8,128)(2,1)S(1)}, u32[]{:S(2)}, u32[]{:S(2)}) collective-permute-start(bf16[4,32,1024]{2,1,0:T(8,128)(2,1)S(1)} %pad_maximum_fusion.1.refs_0_), channel_id=1, source_target_pairs={{0,8},{4,12},{8,0},{12,4},{1,9},{5,13},{9,1},{13,5},{2,10},{6,14},... | collective-permute-start | bytes 786440 | tf_op jit(solution)/shard_map/ppermute | solution.py:48
  108.3 11.1 %collective-permute-start.24 = (bf16[4,32,1024]{2,1,0:T(8,128)(2,1)S(1)}, bf16[4,32,1024]{2,1,0:T(8,128)(2,1)S(1)}, u32[]{:S(2)}, u32[]{:S(2)}) collective-permute-start(bf16[4,32,1024]{2,1,0:T(8,128)(2,1)S(1)} %pad_maximum_fusion.1.refs_0_), channel_id=1, source_target_pairs={{0,12},{4,8},{8,4},{12,0},{1,13},{5,9},{9,5},{13,1},{2,14},{6,10},... | collective-permute-start | bytes 786440 | tf_op jit(solution)/shard_map/ppermute | solution.py:48
  111.9 8.8 %collective-permute-start.60 = (bf16[4,32,1024]{2,1,0:T(8,128)(2,1)S(1)}, bf16[4,32,1024]{2,1,0:T(8,128)(2,1)S(1)}, u32[]{:S(2)}, u32[]{:S(2)}) collective-permute-start(bf16[4,32,1024]{2,1,0:T(8,128)(2,1)S(1)} %pad_maximum_fusion.2.refs_0_), channel_id=1, source_target_pairs={{0,4},{4,0},{8,12},{12,8},{1,5},{5,1},{9,13},{13,9},{2,6},{6,2},{1... | collective-permute-start | bytes 786440 | tf_op jit(solution)/shard_map/ppermute | solution.py:48
  112.5 12.5 %collective-permute-start.61 = (bf16[4,32,1024]{2,1,0:T(8,128)(2,1)S(1)}, bf16[4,32,1024]{2,1,0:T(8,128)(2,1)S(1)}, u32[]{:S(2)}, u32[]{:S(2)}) collective-permute-start(bf16[4,32,1024]{2,1,0:T(8,128)(2,1)S(1)} %pad_maximum_fusion.2.refs_0_), channel_id=1, source_target_pairs={{0,8},{4,12},{8,0},{12,4},{1,9},{5,13},{9,1},{13,5},{2,10},{6,14},... | collective-permute-start | bytes 786440 | tf_op jit(solution)/shard_map/ppermute | solution.py:48
  114.0 11.0 %collective-permute-start.62 = (bf16[4,32,1024]{2,1,0:T(8,128)(2,1)S(1)}, bf16[4,32,1024]{2,1,0:T(8,128)(2,1)S(1)}, u32[]{:S(2)}, u32[]{:S(2)}) collective-permute-start(bf16[4,32,1024]{2,1,0:T(8,128)(2,1)S(1)} %pad_maximum_fusion.2.refs_0_), channel_id=1, source_target_pairs={{0,12},{4,8},{8,4},{12,0},{1,13},{5,9},{9,5},{13,1},{2,14},{6,10},... | collective-permute-start | bytes 786440 | tf_op jit(solution)/shard_map/ppermute | solution.py:48
  126.2 13.3 %collective-permute-start.63 = (f32[128,512]{1,0:T(8,128)S(1)}, f32[128,512]{1,0:T(8,128)S(1)}, u32[]{:S(2)}, u32[]{:S(2)}) collective-permute-start(f32[128,512]{1,0:T(8,128)S(1)} %shard_map.91.refs_0_), channel_id=1, source_target_pairs={{0,16},{16,0},{1,17},{17,1},{2,18},{18,2},{3,19},{19,3},{4,20},{20... | collective-permute-start | bytes 786440 | tf_op jit(solution)/shard_map/ppermute | solution.py:48
  136.0 17.2 %collective-permute-start.29 = (bf16[32,2048]{1,0:T(8,128)(2,1)S(1)}, bf16[32,2048]{1,0:T(8,128)(2,1)S(1)}, u32[]{:S(2)}, u32[]{:S(2)}) collective-permute-start(bf16[32,2048]{1,0:T(8,128)(2,1)S(1)} %get-tuple-element.75), channel_id=1, source_target_pairs={{0,4},{4,0},{8,12},{12,8},{1,5},{5,1},{9,13},{13,9},{2,6},{6,2},{1... | collective-permute-start | bytes 393224 | tf_op jit(solution)/shard_map/ppermute | solution.py:48
  137.4 17.3 %collective-permute-start.30 = (bf16[32,2048]{1,0:T(8,128)(2,1)S(1)}, bf16[32,2048]{1,0:T(8,128)(2,1)S(1)}, u32[]{:S(2)}, u32[]{:S(2)}) collective-permute-start(bf16[32,2048]{1,0:T(8,128)(2,1)S(1)} %get-tuple-element.76), channel_id=1, source_target_pairs={{0,8},{4,12},{8,0},{12,4},{1,9},{5,13},{9,1},{13,5},{2,10},{6,14},... | collective-permute-start | bytes 393224 | tf_op jit(solution)/shard_map/ppermute | solution.py:48
  137.9 16.8 %collective-permute-start.31 = (bf16[32,2048]{1,0:T(8,128)(2,1)S(1)}, bf16[32,2048]{1,0:T(8,128)(2,1)S(1)}, u32[]{:S(2)}, u32[]{:S(2)}) collective-permute-start(bf16[32,2048]{1,0:T(8,128)(2,1)S(1)} %get-tuple-element.77), channel_id=1, source_target_pairs={{0,12},{4,8},{8,4},{12,0},{1,13},{5,9},{9,5},{13,1},{2,14},{6,10},... | collective-permute-start | bytes 393224 | tf_op jit(solution)/shard_map/ppermute | solution.py:48
  152.6 7.4 %collective-permute-start.68 = (bf16[32,2048]{1,0:T(8,128)(2,1)S(1)}, bf16[32,2048]{1,0:T(8,128)(2,1)S(1)}, u32[]{:S(2)}, u32[]{:S(2)}) collective-permute-start(bf16[32,2048]{1,0:T(8,128)(2,1)S(1)} %get-tuple-element.104), channel_id=1, source_target_pairs={{0,8},{4,12},{8,0},{12,4},{1,9},{5,13},{9,1},{13,5},{2,10},{6,14},... | collective-permute-start | bytes 393224 | tf_op jit(solution)/shard_map/ppermute | solution.py:48
  153.1 7.9 %collective-permute-start.69 = (bf16[32,2048]{1,0:T(8,128)(2,1)S(1)}, bf16[32,2048]{1,0:T(8,128)(2,1)S(1)}, u32[]{:S(2)}, u32[]{:S(2)}) collective-permute-start(bf16[32,2048]{1,0:T(8,128)(2,1)S(1)} %get-tuple-element.105), channel_id=1, source_target_pairs={{0,12},{4,8},{8,4},{12,0},{1,13},{5,9},{9,5},{13,1},{2,14},{6,10},... | collective-permute-start | bytes 393224 | tf_op jit(solution)/shard_map/ppermute | solution.py:48
  154.8 8.7 %collective-permute-start.32 = (bf16[32,2048]{1,0:T(8,128)(2,1)S(1)}, bf16[32,2048]{1,0:T(8,128)(2,1)S(1)}, u32[]{:S(2)}, u32[]{:S(2)}) collective-permute-start(bf16[32,2048]{1,0:T(8,128)(2,1)S(1)} %subtract_convert_fusion.1.refs_0_), channel_id=1, source_target_pairs={{0,4},{4,0},{8,12},{12,8},{1,5},{5,1},{9,13},{13,9},{2,6},{6,2},{1... | collective-permute-start | bytes 393224 | tf_op jit(solution)/shard_map/ppermute | solution.py:48
  156.3 8.8 %collective-permute-start.33 = (bf16[32,2048]{1,0:T(8,128)(2,1)S(1)}, bf16[32,2048]{1,0:T(8,128)(2,1)S(1)}, u32[]{:S(2)}, u32[]{:S(2)}) collective-permute-start(bf16[32,2048]{1,0:T(8,128)(2,1)S(1)} %subtract_convert_fusion.1.refs_0_), channel_id=1, source_target_pairs={{0,8},{4,12},{8,0},{12,4},{1,9},{5,13},{9,1},{13,5},{2,10},{6,14},... | collective-permute-start | bytes 393224 | tf_op jit(solution)/shard_map/ppermute | solution.py:48
  157.6 7.5 %collective-permute-start.34 = (bf16[32,2048]{1,0:T(8,128)(2,1)S(1)}, bf16[32,2048]{1,0:T(8,128)(2,1)S(1)}, u32[]{:S(2)}, u32[]{:S(2)}) collective-permute-start(bf16[32,2048]{1,0:T(8,128)(2,1)S(1)} %subtract_convert_fusion.1.refs_0_), channel_id=1, source_target_pairs={{0,12},{4,8},{8,4},{12,0},{1,13},{5,9},{9,5},{13,1},{2,14},{6,10},... | collective-permute-start | bytes 393224 | tf_op jit(solution)/shard_map/ppermute | solution.py:48
  161.1 8.2 %collective-permute-start.70 = (bf16[32,2048]{1,0:T(8,128)(2,1)S(1)}, bf16[32,2048]{1,0:T(8,128)(2,1)S(1)}, u32[]{:S(2)}, u32[]{:S(2)}) collective-permute-start(bf16[32,2048]{1,0:T(8,128)(2,1)S(1)} %subtract_convert_fusion.refs_0_), channel_id=1, source_target_pairs={{0,4},{4,0},{8,12},{12,8},{1,5},{5,1},{9,13},{13,9},{2,6},{6,2},{1... | collective-permute-start | bytes 393224 | tf_op jit(solution)/shard_map/ppermute | solution.py:48
  162.0 10.0 %collective-permute-start.71 = (bf16[32,2048]{1,0:T(8,128)(2,1)S(1)}, bf16[32,2048]{1,0:T(8,128)(2,1)S(1)}, u32[]{:S(2)}, u32[]{:S(2)}) collective-permute-start(bf16[32,2048]{1,0:T(8,128)(2,1)S(1)} %subtract_convert_fusion.refs_0_), channel_id=1, source_target_pairs={{0,8},{4,12},{8,0},{12,4},{1,9},{5,13},{9,1},{13,5},{2,10},{6,14},... | collective-permute-start | bytes 393224 | tf_op jit(solution)/shard_map/ppermute | solution.py:48
  163.5 8.5 %collective-permute-start.72 = (bf16[32,2048]{1,0:T(8,128)(2,1)S(1)}, bf16[32,2048]{1,0:T(8,128)(2,1)S(1)}, u32[]{:S(2)}, u32[]{:S(2)}) collective-permute-start(bf16[32,2048]{1,0:T(8,128)(2,1)S(1)} %subtract_convert_fusion.refs_0_), channel_id=1, source_target_pairs={{0,12},{4,8},{8,4},{12,0},{1,13},{5,9},{9,5},{13,1},{2,14},{6,10},... | collective-permute-start | bytes 393224 | tf_op jit(solution)/shard_map/ppermute | solution.py:48
  166.5 13.1 %collective-permute-start.35 = (bf16[32,2048]{1,0:T(8,128)(2,1)S(1)}, bf16[32,2048]{1,0:T(8,128)(2,1)S(1)}, u32[]{:S(2)}, u32[]{:S(2)}) collective-permute-start(bf16[32,2048]{1,0:T(8,128)(2,1)S(1)} %get-tuple-element.79), channel_id=1, source_target_pairs={{0,1},{1,0},{2,3},{3,2},{4,5},{5,4},{6,7},{7,6},{8,9},{9,8},{10,11... | collective-permute-start | bytes 393224 | tf_op jit(solution)/shard_map/ppermute | solution.py:48
  166.6 14.6 %collective-permute-start.36 = (bf16[32,2048]{1,0:T(8,128)(2,1)S(1)}, bf16[32,2048]{1,0:T(8,128)(2,1)S(1)}, u32[]{:S(2)}, u32[]{:S(2)}) collective-permute-start(bf16[32,2048]{1,0:T(8,128)(2,1)S(1)} %get-tuple-element.80), channel_id=1, source_target_pairs={{0,2},{1,3},{2,0},{3,1},{4,6},{5,7},{6,4},{7,5},{8,10},{9,11},{10,... | collective-permute-start | bytes 393224 | tf_op jit(solution)/shard_map/ppermute | solution.py:48
  169.4 11.8 %collective-permute-start.37 = (bf16[32,2048]{1,0:T(8,128)(2,1)S(1)}, bf16[32,2048]{1,0:T(8,128)(2,1)S(1)}, u32[]{:S(2)}, u32[]{:S(2)}) collective-permute-start(bf16[32,2048]{1,0:T(8,128)(2,1)S(1)} %get-tuple-element.81), channel_id=1, source_target_pairs={{0,3},{1,2},{2,1},{3,0},{4,7},{5,6},{6,5},{7,4},{8,11},{9,10},{10,... | collective-permute-start | bytes 393224 | tf_op jit(solution)/shard_map/ppermute | solution.py:48
  176.8 9.8 %collective-permute-start.74 = (bf16[32,2048]{1,0:T(8,128)(2,1)S(1)}, bf16[32,2048]{1,0:T(8,128)(2,1)S(1)}, u32[]{:S(2)}, u32[]{:S(2)}) collective-permute-start(bf16[32,2048]{1,0:T(8,128)(2,1)S(1)} %get-tuple-element.108), channel_id=1, source_target_pairs={{0,2},{1,3},{2,0},{3,1},{4,6},{5,7},{6,4},{7,5},{8,10},{9,11},{10,... | collective-permute-start | bytes 393224 | tf_op jit(solution)/shard_map/ppermute | solution.py:48
  179.6 7.0 %collective-permute-start.75 = (bf16[32,2048]{1,0:T(8,128)(2,1)S(1)}, bf16[32,2048]{1,0:T(8,128)(2,1)S(1)}, u32[]{:S(2)}, u32[]{:S(2)}) collective-permute-start(bf16[32,2048]{1,0:T(8,128)(2,1)S(1)} %get-tuple-element.109), channel_id=1, source_target_pairs={{0,3},{1,2},{2,1},{3,0},{4,7},{5,6},{6,5},{7,4},{8,11},{9,10},{10,... | collective-permute-start | bytes 393224 | tf_op jit(solution)/shard_map/ppermute | solution.py:48
  (34 other events, 278.1 us)
